TPU v7x, 32 devices: a whole 2x2x4 slice. The times are simulated.
32 devices in a mesh: seq: 2 (over y), fsdp: 16 (over z, x, core).
Axes of the slice: x: 2, y: 2, z: 4, core: 2. Of those that a mesh axis runs over, the one named last changes fastest.
Arguments:
- tokens: bfloat16 [16, 1024, 2048], P('fsdp', 'seq'), may hold values from -6 to 6
- segments: int32 [16, 1024], P('fsdp'), may hold values from -1 to 16, as said below
- attn_gain: bfloat16 [2048], P(('seq', 'fsdp')), may hold values from 0.5 to 1.5
- w_query: bfloat16 [2048, 1536], P(('seq', 'fsdp')), may hold values from -0.125 to 0.125
- key_projection_weight: bfloat16 [2048, 384], P(('seq', 'fsdp')), may hold values from -0.125 to 0.125
- value_projection_weight: bfloat16 [2048, 384], P(('seq', 'fsdp')), may hold values from -0.125 to 0.125
- query_norm_gain: bfloat16 [64], replicated, may hold values from 0.099609375 to 1.8984375
- key_gain: bfloat16 [64], replicated, may hold values from 0.099609375 to 1.8984375
- w_out: bfloat16 [1536, 2048], P(('seq', 'fsdp')), may hold values from -0.625 to 0.625
- ffn_gain: bfloat16 [2048], P(('seq', 'fsdp')), may hold values from 0.5 to 1.5
- w_gate: bfloat16 [2048, 4864], P(('seq', 'fsdp')), may hold values from -0.125 to 0.125
- w_up: bfloat16 [2048, 4864], P(('seq', 'fsdp')), may hold values from -0.125 to 0.125
- w_down: bfloat16 [4864, 2048], P(('seq', 'fsdp')), may hold values from -0.078125 to 0.078125
- cotangent: bfloat16 [16, 1024, 2048], P('fsdp', 'seq'), may hold values from -6 to 6
Outputs:
- output: bfloat16 [16, 1024, 2048], P('fsdp', 'seq')
- input_grad: float32 [16, 1024, 2048], P('fsdp', 'seq')
- attn_gain_grad: float32 [2048], P(('seq', 'fsdp'))
- w_query_grad: float32 [2048, 1536], P(('seq', 'fsdp'))
- w_key_grad: float32 [2048, 384], P(('seq', 'fsdp'))
- w_value_grad: float32 [2048, 384], P(('seq', 'fsdp'))
- query_gain_grad: float32 [64], replicated
- key_gain_grad: float32 [64], replicated
- w_out_grad: float32 [1536, 2048], P(('seq', 'fsdp'))
- ffn_gain_grad: float32 [2048], P(('seq', 'fsdp'))
- w_gate_grad: float32 [2048, 4864], P(('seq', 'fsdp'))
- w_up_grad: float32 [2048, 4864], P(('seq', 'fsdp'))
- w_down_grad: float32 [4864, 2048], P(('seq', 'fsdp'))
Inputs may be any that keep to these rules, and one draw needn't show every extreme that they name: `segments`: in each sequence ids start at 0, rise by one at each new document and end at min(16, 128) before a tail of -1 that fills 1 to 128 positions; in each sequence one document covers the positions 511 and 512.
All inputs are finite; a program needn't handle non-finite values.
Results may differ from a plain program's by a relative error of at most 0.015.
Values may be sent and summed in bfloat16 or wider, within the bound.
No kernel may reach another device: no remote copies, remote signals or barrier semaphores. Data moves between devices by JAX's collectives and lax.ppermute only.
A program may use at most 384 MiB of HBM per device.

v0:
```python
import math

import jax
import jax.numpy as jnp
from jax import lax
from jax.sharding import PartitionSpec as P

QUERY_HEADS = 24
KEY_VALUE_HEADS = 6
HEAD_SIZE = 64


EPS = 1e-06


def passed_along(value, axis, steps):
    count = lax.axis_size(axis)
    first, last = (max(0, -steps), min(count, count - steps))
    return lax.ppermute(value, axis, [(source, source + steps) for source in range(first, last)])


def row_norm_apply(values, gain_vec):
    return values * lax.rsqrt(jnp.mean(values * values, axis=-1, keepdims=True) + EPS) * gain_vec


def apply_rotary(tensor, cosine_table, sine_table):
    middle = tensor.shape[-1] // 2
    former = tensor[..., :middle]
    latter = tensor[..., middle:]
    return jnp.concatenate(
        [former * cosine_table - latter * sine_table, latter * cosine_table + former * sine_table],
        axis=-1,
    )


def doc_positions(segment_row):
    packed_length = segment_row.shape[-1]
    places = jnp.arange(packed_length, dtype=jnp.int32)
    earlier = jnp.concatenate([segment_row[..., :1] + 1, segment_row[..., :-1]], axis=-1)
    starts = jnp.where(segment_row != earlier, places, 0)
    return places - lax.cummax(starts, axis=segment_row.ndim - 1)


def rotary_tables(positions):
    pair_count = HEAD_SIZE // 2
    frequencies = jnp.exp(
        jnp.arange(pair_count, dtype=jnp.float32) * (-2.0 * math.log(10000.0) / HEAD_SIZE)
    )
    phases = positions.astype(jnp.float32)[..., None] * frequencies
    return (jnp.cos(phases)[..., None, :], jnp.sin(phases)[..., None, :])


def swiglu(gate_in, up_in):
    return jax.nn.silu(gate_in) * up_in


def masked_scores(query_head_split, key_head_split, allowed):
    score_scale = HEAD_SIZE ** (-0.5)
    scores = (
        jnp.einsum(
            "qhgd,khd->hgqk", query_head_split, key_head_split, preferred_element_type=jnp.float32
        )
        * score_scale
    )
    return jnp.where(allowed[None, None, :, :], scores, -1e30)


def split_heads(query_block_part, key_block_part, value_block_part):
    query_total_count = query_block_part.shape[0]
    key_total_count = key_block_part.shape[0]
    head_groups = QUERY_HEADS // KEY_VALUE_HEADS
    query_head_split = query_block_part.reshape(
        query_total_count, KEY_VALUE_HEADS, head_groups, HEAD_SIZE
    )
    key_head_split = key_block_part.reshape(key_total_count, KEY_VALUE_HEADS, HEAD_SIZE)
    value_head_split = value_block_part.reshape(key_total_count, KEY_VALUE_HEADS, HEAD_SIZE)
    return (query_head_split, key_head_split, value_head_split)


def attend_one(bundle):
    query_block_part, key_block_part, value_block_part, allowed = bundle
    query_head_split, key_head_split, value_head_split = split_heads(
        query_block_part, key_block_part, value_block_part
    )
    scores = masked_scores(query_head_split, key_head_split, allowed)
    row_peak = jnp.max(scores, axis=-1, keepdims=True)
    row_total = jnp.sum(jnp.exp(scores - row_peak), axis=-1, keepdims=True)
    log_total = row_peak + jnp.log(row_total)
    probs = jnp.exp(scores - log_total).astype(jnp.bfloat16)
    mixed_heads = jnp.einsum(
        "hgqk,khd->qhgd", probs, value_head_split, preferred_element_type=jnp.float32
    )
    return (mixed_heads.reshape(query_block_part.shape[0], QUERY_HEADS * HEAD_SIZE), log_total)


def attend_back(bundle):
    query_block_part, key_block_part, value_block_part, allowed, log_total, grad_block = bundle
    query_head_split, key_head_split, value_head_split = split_heads(
        query_block_part, key_block_part, value_block_part
    )
    score_scale = HEAD_SIZE ** (-0.5)
    scores = masked_scores(query_head_split, key_head_split, allowed)
    probs = jnp.exp(scores - log_total)
    grad_heads = grad_block.reshape(query_head_split.shape)
    grad_probs = jnp.einsum(
        "qhgd,khd->hgqk", grad_heads, value_head_split, preferred_element_type=jnp.float32
    )
    grad_value_rows = jnp.einsum(
        "hgqk,qhgd->khd", probs.astype(jnp.bfloat16), grad_heads, preferred_element_type=jnp.float32
    )
    inner_sum = jnp.sum(grad_probs * probs, axis=-1, keepdims=True)
    grad_scores = (probs * (grad_probs - inner_sum)).astype(jnp.bfloat16)
    grad_queries = (
        jnp.einsum(
            "hgqk,khd->qhgd", grad_scores, key_head_split, preferred_element_type=jnp.float32
        )
        * score_scale
    )
    grad_key_rows = (
        jnp.einsum(
            "hgqk,qhgd->khd", grad_scores, query_head_split, preferred_element_type=jnp.float32
        )
        * score_scale
    )
    key_total_count = key_block_part.shape[0]
    return (
        grad_queries.reshape(query_block_part.shape[0], QUERY_HEADS * HEAD_SIZE),
        grad_key_rows.reshape(key_total_count, KEY_VALUE_HEADS * HEAD_SIZE),
        grad_value_rows.reshape(key_total_count, KEY_VALUE_HEADS * HEAD_SIZE),
    )


def body(
    tokens,
    segments,
    attn_gain,
    w_query,
    key_projection_weight,
    value_projection_weight,
    query_norm_gain,
    key_gain,
    w_out,
    ffn_gain,
    w_gate,
    w_up,
    w_down,
    cotangent,
):
    sequence_count, half_length, feature_dim = tokens.shape
    row_total_count = sequence_count * half_length
    query_full, key_full, value_full, out_full, attn_gain_full = (
        lax.all_gather(w_query, ("seq", "fsdp"), axis=0, tiled=True),
        lax.all_gather(key_projection_weight, ("seq", "fsdp"), axis=0, tiled=True),
        lax.all_gather(value_projection_weight, ("seq", "fsdp"), axis=0, tiled=True),
        lax.all_gather(w_out, ("seq", "fsdp"), axis=0, tiled=True),
        lax.all_gather(attn_gain, ("seq", "fsdp"), axis=0, tiled=True),
    )
    seq_place = lax.axis_index("seq")
    positions_all = doc_positions(segments)
    own_start = seq_place * half_length
    own_segments = lax.dynamic_slice_in_dim(segments, own_start, half_length, 1)
    own_positions = lax.dynamic_slice_in_dim(positions_all, own_start, half_length, 1)
    prior_start = jnp.maximum(own_start - half_length, 0)
    prior_segments = lax.dynamic_slice_in_dim(segments, prior_start, half_length, 1)
    query_places = own_start + jnp.arange(half_length, dtype=jnp.int32)
    key_places = jnp.concatenate([query_places - half_length, query_places])
    key_segments = jnp.concatenate([prior_segments, own_segments], axis=1)
    allowed = (
        (own_segments[:, :, None] == key_segments[:, None, :])
        & (key_places[None, None, :] <= query_places[None, :, None])
        & (key_places[None, None, :] >= 0)
    )
    cosine_table, sine_table = rotary_tables(own_positions.reshape(row_total_count))
    inputs = tokens.reshape(row_total_count, feature_dim).astype(jnp.float32)
    normed_first, first_pull = jax.vjp(row_norm_apply, inputs, attn_gain_full.astype(jnp.float32))
    first_hidden = normed_first.astype(jnp.bfloat16)
    query_rows = jnp.dot(first_hidden, query_full, preferred_element_type=jnp.float32)
    key_unnormed = jnp.dot(first_hidden, key_full, preferred_element_type=jnp.float32)
    value_unnormed = jnp.dot(first_hidden, value_full, preferred_element_type=jnp.float32)

    def heads_fn(query_in, key_input, gain_query, key_norm_gain):
        query_spun = apply_rotary(
            row_norm_apply(query_in.reshape(row_total_count, QUERY_HEADS, HEAD_SIZE), gain_query),
            cosine_table,
            sine_table,
        )
        key_spun = apply_rotary(
            row_norm_apply(
                key_input.reshape(row_total_count, KEY_VALUE_HEADS, HEAD_SIZE), key_norm_gain
            ),
            cosine_table,
            sine_table,
        )
        return (
            query_spun.reshape(row_total_count, QUERY_HEADS * HEAD_SIZE),
            key_spun.reshape(row_total_count, KEY_VALUE_HEADS * HEAD_SIZE),
        )

    rotary_result, heads_pull = jax.vjp(
        heads_fn,
        query_rows,
        key_unnormed,
        query_norm_gain.astype(jnp.float32),
        key_gain.astype(jnp.float32),
    )
    query_rotary = (
        rotary_result[0]
        .astype(jnp.bfloat16)
        .reshape(sequence_count, half_length, QUERY_HEADS * HEAD_SIZE)
    )
    key_rotary = (
        rotary_result[1]
        .astype(jnp.bfloat16)
        .reshape(sequence_count, half_length, KEY_VALUE_HEADS * HEAD_SIZE)
    )
    value_narrow = value_unnormed.astype(jnp.bfloat16).reshape(
        sequence_count, half_length, KEY_VALUE_HEADS * HEAD_SIZE
    )
    prior_pair = passed_along(jnp.stack([key_rotary, value_narrow]), "seq", 1)
    all_keys = jnp.concatenate([prior_pair[0], key_rotary], axis=1)
    all_values = jnp.concatenate([prior_pair[1], value_narrow], axis=1)
    mixed, log_totals = lax.map(attend_one, (query_rotary, all_keys, all_values, allowed))
    attn_low = mixed.reshape(row_total_count, QUERY_HEADS * HEAD_SIZE).astype(jnp.bfloat16)
    middle = inputs + jnp.dot(attn_low, out_full, preferred_element_type=jnp.float32)
    gate_full, up_full, down_full, ffn_gain_full = (
        lax.all_gather(w_gate, ("seq", "fsdp"), axis=0, tiled=True),
        lax.all_gather(w_up, ("seq", "fsdp"), axis=0, tiled=True),
        lax.all_gather(w_down, ("seq", "fsdp"), axis=0, tiled=True),
        lax.all_gather(ffn_gain, ("seq", "fsdp"), axis=0, tiled=True),
    )
    normed_second, second_pull = jax.vjp(row_norm_apply, middle, ffn_gain_full.astype(jnp.float32))
    hidden_second = normed_second.astype(jnp.bfloat16)
    gate_pre = jnp.dot(hidden_second, gate_full, preferred_element_type=jnp.float32)
    up_pre = jnp.dot(hidden_second, up_full, preferred_element_type=jnp.float32)
    activated, swiglu_pull = jax.vjp(swiglu, gate_pre, up_pre)
    act_low = activated.astype(jnp.bfloat16)
    result = middle + jnp.dot(act_low, down_full, preferred_element_type=jnp.float32)
    output = result.reshape(sequence_count, half_length, feature_dim).astype(jnp.bfloat16)
    gate_full, up_full, down_full = (
        lax.all_gather(w_gate, ("seq", "fsdp"), axis=0, tiled=True),
        lax.all_gather(w_up, ("seq", "fsdp"), axis=0, tiled=True),
        lax.all_gather(w_down, ("seq", "fsdp"), axis=0, tiled=True),
    )
    grad_low = cotangent.reshape(row_total_count, feature_dim)
    grad_result = grad_low.astype(jnp.float32)
    grad_act = jnp.einsum("md,fd->mf", grad_low, down_full, preferred_element_type=jnp.float32)
    grad_gate, grad_up = swiglu_pull(grad_act)
    grad_gate_low = grad_gate.astype(jnp.bfloat16)
    grad_up_low = grad_up.astype(jnp.bfloat16)
    grad_hidden_second = jnp.einsum(
        "mf,df->md", grad_gate_low, gate_full, preferred_element_type=jnp.float32
    ) + jnp.einsum("mf,df->md", grad_up_low, up_full, preferred_element_type=jnp.float32)
    grad_middle_part, grad_ffn_gain = second_pull(grad_hidden_second)
    grad_middle = grad_result + grad_middle_part
    grad_down_w = jnp.einsum("mf,md->fd", act_low, grad_low, preferred_element_type=jnp.float32)
    grad_gate_w = jnp.einsum(
        "md,mf->df", hidden_second, grad_gate_low, preferred_element_type=jnp.float32
    )
    grad_up_w = jnp.einsum(
        "md,mf->df", hidden_second, grad_up_low, preferred_element_type=jnp.float32
    )
    ffn_grads = (
        lax.psum_scatter(grad_gate_w, ("seq", "fsdp"), scatter_dimension=0, tiled=True),
        lax.psum_scatter(grad_up_w, ("seq", "fsdp"), scatter_dimension=0, tiled=True),
        lax.psum_scatter(grad_down_w, ("seq", "fsdp"), scatter_dimension=0, tiled=True),
        lax.psum_scatter(grad_ffn_gain, ("seq", "fsdp"), scatter_dimension=0, tiled=True),
    )
    gate_owned, up_owned, down_owned, ffn_gain_owned = (
        ffn_grads[0],
        ffn_grads[1],
        ffn_grads[2],
        ffn_grads[3],
    )
    query_full, key_full, value_full, out_full = (
        lax.all_gather(w_query, ("seq", "fsdp"), axis=0, tiled=True),
        lax.all_gather(key_projection_weight, ("seq", "fsdp"), axis=0, tiled=True),
        lax.all_gather(value_projection_weight, ("seq", "fsdp"), axis=0, tiled=True),
        lax.all_gather(w_out, ("seq", "fsdp"), axis=0, tiled=True),
    )
    grad_branch = grad_middle.astype(jnp.bfloat16)
    grad_out_w = jnp.einsum("ma,md->ad", attn_low, grad_branch, preferred_element_type=jnp.float32)
    grad_attn = jnp.einsum(
        "md,ad->ma", grad_branch, out_full, preferred_element_type=jnp.float32
    ).astype(jnp.bfloat16)
    grad_attn = grad_attn.reshape(sequence_count, half_length, QUERY_HEADS * HEAD_SIZE)
    grad_query_rotated, grad_k_all, grad_v_all = lax.map(
        attend_back, (query_rotary, all_keys, all_values, allowed, log_totals, grad_attn)
    )
    prior_grads = passed_along(
        jnp.stack([grad_k_all[:, :half_length], grad_v_all[:, :half_length]]).astype(jnp.bfloat16),
        "seq",
        -1,
    ).astype(jnp.float32)
    grad_key_rotated = grad_k_all[:, half_length:] + prior_grads[0]
    grad_value_rows = grad_v_all[:, half_length:] + prior_grads[1]
    grad_queries, grad_key_rows, grad_qgain, grad_kgain = heads_pull(
        (
            grad_query_rotated.reshape(row_total_count, QUERY_HEADS * HEAD_SIZE),
            grad_key_rotated.reshape(row_total_count, KEY_VALUE_HEADS * HEAD_SIZE),
        )
    )
    grad_q_low = grad_queries.astype(jnp.bfloat16)
    grad_k_low = grad_key_rows.astype(jnp.bfloat16)
    grad_value_narrow = grad_value_rows.reshape(
        row_total_count, KEY_VALUE_HEADS * HEAD_SIZE
    ).astype(jnp.bfloat16)
    grad_query_w = jnp.einsum(
        "md,mh->dh", first_hidden, grad_q_low, preferred_element_type=jnp.float32
    )
    grad_key_w = jnp.einsum(
        "md,mh->dh", first_hidden, grad_k_low, preferred_element_type=jnp.float32
    )
    grad_value_w = jnp.einsum(
        "md,mh->dh", first_hidden, grad_value_narrow, preferred_element_type=jnp.float32
    )
    grad_hidden_first = jnp.einsum(
        "mh,dh->md", grad_q_low, query_full, preferred_element_type=jnp.float32
    )
    grad_hidden_first = grad_hidden_first + jnp.einsum(
        "mh,dh->md", grad_k_low, key_full, preferred_element_type=jnp.float32
    )
    grad_hidden_first = grad_hidden_first + jnp.einsum(
        "mh,dh->md", grad_value_narrow, value_full, preferred_element_type=jnp.float32
    )
    grad_inputs_part, grad_attn_gain = first_pull(grad_hidden_first)
    grad_inputs = (grad_middle + grad_inputs_part).reshape(sequence_count, half_length, feature_dim)
    spare_gain = jnp.zeros_like(grad_attn_gain)
    attn_grads = (
        lax.psum_scatter(grad_query_w, ("seq", "fsdp"), scatter_dimension=0, tiled=True),
        lax.psum_scatter(grad_key_w, ("seq", "fsdp"), scatter_dimension=0, tiled=True),
        lax.psum_scatter(grad_value_w, ("seq", "fsdp"), scatter_dimension=0, tiled=True),
        lax.psum_scatter(grad_out_w, ("seq", "fsdp"), scatter_dimension=0, tiled=True),
        lax.psum_scatter(grad_attn_gain, ("seq", "fsdp"), scatter_dimension=0, tiled=True),
        lax.psum_scatter(spare_gain, ("seq", "fsdp"), scatter_dimension=0, tiled=True),
    )
    gain_grads = lax.psum((grad_qgain, grad_kgain), ("seq", "fsdp"))
    return (
        output,
        grad_inputs,
        attn_grads[4],
        attn_grads[0],
        attn_grads[1],
        attn_grads[2],
        gain_grads[0],
        gain_grads[1],
        attn_grads[3],
        ffn_gain_owned,
        gate_owned,
        up_owned,
        down_owned,
    )


def solution(mesh):
    in_specs = (
        P("fsdp", "seq", None),
        P("fsdp", None),
        P(("seq", "fsdp")),
        P(("seq", "fsdp"), None),
        P(("seq", "fsdp"), None),
        P(("seq", "fsdp"), None),
        P(),
        P(),
        P(("seq", "fsdp"), None),
        P(("seq", "fsdp")),
        P(("seq", "fsdp"), None),
        P(("seq", "fsdp"), None),
        P(("seq", "fsdp"), None),
        P("fsdp", "seq", None),
    )
    out_specs = (
        P("fsdp", "seq", None),
        P("fsdp", "seq", None),
        P(("seq", "fsdp")),
        P(("seq", "fsdp"), None),
        P(("seq", "fsdp"), None),
        P(("seq", "fsdp"), None),
        P(),
        P(),
        P(("seq", "fsdp"), None),
        P(("seq", "fsdp")),
        P(("seq", "fsdp"), None),
        P(("seq", "fsdp"), None),
        P(("seq", "fsdp"), None),
    )
    return jax.shard_map(body, mesh=mesh, in_specs=in_specs, out_specs=out_specs, check_vma=False)
```

profile of v0, /device:TPU:1, one launch (start us, length us, event | category | flops | bytes accessed | tf_op | source)
XLA Modules:
  0.0 2691.5 jit_solution(3594599773468543371)
XLA Ops:
  13.7 40.7 %all-reduce.9 = (bf16[2048]{0:T(1024)(128)(2,1)S(1)}, bf16[2048]{0:T(1024)(128)(2,1)S(1)}) all-reduce(bf16[2048]{0:T(1024)(128)(2,1)S(1)} %dynamic-update-slice, bf16[2048]{0:T(1024)(128)(2,1)S(1)} %dynamic-update-slice.1), channel_id=1, replica_groups=mesh['seq'=2,'fsdp'=16] {'seq','fsdp'}, use_global_device_ids=true, to_apply=%add.4 | all-reduce | flops 4096 | bytes 16384
  74.8 50.4 %all-gather.10.cloned.1.call-done = bf16[2048,384]{1,0:T(8,128)(2,1)} async-done(((bf16[64,384]{1,0:T(8,128)(2,1)}), bf16[2048,384]{1,0:T(8,128)(2,1)}) %all-gather.10.cloned.1.call-update) | async-done | bytes 1572880 | tf_op jit(solution)/shard_map/all_gather | solution.py:154
  149.8 47.9 %all-gather.12.cloned.1.call-done = bf16[2048,1536]{1,0:T(8,128)(2,1)} async-done(((bf16[64,1536]{1,0:T(8,128)(2,1)}), bf16[2048,1536]{1,0:T(8,128)(2,1)}) %all-gather.12.cloned.1.call-update) | async-done | bytes 6291472 | tf_op jit(solution)/shard_map/all_gather | solution.py:152
  215.5 21.4 fusion.4
  236.9 21.5 exponential_reduce_fusion
  258.5 21.1 convolution_convert_fusion.1
  288.6 110.7 %all-gather.16.cloned.1.call-done = bf16[2048,4864]{1,0:T(8,128)(2,1)} async-done(((bf16[64,4864]{1,0:T(8,128)(2,1)}), bf16[2048,4864]{1,0:T(8,128)(2,1)}) %all-gather.16.cloned.1.call-update) | async-done | bytes 19922960 | tf_op jit(solution)/shard_map/all_gather | solution.py:226
  416.5 113.2 %all-gather.18.cloned.1.call-done = bf16[2048,4864]{1,0:T(8,128)(2,1)} async-done(((bf16[64,4864]{1,0:T(8,128)(2,1)}), bf16[2048,4864]{1,0:T(8,128)(2,1)}) %all-gather.18.cloned.1.call-update) | async-done | bytes 19922960 | tf_op jit(solution)/shard_map/all_gather | solution.py:227
  547.0 113.3 %all-gather.20.cloned.1.call-done = bf16[4864,2048]{1,0:T(8,128)(2,1)} async-done(((bf16[152,2048]{1,0:T(8,128)(2,1)}), bf16[4864,2048]{1,0:T(8,128)(2,1)}) %all-gather.20.cloned.1.call-update) | async-done | bytes 19922960 | tf_op jit(solution)/shard_map/all_gather | solution.py:228
  660.3 25.2 multiply_convert_fusion
  702.8 20.6 multiply_reduce_fusion
  739.1 20.1 fusion.60
  759.2 34.2 %fusion = (f32[6,4,512]{2,1,0:T(4,128)S(1)}, f32[6,1024,512,4]{2,1,3,0:T(8,128)}) fusion(f32[6,1024,512,4]{2,1,3,0:T(8,128)} %get-tuple-element.102, f32[6,4,512]{2,1,0:T(4,128)S(1)} %bitcast.231, pred[512,1024]{0,1:T(8,128)(4,1)S(1)} %and_and_fusion, bf16[512,6,4,64]{0,3,2,1:T(8,128)(2,1)S(1)} %bitcast.211, bf16[512,6,64]{0,2,1:T(8,128)(2,1)S(1)} %bitcast.221, ...), kind=kOutput, calls=%fused_computation.2 | convolution fusion | flops 1675087872 | bytes 103645184 | tf_op jit(solution)/shard_map/while/body/eval_jaxpr/qhgd,khd->hgqk/dot_general | solution.py:105
  794.7 41.1 %fusion.2 = bf16[6,4,512,1024]{2,3,1,0:T(8,128)(2,1)} fusion(f32[6,1024,512,4]{2,1,3,0:T(8,128)} %get-tuple-element.107, f32[6,1024,512,4]{2,1,3,0:T(8,128)} %get-tuple-element.102, f32[6,4,512]{2,1,0:T(4,128)S(1)} %get-tuple-element.106, f32[6,4,512]{2,1,0:T(4,128)S(1)} %bitcast.232, pred[512,1024]{0,1:T(8,128)(4,1)S(1)} %and_and_fusion), kind=kLoop, calls=%fused_computation.4 | loop fusion | flops 75497472 | bytes 126451712 | tf_op jit(solution)/shard_map/while/body/eval_jaxpr/convert_element_type | solution.py:112
  915.8 21.7 fusion.87
  937.5 21.1 fusion.88
  958.8 20.7 fusion.29
  1009.3 39.1 %all-reduce.8 = (f32[2048]{0:T(1024)S(1)}, f32[64]{0:T(128)}, f32[64]{0:T(128)}, f32[2048]{0:T(1024)S(1)}) all-reduce(f32[2048]{0:T(1024)S(1)} %get-tuple-element.68, f32[64]{0:T(128)S(1)} %get-tuple-element.56, f32[64]{0:T(128)S(1)} %copy-done.54, f32[2048]{0:T(1024)S(1)} %copy-done.49), channel_id=2, replica_groups=mesh['seq'=2,'fsdp'=16] {'seq','fsdp'}, use_global_device_ids=true, to_apply=%region_14.15.clone | all-reduce | flops 4224 | bytes 33792
  1056.1 26.7 reduce-scatter.12.cloned.1.call-done
  1082.8 161.2 %reduce-scatter.8.cloned.1.call-done = f32[64,1536]{1,0:T(8,128)} async-done(((f32[2048,1536]{1,0:T(8,128)}), f32[64,1536]{1,0:T(8,128)}) %reduce-scatter.8.cloned.1.call-update) | async-done | bytes 393232 | tf_op jit(solution)/shard_map/reduce_scatter | solution.py:329
  1243.9 162.2 %reduce-scatter.14.cloned.1.call-done = f32[48,2048]{1,0:T(8,128)} async-done(((f32[1536,2048]{1,0:T(8,128)}), f32[48,2048]{1,0:T(8,128)}) %reduce-scatter.14.cloned.1.call-update) | async-done | bytes 393232 | tf_op jit(solution)/shard_map/reduce_scatter | solution.py:332
  1406.1 426.6 %reduce-scatter.16.cloned.1.call-done = f32[64,4864]{1,0:T(8,128)} async-done(((f32[2048,4864]{1,0:T(8,128)}), f32[64,4864]{1,0:T(8,128)}) %reduce-scatter.16.cloned.1.call-update) | async-done | bytes 1245200 | tf_op jit(solution)/shard_map/reduce_scatter | solution.py:263
  1832.7 426.0 %reduce-scatter.18.cloned.1.call-done = f32[64,4864]{1,0:T(8,128)} async-done(((f32[2048,4864]{1,0:T(8,128)}), f32[64,4864]{1,0:T(8,128)}) %reduce-scatter.18.cloned.1.call-update) | async-done | bytes 1245200 | tf_op jit(solution)/shard_map/reduce_scatter | solution.py:264
  2258.6 425.8 %reduce-scatter.20.cloned.1.call-done = f32[152,2048]{1,0:T(8,128)} async-done(((f32[4864,2048]{1,0:T(8,128)}), f32[152,2048]{1,0:T(8,128)}) %reduce-scatter.20.cloned.1.call-update) | async-done | bytes 1245200 | tf_op jit(solution)/shard_map/reduce_scatter | solution.py:265
  (224 shorter events, 263.0 us)
Async XLA Ops:
  7.2 63.8 %copy-start.3 = (bf16[1,512,2048]{2,1,0:T(8,128)(2,1)S(1)}, bf16[1,512,2048]{2,1,0:T(8,128)(2,1)}, u32[]{:S(2)}) copy-start(bf16[1,512,2048]{2,1,0:T(8,128)(2,1)} %param.14) | copy-start | bytes 6291460
  7.2 61.2 %all-gather.8.cloned.1.call-start = ((), (), s32[]{:S(2)}) async-start(), calls=%async_computation.7 | async-start | bytes 1622016 | tf_op jit(solution)/shard_map/all_gather | solution.py:153
  7.9 117.2 %all-gather.10.cloned.1.call-start = ((), (), s32[]{:S(2)}) async-start(), calls=%async_computation.8 | async-start | bytes 1622016 | tf_op jit(solution)/shard_map/all_gather | solution.py:154
  8.7 189.0 %all-gather.12.cloned.1.call-start = ((), (), s32[]{:S(2)}) async-start(), calls=%async_computation.9 | async-start | bytes 6488064 | tf_op jit(solution)/shard_map/all_gather | solution.py:152
  9.4 270.2 %all-gather.14.cloned.1.call-start = ((), (), s32[]{:S(2)}) async-start(), calls=%async_computation.10 | async-start | bytes 6488064 | tf_op jit(solution)/shard_map/all_gather | solution.py:155
  10.0 389.3 %all-gather.16.cloned.1.call-start = ((), (), s32[]{:S(2)}) async-start(), calls=%async_computation.11 | async-start | bytes 20545536 | tf_op jit(solution)/shard_map/all_gather | solution.py:226
  10.6 519.1 %all-gather.18.cloned.1.call-start = ((), (), s32[]{:S(2)}) async-start(), calls=%async_computation.12 | async-start | bytes 20545536 | tf_op jit(solution)/shard_map/all_gather | solution.py:227
  11.1 649.1 %all-gather.20.cloned.1.call-start = ((), (), s32[]{:S(2)}) async-start(), calls=%async_computation.13 | async-start | bytes 20545536 | tf_op jit(solution)/shard_map/all_gather | solution.py:228
  11.9 1044.2 %reduce-scatter.10.cloned.1.call-start = ((), (), s32[]{:S(2)}) async-start(), calls=%async_computation.15 | async-start | bytes 3244032 | tf_op jit(solution)/shard_map/reduce_scatter | solution.py:330
  54.4 152.0 %copy-start.40 = (f32[2048]{0:T(1024)}, f32[2048]{0:T(1024)S(1)}, u32[]{:S(2)}) copy-start(f32[2048]{0:T(1024)S(1)} %convert_element_type.152) | copy-start | bytes 24580
  60.5 70.8 %copy-start.46 = (s32[1,512]{1,0:T(1,128)}, s32[1,512]{1,0:T(1,128)S(1)}, u32[]{:S(2)}) copy-start(s32[1,512]{1,0:T(1,128)S(1)} %get-tuple-element.94) | copy-start | bytes 6148
  62.9 150.1 %copy-start.20 = (f32[512,32]{0,1:T(8,128)}, f32[512,32]{0,1:T(8,128)S(1)}, u32[]{:S(2)}) copy-start(f32[512,32]{0,1:T(8,128)S(1)} %get-tuple-element.95) | copy-start | bytes 196612
  62.9 150.1 %copy-start.22 = (f32[512,32]{0,1:T(8,128)}, f32[512,32]{0,1:T(8,128)S(1)}, u32[]{:S(2)}) copy-start(f32[512,32]{0,1:T(8,128)S(1)} %get-tuple-element.96) | copy-start | bytes 196612
  74.8 140.7 %copy-start.10 = (bf16[512,6,64]{0,2,1:T(8,128)(2,1)}, bf16[512,6,64]{0,2,1:T(8,128)(2,1)S(1)}, u32[]{:S(2)}) copy-start(bf16[512,6,64]{0,2,1:T(8,128)(2,1)S(1)} %maximum_convert_fusion) | copy-start | bytes 1179652
  127.8 21.2 collective-permute-start
  149.8 65.7 %copy-start.14 = (bf16[1,1,512,384]{2,3,1,0:T(8,128)(2,1)}, bf16[1,1,512,384]{2,3,1,0:T(8,128)(2,1)S(1)}, u32[]{:S(2)}) copy-start(bf16[1,1,512,384]{2,3,1,0:T(8,128)(2,1)S(1)} %get-tuple-element.91) | copy-start | bytes 1179652
  288.6 241.1 %copy-start.18 = (bf16[512,2048]{1,0:T(8,128)(2,1)}, bf16[512,2048]{1,0:T(8,128)(2,1)S(1)}, u32[]{:S(2)}) copy-start(bf16[512,2048]{1,0:T(8,128)(2,1)S(1)} %multiply_convert_fusion.2) | copy-start | bytes 6291460
  851.3 20.9 collective-permute-start.1
  878.0 204.7 %reduce-scatter.12.cloned.1.call-start = ((), (), s32[]{:S(2)}) async-start(), calls=%async_computation.16 | async-start | bytes 3244032 | tf_op jit(solution)/shard_map/reduce_scatter | solution.py:331
  881.3 362.6 %reduce-scatter.8.cloned.1.call-start = ((), (), s32[]{:S(2)}) async-start(), calls=%async_computation.14 | async-start | bytes 12976128 | tf_op jit(solution)/shard_map/reduce_scatter | solution.py:329
  904.9 501.1 %reduce-scatter.14.cloned.1.call-start = ((), (), s32[]{:S(2)}) async-start(), calls=%async_computation.17 | async-start | bytes 12976128 | tf_op jit(solution)/shard_map/reduce_scatter | solution.py:332
  915.7 916.9 %reduce-scatter.16.cloned.1.call-start = ((), (), s32[]{:S(2)}) async-start(), calls=%async_computation.18 | async-start | bytes 41091072 | tf_op jit(solution)/shard_map/reduce_scatter | solution.py:263
  937.5 1321.2 %reduce-scatter.18.cloned.1.call-start = ((), (), s32[]{:S(2)}) async-start(), calls=%async_computation.19 | async-start | bytes 41091072 | tf_op jit(solution)/shard_map/reduce_scatter | solution.py:264
  958.7 1725.8 %reduce-scatter.20.cloned.1.call-start = ((), (), s32[]{:S(2)}) async-start(), calls=%async_computation.20 | async-start | bytes 41091072 | tf_op jit(solution)/shard_map/reduce_scatter | solution.py:265
  (47 other events, 543.5 us)
Sparse Core Ops, SparseCore 0:
  10.9 57.4 all-gather.7
  71.3 53.8 all-gather.9
  128.0 69.6 all-gather.11
  200.4 68.0 all-gather.13
  271.3 127.9 all-gather.15
  402.1 127.5 all-gather.17
  532.6 127.5 all-gather.19
  878.2 98.0 reduce-scatter.9
  982.2 100.4 reduce-scatter.11
  1089.2 154.6 reduce-scatter.7
  1251.6 154.4 reduce-scatter.13
  1408.8 423.8 reduce-scatter.15
  1835.6 423.0 reduce-scatter.17
  2261.4 423.0 reduce-scatter.19
where the time goes:
time: 2700 us; the launch traced here: 2690 us
  waiting for transfers between devices  2110 us (78%)
  matrix products  361 us (13%)
  other arithmetic  90.1 us (3%)
  blocking collectives  79.8 us (3%)
  local copies, waits for them, and re-layouts  29.6 us (1%)
    reduce_scatter x1, waiting for transfers between devices, body(): lax.psum_scatter(grad_gate_w, ('seq', 'fsdp'), scatter_dimension=0, tiled...  427 us
    reduce_scatter x1, waiting for transfers between devices, body(): lax.psum_scatter(grad_up_w, ('seq', 'fsdp'), scatter_dimension=0, tiled=T...  426 us
    reduce_scatter x1, waiting for transfers between devices, body(): lax.psum_scatter(grad_down_w, ('seq', 'fsdp'), scatter_dimension=0, tiled...  426 us
    reduce_scatter x1, waiting for transfers between devices, body(): lax.psum_scatter(grad_out_w, ('seq', 'fsdp'), scatter_dimension=0, tiled=...  162 us
    reduce_scatter x1, waiting for transfers between devices, body(): lax.psum_scatter(grad_query_w, ('seq', 'fsdp'), scatter_dimension=0, tile...  161 us
    all_gather x1, waiting for transfers between devices, body(): lax.all_gather(w_down, ('seq', 'fsdp'), axis=0, tiled=True)  113 us
    all_gather x1, waiting for transfers between devices, body(): lax.all_gather(w_up, ('seq', 'fsdp'), axis=0, tiled=True)  113 us
    all_gather x1, waiting for transfers between devices, body(): lax.all_gather(w_gate, ('seq', 'fsdp'), axis=0, tiled=True)  111 us
  transfers between devices with their start and end apart: 16, of which 14 were waited for; matrix products, arithmetic and copies ran while one was open for 10% of the time, Pallas kernels for 0%

commit v1 on v0

v1 whole, which is shorter than its diff:
```python
import functools
import math

import jax
import jax.numpy as jnp
from jax import lax
from jax.experimental import pallas as pl
from jax.experimental.pallas import tpu as pltpu
from jax.sharding import Mesh, PartitionSpec as P

EPS = 1e-06
BF = jnp.bfloat16
F32 = jnp.float32
HEAD_SIZE = 64
TILE = 128
SCALE = HEAD_SIZE ** (-0.5)
VMEM_LIMIT = 56 * 2**20


def dot(a, b):
    return lax.dot_general(a, b, (((1,), (0,)), ((), ())), preferred_element_type=F32)


def dot_nt(a, b):
    return lax.dot_general(a, b, (((1,), (1,)), ((), ())), preferred_element_type=F32)


def dot_tn(a, b):
    return lax.dot_general(a, b, (((0,), (0,)), ((), ())), preferred_element_type=F32)


def call(kernel, grid, in_specs, out_specs, out_shape, name, scratch=(), scalars=()):
    scalars = [jnp.asarray(s, jnp.int32).reshape(-1) for s in scalars]
    return functools.partial(
        pl.pallas_call(
            kernel,
            grid_spec=pltpu.PrefetchScalarGridSpec(
                num_scalar_prefetch=len(scalars),
                grid=grid,
                in_specs=in_specs,
                out_specs=out_specs,
                scratch_shapes=scratch,
            ),
            out_shape=out_shape,
            compiler_params=pltpu.CompilerParams(vmem_limit_bytes=VMEM_LIMIT),
            name=name,
        ),
        *scalars,
    )


def shaped(shape, dtype):
    return jax.ShapeDtypeStruct(shape, dtype)


def whole(shape):
    return pl.BlockSpec(shape, lambda *_: (0,) * len(shape))


def once(shape):
    return pl.BlockSpec(shape, lambda *_: (0,) * len(shape), pipeline_mode=pl.Buffered(1))


def row_blocks(tile, cols):
    return pl.BlockSpec((tile, cols), lambda i, *_: (i, 0))


def group_blocks(tile, cols, group, per_group):
    return pl.BlockSpec(
        (tile, cols), lambda i, *_: (jnp.clip(i - group * per_group, 0, per_group - 1), 0)
    )


def pick_group(refs, per_group):
    value = refs[0][...]
    for g in range(1, len(refs)):
        value = jnp.where(pl.program_id(0) >= g * per_group, refs[g][...], value)
    return value


def lane_of(shape):
    return lax.broadcasted_iota(jnp.int32, shape, 1)


def half_sums(values, even):
    low = jnp.sum(jnp.where(even, values, 0.0), axis=-1, keepdims=True)
    high = jnp.sum(jnp.where(even, 0.0, values), axis=-1, keepdims=True)
    return jnp.where(even, low, high)


def turned(values, first):
    return jnp.where(first, pltpu.roll(values, TILE - 32, 1), pltpu.roll(values, 32, 1))


def project(groups, weight_all, core, q_gain, k_gain, cos, sin, q_cols, kv_cols):
    half, width = groups[0].shape
    cols = q_cols + 2 * kv_cols
    q_tiles, k_heads = q_cols // TILE, kv_cols // HEAD_SIZE
    raw_cols = (q_tiles + (k_heads + 1) // 2) * TILE
    tile = 256
    per = half // tile
    count = len(groups)
    rows = count * half

    def kernel(core_ref, *refs):
        hid, (w_ref, qg_ref, kg_ref, cos_ref, sin_ref, q_ref, kv_ref, raw_ref) = refs[:count], refs[count:]
        lane = lane_of((tile, TILE))
        even, first = lane < HEAD_SIZE, lane % HEAD_SIZE < HEAD_SIZE // 2
        out = dot(pick_group(hid, per), w_ref[...])
        cos, sin = cos_ref[...], sin_ref[...]
        raw_ref[...] = out[:, :raw_cols]
        for t in range(cols // TILE):
            x = out[:, t * TILE : (t + 1) * TILE]
            heads_left = k_heads - 2 * (t - q_tiles)
            y = x
            if heads_left > 0:
                gain = qg_ref[...] if t < q_tiles else kg_ref[...]
                y = x * lax.rsqrt(half_sums(x * x, even) * (1.0 / HEAD_SIZE) + EPS) * gain
                y = y * cos + turned(y, first) * sin
                if t >= q_tiles and heads_left == 1:
                    y = jnp.where(even, y, x)
            if t < q_tiles:
                q_ref[:, t * TILE : (t + 1) * TILE] = y.astype(BF)
            else:
                kv_ref[:, (t - q_tiles) * TILE : (t - q_tiles + 1) * TILE] = y.astype(BF)

    return call(
        kernel,
        (rows // tile,),
        [group_blocks(tile, width, g, per) for g in range(count)]
        + [pl.BlockSpec((width, cols), lambda i, c: (0, c[0]), pipeline_mode=pl.Buffered(1))]
        + [whole((1, TILE))] * 2 + [row_blocks(tile, TILE)] * 2,
        [row_blocks(tile, q_cols), row_blocks(tile, 2 * kv_cols), row_blocks(tile, raw_cols)],
        [shaped((rows, q_cols), BF), shaped((rows, 2 * kv_cols), BF), shaped((rows, raw_cols), F32)],
        "project_heads",
        scalars=[core],
    )(*groups, weight_all, q_gain, k_gain, cos, sin)


def head_grads(parts, raw, first_tile, heads, gain, cos, sin):
    rows, cols = parts[0].shape
    normed = (heads + 1) // 2
    count, tile = len(parts), 256

    def kernel(*refs):
        ds, (raw_ref, gain_ref, cos_ref, sin_ref, g_ref, sum_ref) = refs[:count], refs[count:]
        lane = lane_of((tile, TILE))
        even, first = lane < HEAD_SIZE, lane % HEAD_SIZE < HEAD_SIZE // 2
        cos, sin, gain = cos_ref[...], sin_ref[...], gain_ref[...]

        @pl.when(pl.program_id(0) == 0)
        def _():
            sum_ref[...] = jnp.zeros_like(sum_ref)

        for t in range(cols // TILE):
            at = slice(t * TILE, (t + 1) * TILE)
            d = sum(ref[:, at].astype(F32) for ref in ds)
            y = d
            if t < normed:
                x = raw_ref[:, at]
                r = lax.rsqrt(half_sums(x * x, even) * (1.0 / HEAD_SIZE) + EPS)
                n = x * r
                back = d * cos - turned(d, first) * sin
                dn = back * n
                w = back * gain
                y = r * (w - n * (half_sums(w * n, even) * (1.0 / HEAD_SIZE)))
                if heads - 2 * t == 1:
                    y = jnp.where(even, y, d)
                    dn = jnp.where(even, dn, 0.0)
                sum_ref[...] += jnp.sum(dn.reshape(tile // 8, 8, TILE), axis=0)
            g_ref[:, at] = y.astype(BF)

    raw_at = first_tile // normed
    return call(
        kernel,
        (rows // tile,),
        [row_blocks(tile, cols)] * count
        + [pl.BlockSpec((tile, normed * TILE), lambda i: (i, raw_at)), whole((1, TILE))]
        + [row_blocks(tile, TILE)] * 2,
        [row_blocks(tile, cols), whole((8, TILE))],
        [shaped((rows, cols), BF), shaped((8, TILE), F32)],
        "head_grads",
    )(*parts, raw, gain, cos, sin)


def stacked(ref, g, even):
    out = []
    for p in range(2):
        pair = ref[0, :, (2 * g + p) * TILE : (2 * g + p + 1) * TILE]
        zero = jnp.zeros_like(pair)
        out += [jnp.where(even, pair, zero), jnp.where(even, zero, pair)]
    return jnp.concatenate(out, axis=0)


def unstacked(values, p, even):
    base = 2 * p * TILE
    return jnp.where(even, values[base : base + TILE], values[base + TILE : base + 2 * TILE])


def widen(refs, k_ref, v_ref, heads):
    at = 0
    for ref in refs:
        for r in range(0, ref.shape[1], TILE):
            rows = slice(at, at + TILE)
            lane = lane_of((TILE, TILE))
            even = lane < HEAD_SIZE
            for t in range(heads):
                x = ref[0, r : r + TILE, t * TILE : (t + 1) * TILE].astype(F32)
                other = pltpu.roll(x, HEAD_SIZE, 1)
                for part, value in enumerate((jnp.where(even, x, other), jnp.where(even, other, x))):
                    n = 2 * t + part
                    out = k_ref if n < heads else v_ref
                    out[rows, (n % heads) * TILE : (n % heads + 1) * TILE] = value.astype(BF)
            at += TILE


def narrow(k_ref, v_ref, rows, t, heads, even):
    tiles = []
    for n in (2 * t, 2 * t + 1):
        ref, scale = (k_ref, SCALE) if n < heads else (v_ref, 1.0)
        x = ref[rows, (n % heads) * TILE : (n % heads + 1) * TILE]
        tiles.append((x + pltpu.roll(x, HEAD_SIZE, 1)) * scale)
    return jnp.where(even, tiles[0], tiles[1])


def attend(low_block, q, kv_prior, kv, qseg, kseg):
    batch, rows, cols = q.shape
    blocks = rows // TILE
    heads = kv.shape[2] // TILE
    keys = 2 * rows

    def kernel(lo_ref, q_ref, prior_ref, kv_ref, qseg_ref, kseg_ref, o_ref, lse_ref, acc_ref, sum_ref, k_ref, v_ref):
        b, i = pl.program_id(0), pl.program_id(1)
        lane = lane_of((TILE, TILE))
        even = lane < HEAD_SIZE

        @pl.when(i == 0)
        def _():
            widen((prior_ref, kv_ref), k_ref, v_ref, heads)

        qs = [stacked(q_ref, g, even) for g in range(heads)]
        acc_ref[...] = jnp.zeros_like(acc_ref)
        sum_ref[...] = jnp.zeros_like(sum_ref)
        seg = qseg_ref[0]
        row_at = lax.broadcasted_iota(jnp.int32, (TILE, TILE), 0) + (i + blocks) * TILE

        def step(j, carry):
            at = pl.ds(pl.multiple_of(j * TILE, TILE), TILE)
            ok = (seg == kseg_ref[0, pl.ds(j, 1), :]) & (lane + j * TILE <= row_at)
            bias = jnp.where(ok, 0.0, -1e30)
            bias = jnp.concatenate([bias] * 4, axis=0)
            for g in range(heads):
                col = slice(g * TILE, (g + 1) * TILE)
                e = jnp.exp(dot_nt(qs[g], k_ref[at, col]) * SCALE + bias)
                sum_ref[g] += e
                acc_ref[g] += dot(e.astype(BF), v_ref[at, col])
            return carry

        lax.fori_loop(lo_ref[b * blocks + i], i + blocks + 1, step, 0)
        lse = jnp.zeros((TILE, TILE), F32)
        for g in range(heads):
            total = jnp.sum(sum_ref[g], axis=-1, keepdims=True)
            out = acc_ref[g] / total
            log = jnp.log(total)
            for p in range(2):
                o_ref[0, :, (2 * g + p) * TILE : (2 * g + p + 1) * TILE] = unstacked(out, p, even).astype(BF)
            for h in range(4):
                lse = jnp.where(lane == 4 * g + h, log[h * TILE : (h + 1) * TILE], lse)
        lse_ref[0] = lse

    per_q = lambda n: pl.BlockSpec((1, TILE, n), lambda b, i, lo: (b, i, 0))
    per_b = lambda s: pl.BlockSpec((1,) + s[1:], lambda b, i, lo: (b, 0, 0))
    return call(
        kernel,
        (batch, blocks),
        [per_q(cols), per_b(kv.shape), per_b(kv.shape), per_q(1), per_b(kseg.shape)],
        [per_q(cols), per_q(TILE)],
        [shaped(q.shape, BF), shaped((batch, rows, TILE), F32)],
        "attend",
        [pltpu.VMEM((heads, 4 * TILE, TILE), F32)] * 2 + [pltpu.VMEM((keys, heads * TILE), BF)] * 2,
        [low_block],
    )(q, kv_prior, kv, qseg, kseg)


def attend_back(low_block, q, kv_prior, kv, qseg, kseg, o, lse, do):
    batch, rows, cols = q.shape
    blocks = rows // TILE
    heads = kv.shape[2] // TILE
    keys = 2 * rows

    def kernel(lo_ref, q_ref, prior_ref, kv_ref, qseg_ref, kseg_ref, o_ref, lse_ref, do_ref, dq_ref, dprior_ref, dkv_ref, acc_ref, k_ref, v_ref, dk_ref, dv_ref):
        b, i = pl.program_id(0), pl.program_id(1)
        lane = lane_of((TILE, TILE))
        even = lane < HEAD_SIZE

        @pl.when(i == 0)
        def _():
            widen((prior_ref, kv_ref), k_ref, v_ref, heads)
            dk_ref[...] = jnp.zeros_like(dk_ref)
            dv_ref[...] = jnp.zeros_like(dv_ref)

        qs = [stacked(q_ref, g, even) for g in range(heads)]
        dos = [stacked(do_ref, g, even) for g in range(heads)]
        lses, deltas = [], []
        for g in range(heads):
            os = stacked(o_ref, g, even)
            deltas.append(jnp.sum(os.astype(F32) * dos[g].astype(F32), axis=-1, keepdims=True))
            each = [
                jnp.sum(jnp.where(lane == 4 * g + h, lse_ref[0], 0.0), axis=-1, keepdims=True)
                for h in range(4)
            ]
            lses.append(jnp.concatenate(each, axis=0))
        acc_ref[...] = jnp.zeros_like(acc_ref)
        seg = qseg_ref[0]
        row_at = lax.broadcasted_iota(jnp.int32, (TILE, TILE), 0) + (i + blocks) * TILE

        def step(j, carry):
            at = pl.ds(pl.multiple_of(j * TILE, TILE), TILE)
            ok = (seg == kseg_ref[0, pl.ds(j, 1), :]) & (lane + j * TILE <= row_at)
            bias = jnp.where(ok, 0.0, -1e30)
            bias = jnp.concatenate([bias] * 4, axis=0)
            for g in range(heads):
                col = slice(g * TILE, (g + 1) * TILE)
                k, v = k_ref[at, col], v_ref[at, col]
                p = jnp.exp(dot_nt(qs[g], k) * SCALE + (bias - lses[g]))
                ds = (p * (dot_nt(dos[g], v) - deltas[g])).astype(BF)
                dv_ref[at, col] += dot_tn(p.astype(BF), dos[g])
                dk_ref[at, col] += dot_tn(ds, qs[g])
                acc_ref[g] += dot(ds, k)
            return carry

        lax.fori_loop(lo_ref[b * blocks + i], i + blocks + 1, step, 0)
        for g in range(heads):
            for p in range(2):
                dq_ref[0, :, (2 * g + p) * TILE : (2 * g + p + 1) * TILE] = (
                    unstacked(acc_ref[g], p, even) * SCALE
                )

        @pl.when(i == blocks - 1)
        def _():
            for r in range(0, rows, TILE):
                for t in range(heads):
                    col = slice(t * TILE, (t + 1) * TILE)
                    dprior_ref[0, r : r + TILE, col] = narrow(
                        dk_ref, dv_ref, slice(r, r + TILE), t, heads, even
                    ).astype(BF)
                    dkv_ref[0, r : r + TILE, col] = narrow(
                        dk_ref, dv_ref, slice(rows + r, rows + r + TILE), t, heads, even
                    )

    per_q = lambda n: pl.BlockSpec((1, TILE, n), lambda b, i, lo: (b, i, 0))
    per_b = lambda s: pl.BlockSpec((1,) + s[1:], lambda b, i, lo: (b, 0, 0))
    wide = (keys, heads * TILE)
    return call(
        kernel,
        (batch, blocks),
        [per_q(cols), per_b(kv.shape), per_b(kv.shape), per_q(1), per_b(kseg.shape)]
        + [per_q(cols), per_q(TILE), per_q(cols)],
        [per_q(cols), per_b(kv.shape), per_b(kv.shape)],
        [shaped(q.shape, F32), shaped(kv.shape, BF), shaped(kv.shape, F32)],
        "attend_back",
        [pltpu.VMEM((heads, 4 * TILE, TILE), F32)]
        + [pltpu.VMEM(wide, BF)] * 2 + [pltpu.VMEM(wide, F32)] * 2,
        [low_block],
    )(q, kv_prior, kv, qseg, kseg, o, lse, do)


def hidden_units(hidden, low, gate_up, down):
    half, width = hidden[0].shape
    cols = down.shape[0]
    tile = 256
    per = half // tile
    count = len(hidden)

    def kernel(*refs):
        hid, lows = refs[:count], refs[count : 2 * count]
        gu_ref, wd_ref, act_ref, grad_ref = refs[2 * count :]
        x, y = pick_group(hid, per), pick_group(lows, per)
        step = 256
        for c in range(0, cols, step):
            n = min(step, cols - c)
            gate = dot(x, gu_ref[:, c : c + n])
            up = dot(x, gu_ref[:, cols + c : cols + c + n])
            grad = dot_nt(y, wd_ref[c : c + n, :])
            sig = 1.0 / (1.0 + jnp.exp(-gate))
            silu = gate * sig
            act_ref[:, c : c + n] = (silu * up).astype(BF)
            grad_ref[:, c : c + n] = (grad * up * (sig * (1.0 + gate * (1.0 - sig)))).astype(BF)
            grad_ref[:, cols + c : cols + c + n] = (grad * silu).astype(BF)

    groups = [group_blocks(tile, width, g, per) for g in range(count)]
    rows = count * half
    return call(
        kernel,
        (rows // tile,),
        groups + groups + [once(gate_up.shape), once(down.shape)],
        [row_blocks(tile, cols), row_blocks(tile, 2 * cols)],
        [shaped((rows, cols), BF), shaped((rows, 2 * cols), BF)],
        "hidden_units",
    )(*hidden, *low, gate_up, down)


def tall_grad(groups, rights, bit, name):
    half, width = groups[0].shape
    cols = rights[0].shape[1]
    count, pairs = len(groups), len(rights)
    tile = 512
    steps = width // tile
    split = bit is not None
    side = steps // 2 if split else 0

    def kernel(bit_ref, *refs):
        lefts, right, outs = refs[:count], refs[count : count + pairs], refs[count + pairs :]
        total = None
        for g in range(count):
            r = right[g // 2][(g % 2) * half : (g % 2 + 1) * half, :]
            term = dot_tn(lefts[g][...], r)
            total = term if total is None else total + term

        @pl.when(pl.program_id(0) >= side)
        def _():
            outs[0][...] = total.astype(BF)

        if split:

            @pl.when(pl.program_id(0) < side)
            def _():
                outs[1][...] = total.astype(BF)

    def column(i, bit):
        if not split:
            return (0, i)
        return (0, i % side + side * jnp.where(i >= side, bit[0], 1 - bit[0]))

    out_specs = [pl.BlockSpec((tile, cols), lambda i, b: (jnp.maximum(i - side, 0), 0))]
    if split:
        out_specs.append(pl.BlockSpec((tile, cols), lambda i, b: (jnp.minimum(i, side - 1), 0)))
    return call(
        kernel,
        (steps,),
        [pl.BlockSpec((half, tile), column)] * count + [once(r.shape) for r in rights],
        out_specs,
        [shaped(((steps - side) * tile, cols), BF)] * len(out_specs),
        name,
        scalars=[bit if split else 0],
    )(*groups, *rights)


def wide_grad(lefts, groups, name):
    half, width = groups[0].shape
    cols = lefts[0].shape[1]
    count, pairs = len(groups), len(lefts)
    tile = 512

    def kernel(*refs):
        total = None
        for g in range(count):
            left = refs[g // 2][(g % 2) * half : (g % 2 + 1) * half, :]
            term = dot_tn(left, refs[pairs + g][...])
            total = term if total is None else total + term
        refs[-1][...] = total.astype(BF)

    return call(
        kernel,
        (width // tile,),
        [once(a.shape) for a in lefts] + [pl.BlockSpec((half, tile), lambda i: (0, i))] * count,
        pl.BlockSpec((cols, tile), lambda i: (0, i)),
        shaped((cols, width), BF),
        name,
    )(*lefts, *groups)


def sum_products(lefts, rights, transposed, name, core=0, part=None):
    rows = lefts[0].shape[0]
    width = rights[0].shape[0] if transposed else rights[0].shape[1]
    tile, count = 512, len(lefts)

    def kernel(core_ref, *refs):
        total = None
        for a, b in zip(refs[:count], refs[count : 2 * count]):
            term = dot_nt(a[...], b[...]) if transposed else dot(a[...], b[...])
            total = term if total is None else total + term
        refs[-2][...] = total[: rows // 2]
        refs[-1][...] = total[rows // 2 :].astype(BF)

    at = lambda c: c[0] if part else 0
    if transposed:
        right = [
            pl.BlockSpec((tile, part or r.shape[1]), lambda i, c: (i, at(c))) for r in rights
        ]
    else:
        right = [
            pl.BlockSpec((part or r.shape[0], tile), lambda i, c: (at(c), i)) for r in rights
        ]
    column = pl.BlockSpec((rows // 2, tile), lambda i, c: (0, i))
    return call(
        kernel,
        (width // tile,),
        [once(a.shape) for a in lefts] + right,
        [column, column],
        [shaped((rows // 2, width), F32), shaped((rows // 2, width), BF)],
        name,
        scalars=[core],
    )(*lefts, *rights)


def first_sum(grad_q, grad_kv, weights, core):
    rows, part = grad_kv.shape
    width, tile = weights.shape[0], 512
    count = grad_q.shape[1] // part + 1

    def kernel(core_ref, *refs):
        total = None
        for a, b in zip(refs[:count], refs[count : 2 * count]):
            term = dot_nt(a[...], b[...])
            total = term if total is None else total + term
        refs[-2][...] = total[: rows // 2]
        refs[-1][...] = total[rows // 2 :].astype(BF)

    column_of = lambda n: pl.BlockSpec(
        (rows, part), lambda i, c: (0, n), pipeline_mode=pl.Buffered(1)
    )
    weight_of = lambda n: pl.BlockSpec((tile, part), lambda i, c: (i, count * c[0] + n))
    column = pl.BlockSpec((rows // 2, tile), lambda i, c: (0, i))
    return call(
        kernel,
        (width // tile,),
        [column_of(n) for n in range(count - 1)] + [column_of(0)]
        + [weight_of(n) for n in range(count)],
        [column, column],
        [shaped((rows // 2, width), F32), shaped((rows // 2, width), BF)],
        "first_sum",
        scalars=[core],
    )(*[grad_q] * (count - 1), grad_kv, *[weights] * count)


def token_product(groups, weight, core, part, name):
    half, width = groups[0].shape
    tile = 256
    per, count = half // tile, len(groups)

    def kernel(core_ref, *refs):
        refs[-1][...] = dot_nt(pick_group(refs[:count], per), refs[count][...]).astype(BF)

    return call(
        kernel,
        (count * per,),
        [group_blocks(tile, width, g, per) for g in range(count)]
        + [pl.BlockSpec((part, width), lambda i, c: (c[0], 0), pipeline_mode=pl.Buffered(1))],
        row_blocks(tile, part),
        shaped((count * half, part), BF),
        name,
        scalars=[core],
    )(*groups, weight)


def unit_moves(groups, size, pieces, padded):
    moves = []
    for n in range(2):
        for j, (a, b) in enumerate(pieces):
            for owner in range(4 * groups):
                at = ((2 * j + n) * groups + owner // 4) * padded
                moves.append((n, owner % 4, owner * size + a, at, b - a))
    return moves


def split_units(gate, up, groups, size, pieces, padded):
    rows, cols = gate.shape
    moves = unit_moves(groups, size, pieces, padded)
    share = 2 * len(pieces) * groups * padded

    def kernel(gate_ref, up_ref, out_ref, wide, kinds):
        kinds[...] = jnp.zeros_like(kinds)
        for n, ref in enumerate((gate_ref, up_ref)):
            wide[...] = ref[...].astype(F32)
            for m, c, src, dst, width in moves:
                if m == n:
                    kinds[c, :, dst : dst + width] = wide[:, src : src + width]
        out_ref[...] = kinds[...].astype(BF)

    out = shaped((4, rows, share), BF)
    return call(
        kernel,
        (1,),
        [whole((rows, cols))] * 2,
        whole(out.shape),
        out,
        "split_units",
        [pltpu.VMEM((rows, cols), F32), pltpu.VMEM(out.shape, F32)],
    )(gate, up)


def join_units(classes, groups, size, pieces, padded):
    rows = classes[0].shape[0]
    moves = unit_moves(groups, size, pieces, padded)

    def kernel(a_ref, b_ref, c_ref, d_ref, gate_ref, up_ref):
        for n, c, src, dst, width in moves:
            ref = (a_ref, b_ref, c_ref, d_ref)[c]
            (gate_ref, up_ref)[n][:, src : src + width] = ref[:, dst : dst + width]

    out = shaped((rows, 4 * groups * size), F32)
    return call(
        kernel,
        (1,),
        [whole(classes[0].shape)] * 4,
        [whole(out.shape)] * 2,
        [out] * 2,
        "join_units",
    )(*classes)


QUERY_HEADS = 24
KEY_VALUE_HEADS = 6
AXES = ("seq", "z", "x", "core")
CHUNKS = 2
UNITS, DOWN, OUT, QKV = range(4)
PLAN = {
    (UNITS, 0): (0, 1, 2),
    (DOWN, 0): (0, 1, 2),
    (UNITS, 1): (1, 2, 3),
    (DOWN, 1): (2, 3, 4),
    (DOWN, 0, True): (5, 6, 7),
    (UNITS, 0, True): (5, 6, 7),
    (DOWN, 1, True): (6, 7, 8),
    (UNITS, 1, True): (7, 8, 9),
    (OUT, 0, True): (9, 10, 11, 12),
    (OUT, 1, True): (9, 10, 11, 12),
    (QKV, 0, True): (11, 12, 13, 14),
    (QKV, 1, True): (12, 13, 14, 15),
}


def swap_core(value):
    return lax.ppermute(value, "core", [(0, 1), (1, 0)])


def core_pick(first, second):
    return jnp.where(lax.axis_index("core") == 0, first, second)


def core_concat(own, other, axis=0):
    return core_pick(
        jnp.concatenate([own, other], axis=axis), jnp.concatenate([other, own], axis=axis)
    )


def swap_seq(value):
    return lax.ppermute(value, "seq", [(0, 1), (1, 0)])


def swap_x(value):
    return lax.ppermute(value, "x", [(0, 1), (1, 0)])


def x_pick(first, second):
    return jnp.where(lax.axis_index("x") == 0, first, second)


def group_axes():
    bits = lax.axis_size("z").bit_length() - 1
    return [("seq", 1)] + [("z", 1 << k) for k in reversed(range(bits))]


def orders_of(name):
    cube = group_axes()
    far, near, seq = cube[1:-1], cube[-1:], cube[:1]
    what, number = name[:2]
    if what in (OUT, QKV):
        x = [("x", 1)]
        cube = cube + x
        stages = [far, seq, near, x] if number else [far, x, near, seq]
    else:
        stages = [far, seq, near] if what == DOWN else [far, near, seq]
    return cube, [s[::-1] for s in stages[::-1]] if len(name) > 2 else stages


def hop_bit(hop):
    axis, step = hop
    return lax.axis_index(axis) // step % 2


def exchange(value, hop):
    axis, step = hop
    return lax.ppermute(value, axis, [(i, i ^ step) for i in range(lax.axis_size(axis))])


def place_kernel(bit_ref, own_ref, got_ref, out_ref):
    bit = bit_ref[0]
    out_ref[:, pl.ds(bit, 1)] = own_ref[...][:, None]
    out_ref[:, pl.ds(1 - bit, 1)] = got_ref[...][:, None]


def placed(own, got, dim, bit):
    shape = own.shape
    lead, inner = math.prod(shape[:dim]), math.prod(shape[dim:-2])
    flat = (lead, inner) + shape[-2:]
    part = math.gcd(inner, 2) if lead == 1 else inner
    block = (1, part) + shape[-2:]
    side = pl.BlockSpec(block, lambda i, j, bit: (i, j, 0, 0))
    out = call(
        place_kernel,
        (lead, inner // part),
        [side, side],
        pl.BlockSpec((1, 2) + block[1:], lambda i, j, bit: (i, 0, j, 0, 0)),
        shaped((lead, 2) + flat[1:], own.dtype),
        "place",
        scalars=[bit],
    )(own.reshape(flat), got.reshape(flat))
    return out.reshape(shape[:dim] + (2,) + shape[dim + 1 :])


class Values:
    def __init__(self):
        for name in ("low", "hidden", "wgu", "wd", "act", "ggu", "keep", "home"):
            setattr(self, name, {})


class Flow:
    def __init__(self):
        self.live = Values()
        self.rest, self.flight, self.later, self.stage, self.now = {}, {}, {}, {}, 0

    def fence(self):
        values, parts = lax.optimization_barrier((vars(self.live), self.rest))
        vars(self.live).update(values)
        self.rest = parts

    def gather(self, name, block):
        self.rest[name] = block.reshape((1,) * len(orders_of(name)[0]) + block.shape)
        self.stage[name] = 0

    def scatter(self, name, rows, grad, sent=None):
        self.stage[name] = 0
        shape = [2] * len(orders_of(name)[0])
        if sent is None:
            self.rest[name] = grad.reshape(shape + [rows, grad.shape[1]])
        else:
            shape[self.hop(name)[1]] = 1
            self.rest[name] = tuple(v.reshape(shape + [rows, v.shape[1]]) for v in (grad, sent))

    def hop(self, name):
        cube, stages = orders_of(name)
        hop = sum(stages, [])[self.stage[name]]
        return hop, cube.index(hop)

    def start(self, name):
        hop, dim = self.hop(name)
        bit, value = hop_bit(hop), self.rest.pop(name)
        if isinstance(value, tuple):
            value, sent = value
        elif len(name) > 2:
            sent = lax.dynamic_slice_in_dim(value, 1 - bit, 1, dim)
        else:
            sent = value
        self.flight[name] = (value, exchange(sent, hop), dim, bit)

    def land(self, name):
        keep, got, dim, bit = self.flight.pop(name)
        self.stage[name] += 1
        stages = orders_of(name)[1]
        ends = [sum(map(len, stages[: k + 1])) for k in range(len(stages))]
        last = self.stage[name] == ends[-1]
        if len(name) > 2:
            if keep.shape[dim] == 2:
                keep = lax.dynamic_slice_in_dim(keep, bit, 1, dim)
            total = keep.astype(F32) + got.astype(F32)
            self.rest[name] = total if last else total.astype(BF)
        elif last:
            self.rest[name] = (keep, got)
            self.stage[name] = (dim, bit)
        else:
            self.rest[name] = placed(keep, got, dim, bit)
        if not last and self.stage[name] not in ends:
            self.start(name)
            self.land(name)

    def take(self, name):
        value = self.rest.pop(name)
        dims = len(orders_of(name)[0])
        if len(name) > 2:
            return value.reshape(value.shape[dims:])
        value = placed(*value, *self.stage[name])
        return value.reshape((-1,) + value.shape[dims + 1 :])

    def post(self, value, name, key=None, wait=0):
        self.later[name, key] = (value, self.now + wait)

    def interval(self, *work):
        active = [name for name, at in PLAN.items() if self.now in at]
        for name in active:
            self.start(name)
        for piece in work:
            piece()
        for name in active:
            self.land(name)
        for name, key in [n for n, (_, at) in self.later.items() if at == self.now]:
            value = self.later.pop((name, key))[0]
            if key is None:
                setattr(self.live, name, value)
            else:
                getattr(self.live, name)[key] = value
        self.fence()
        self.now += 1


def row_norm(values):
    scale = lax.rsqrt(jnp.mean(values * values, axis=-1, keepdims=True) + EPS)
    return values * scale, scale


def norm_back(grad, normed, scale, gain):
    u = grad * gain
    return scale * (u - normed * jnp.mean(u * normed, axis=-1, keepdims=True))


def doc_positions(segment_row):
    length = segment_row.shape[-1]
    places = jnp.arange(length, dtype=jnp.int32)
    earlier = jnp.concatenate([segment_row[..., :1] + 1, segment_row[..., :-1]], axis=-1)
    starts = jnp.where(segment_row != earlier, places, 0)
    latest = jnp.max(
        jnp.where(places[None, :] <= places[:, None], starts[..., None, :], 0), axis=-1
    )
    return places - latest


def rotary_tables(positions):
    pair_count = HEAD_SIZE // 2
    frequencies = jnp.exp(
        jnp.arange(pair_count, dtype=F32) * (-2.0 * math.log(10000.0) / HEAD_SIZE)
    )
    phases = positions.astype(F32)[..., None] * frequencies
    cos, sin = jnp.cos(phases), jnp.sin(phases)
    return jnp.tile(cos, (1, 4)), jnp.tile(jnp.concatenate([-sin, sin], axis=1), (1, 2))


def split_rows(rows, pieces):
    units, rest = rows // 8, rows % 8
    sizes = [8 * (units // pieces + (i < units % pieces)) for i in range(pieces)]
    sizes[-1] += rest
    ends = [sum(sizes[: i + 1]) for i in range(pieces)]
    return [(e - s, e) for s, e in zip(sizes, ends)]


def halves(w):
    n = w.shape[1] // 2
    return w[:, :n], w[:, n:]


def body(
    tokens,
    segments,
    attn_gain,
    w_query,
    key_projection_weight,
    value_projection_weight,
    query_norm_gain,
    key_gain,
    w_out,
    ffn_gain,
    w_gate,
    w_up,
    w_down,
    cotangent,
):
    _, half, width = tokens.shape
    ny, nz, nx = (lax.axis_size(a) for a in ("seq", "z", "x"))
    groups = ny * nz
    core, seq, x_at = (lax.axis_index(a) for a in ("core", "seq", "x"))
    q_cols, kv_cols = w_query.shape[1] // 2, key_projection_weight.shape[1] // 2
    kv_heads = KEY_VALUE_HEADS // 2
    out_rows, ff_rows, in_rows = w_out.shape[0], w_down.shape[0], w_gate.shape[0]
    pieces = split_rows(ff_rows, CHUNKS)
    step = TILE // math.gcd(TILE, groups)
    padded = -(-max(b - a for a, b in pieces) // step) * step
    share = groups * padded
    flow = Flow()
    do = lambda f, *a: (lambda: f(*a))

    def pair(value):
        return [value, swap_core(value)]

    def trade(value):
        return lax.ppermute(value, ("seq", "core"), [(0, 0), (1, 2), (2, 1), (3, 3)])

    weights = (w_query, key_projection_weight, value_projection_weight)
    lows, highs = zip(*(halves(w) for w in weights))
    gains = jnp.pad(jnp.stack([attn_gain, ffn_gain], axis=1), ((0, 0), (0, TILE - 2)))
    qkv_all = lax.all_gather(
        jnp.concatenate(lows + highs + (gains,), axis=1), AXES, axis=0, tiled=True
    )

    quarters = split_units(w_gate, w_up, groups, ff_rows, pieces, padded)
    mine = [core_pick(quarters[2 * x], quarters[2 * x + 1]) for x in range(2)]
    theirs = [core_pick(quarters[2 * x + 1], quarters[2 * x]) for x in range(2)]
    sent = x_pick(jnp.concatenate(theirs), jnp.concatenate(theirs[::-1]))
    got = swap_core(sent)
    near = core_concat(x_pick(mine[0], mine[1]), got[:in_rows])
    far = swap_x(core_concat(x_pick(mine[1], mine[0]), got[in_rows:]))
    block = x_pick(jnp.concatenate([near, far]), jnp.concatenate([far, near]))
    live = flow.live
    for j, (a, b) in enumerate(pieces):
        units_block = block[:, 2 * j * share : 2 * (j + 1) * share]
        down_block = jnp.pad(w_down[a:b], ((0, padded - b + a), (0, 0)))
        flow.gather((UNITS, j), units_block)
        flow.gather((DOWN, j), down_block)
    live.w_out = w_out
    pending = {}

    def gather_qkv():
        flow.live.qkv = qkv_all

    def gather_out():
        pending[OUT] = lax.all_gather(flow.live.w_out, AXES, axis=0, tiled=True)

    def tables():
        live = flow.live
        segments_pair = jnp.concatenate(pair(segments), axis=0)
        positions = doc_positions(segments_pair)
        own_start = seq * half
        own_positions = lax.dynamic_slice_in_dim(positions, own_start, half, 1)
        order_ids = jnp.where(segments_pair < 0, 1 << 20, segments_pair)
        own_ids = lax.dynamic_slice_in_dim(order_ids, own_start, half, 1)
        prior_ids = lax.dynamic_slice_in_dim(order_ids, jnp.maximum(own_start - half, 0), half, 1)
        prior_ids = jnp.where(own_start >= half, prior_ids, -2)
        key_ids = jnp.concatenate([prior_ids, own_ids], axis=1)
        low_block = jnp.sum(key_ids[:, None, :] < own_ids[:, ::TILE, None], axis=-1) // TILE
        live.low_block = low_block.astype(jnp.int32)
        live.query_ids = own_ids[:, :, None]
        live.key_ids = key_ids.reshape(2, -1, TILE)
        live.cos, live.sin = rotary_tables(own_positions.reshape(2 * half))
        live.q_gain = jnp.tile(query_norm_gain.astype(F32), 2).reshape(1, TILE)
        live.k_gain = jnp.tile(key_gain.astype(F32), 2).reshape(1, TILE)

    def first_norm():
        live = flow.live
        live.low[0] = pair(cotangent.reshape(half, width))
        live.normed, live.scale = row_norm(tokens.reshape(half, width).astype(F32))

    def far_low():
        flow.post(swap_x(flow.live.low[0][0]), "far_low")

    def near_low():
        flow.live.low[1] = pair(flow.live.far_low)

    def heads():
        live = flow.live
        n = q_cols + 2 * kv_cols
        live.gains = live.qkv[:, 2 * n : 2 * n + 2].T.astype(F32)
        live.hidden_first = pair((live.normed * live.gains[0]).astype(BF))
        q_rot, kv, live.raw = project(
            live.hidden_first, live.qkv, core, live.q_gain, live.k_gain, live.cos,
            live.sin, q_cols, kv_cols,
        )
        live.q, live.kv = q_rot.reshape(2, half, -1), kv.reshape(2, half, -1)
        flow.post(swap_seq(live.kv), "prior_kv")

    def attention():
        live = flow.live
        attn, live.lse = attend(
            live.low_block, live.q, live.prior_kv, live.kv, live.query_ids,
            live.key_ids,
        )
        live.attn = attn.reshape(2 * half, q_cols)

    def near_rows(sums):
        return sums[0] + swap_core(sums[1]).astype(F32)

    def branch():
        live = flow.live
        live.out = pending.pop(OUT)
        term = near_rows(
            sum_products([live.attn], [live.out], False, "branch", core, q_cols)
        )
        live.middle = tokens.reshape(half, width).astype(F32) + term
        live.normed2, live.scale2 = row_norm(live.middle)
        hidden = (live.normed2 * live.gains[1]).astype(BF)
        live.hidden[0] = pair(hidden)

    def far_hidden():
        flow.post(swap_x(flow.live.hidden[0][0]), "far_hidden")

    def near_hidden():
        flow.live.hidden[1] = pair(flow.live.far_hidden)

    def units(j, h):
        live = flow.live
        if h == 0:
            live.wgu[j], live.wd[j] = flow.take((UNITS, j)), flow.take((DOWN, j))
        live.act[j, h], live.ggu[j, h] = hidden_units(
            live.hidden[h], live.low[h], live.wgu[j], live.wd[j]
        )

    def down_grad(j):
        live = flow.live
        acts = [live.act[j, h] for h in range(2)]
        grad = wide_grad(acts, live.low[0] + live.low[1], "down_grad")
        flow.scatter((DOWN, j, True), padded, grad)

    def units_grad(j):
        live = flow.live
        grads = [live.ggu[j, h] for h in range(2)]
        grads = tall_grad(live.hidden[0] + live.hidden[1], grads, seq, "units_grad")
        flow.scatter((UNITS, j, True), 4 * in_rows, *grads)

    def hidden_sum(h):
        live = flow.live
        js = range(CHUNKS)
        total = near_rows(
            sum_products(
                [live.ggu[j, h] for j in js], [live.wgu[j] for j in js], True, "hidden_sum"
            )
        )
        if h:
            live.far_grad_sum = total.astype(BF)
        else:
            live.near_grad = total

    def far_grad():
        flow.post(swap_x(flow.live.far_grad_sum), "far_grad")

    def down_sum(h):
        live = flow.live
        js = range(CHUNKS)
        total = near_rows(
            sum_products(
                [live.act[j, h] for j in js], [live.wd[j] for j in js], False, "down_sum"
            )
        )
        if h:
            live.far_result_sum = total.astype(BF)
        else:
            live.near_result = total

    def far_result():
        flow.post(swap_x(flow.live.far_result_sum), "far_result")

    def second_back():
        live = flow.live
        grad = live.near_grad + live.far_grad.astype(F32)
        live.grad_middle = cotangent.reshape(half, width).astype(F32) + norm_back(
            grad, live.normed2, live.scale2, live.gains[1]
        )
        live.grad_branch = pair(live.grad_middle.astype(BF))

    def out_grad():
        live = flow.live
        live.grad_attn = token_product(
            live.grad_branch, live.out, core, q_cols, "grad_attn"
        )
        grad = wide_grad([live.attn], live.grad_branch, "out_grad")
        grad = grad.reshape(nz * nx, 2, out_rows, width).transpose(1, 0, 2, 3)
        grad = grad.reshape(groups * nx * out_rows, width)
        flow.scatter((OUT, 0, True), out_rows, grad[:, : width // 2])
        flow.scatter((OUT, 1, True), out_rows, grad[:, width // 2 :])

    def attention_back():
        live = flow.live
        dq, live.sent_dkv, live.dkv = attend_back(
            live.low_block, live.q, live.prior_kv, live.kv, live.query_ids,
            live.key_ids, live.attn.reshape(2, half, q_cols), live.lse,
            live.grad_attn.reshape(2, half, q_cols),
        )
        live.dq = dq.reshape(2 * half, q_cols)

    def prior_back():
        flow.post(swap_seq(flow.live.sent_dkv), "prior_dkv")

    def queries_back():
        live = flow.live
        live.grad_q, live.q_part = head_grads(
            [live.dq], live.raw, 0, q_cols // HEAD_SIZE, live.q_gain, live.cos, live.sin
        )
        grads = tall_grad(live.hidden_first, [live.grad_q], seq, "q_grad")
        flow.scatter((QKV, 0, True), 2 * in_rows, *grads)

    def keys_back():
        live = flow.live
        tall = lambda v: v.reshape(2 * half, -1)
        live.grad_kv, k_part = head_grads(
            [tall(live.dkv), tall(live.prior_dkv)], live.raw, q_cols // TILE,
            kv_cols // HEAD_SIZE, live.k_gain, live.cos, live.sin,
        )
        grad = tall_grad(live.hidden_first, [live.grad_kv], None, "kv_grad")
        flow.scatter((QKV, 1, True), 2 * in_rows, grad[0])
        parts = jnp.stack([live.q_part, k_part]).sum(axis=1)
        live.head_gains = parts.reshape(2, 2, HEAD_SIZE).sum(axis=1)

    def first_back():
        live = flow.live
        grad = near_rows(first_sum(live.grad_q, live.grad_kv, live.qkv, core))
        live.input_grad = live.grad_middle + norm_back(
            grad, live.normed, live.scale, live.gains[0]
        )

    def finish_output():
        live = flow.live
        total = live.near_result + live.far_result.astype(F32)
        live.output = (live.middle + total).astype(BF)

    def gain_hops(hops):
        for hop in hops:
            flow.live.head_gains = flow.live.head_gains + exchange(flow.live.head_gains, hop)

    def home(j):
        rows = flow.take((UNITS, j, True)).reshape(2, 2 * in_rows, -1)
        flow.live.keep[j] = x_pick(rows[0], rows[1])
        flow.post(swap_x(x_pick(rows[1], rows[0])), "home", j)

    def own_shard(block):
        block = block.reshape(2, in_rows, -1)
        got = swap_core(core_pick(block[1], block[0]))
        return core_pick(block[0], block[1]), got

    def gain_grad(gain, pairs):
        total = sum(jnp.sum(w.astype(F32) * g, axis=1) for w, g in pairs)
        return total / gain.astype(F32)

    def finish_units():
        live = flow.live
        classes = []
        near, far = (
            own_shard(jnp.concatenate([v[j] for j in range(CHUNKS)], axis=1))
            for v in (live.keep, live.home)
        )
        for x in range(2):
            keep, got = (x_pick(*((n, f) if x == 0 else (f, n))) for n, f in zip(near, far))
            classes += [core_pick(keep, got), core_pick(got, keep)]
        live.grad_wg, live.grad_wu = join_units(classes, groups, ff_rows, pieces, padded)
        live.ffn_gain = gain_grad(ffn_gain, ((w_gate, live.grad_wg), (w_up, live.grad_wu)))
        downs = [flow.take((DOWN, j, True))[: b - a] for j, (a, b) in enumerate(pieces)]
        live.grad_wd = jnp.concatenate(downs, axis=0)

    def finish_out():
        grad = jnp.concatenate([flow.take((OUT, n, True)) for n in range(2)], axis=1)
        flow.live.grad_wo = trade(grad)

    gain_order = [("core", 1), ("x", 1)] + group_axes()
    schedule = (
        (tables, first_norm, gather_qkv),
        (gather_out, far_low, heads),
        (attention, branch, near_low),
        (far_hidden, do(units, 0, 0)),
        (near_hidden, do(units, 0, 1), do(down_grad, 0), do(units_grad, 0)),
        (do(units, 1, 0), do(units, 1, 1), do(down_grad, 1)),
        (do(units_grad, 1), do(hidden_sum, 1)),
        (far_grad, do(hidden_sum, 0), do(down_sum, 1), do(down_sum, 0)),
        (far_result, do(home, 0), second_back, out_grad),
        (attention_back,),
        (prior_back, do(home, 1), queries_back, finish_output),
        (keys_back,),
        (first_back,),
        (finish_units, do(gain_hops, gain_order[:2])),
        (finish_out, do(gain_hops, gain_order[2:4]),),
        (do(gain_hops, gain_order[4:]),),
    )
    for work in schedule:
        flow.interval(*work)
    live = flow.live

    grads = []
    for n in range(2):
        keep, got = own_shard(flow.take((QKV, n, True)))
        grads.append((core_pick(keep, got), core_pick(got, keep)))
    grad_wq = jnp.concatenate(grads[0], axis=1)
    grad_wk = jnp.concatenate([g[:, :kv_cols] for g in grads[1]], axis=1)
    grad_wv = jnp.concatenate([g[:, kv_cols:] for g in grads[1]], axis=1)
    attn_gain_grad = gain_grad(attn_gain, zip(weights, (grad_wq, grad_wk, grad_wv)))
    return (
        live.output.reshape(1, half, width),
        live.input_grad.reshape(1, half, width),
        attn_gain_grad,
        grad_wq,
        grad_wk,
        grad_wv,
        live.head_gains[0],
        live.head_gains[1],
        live.grad_wo,
        live.ffn_gain,
        live.grad_wg,
        live.grad_wu,
        live.grad_wd,
    )


def solution(mesh):
    ny, nf = mesh.shape["seq"], mesh.shape["fsdp"]
    fine = Mesh(mesh.devices.reshape(ny, nf // 4, 2, 2), AXES)
    fsdp = ("z", "x", "core")
    rows = P(fsdp, "seq", None)
    vec, mat = P(AXES), P(AXES, None)
    in_specs = (rows, P(fsdp, None), vec, mat, mat, mat, P(), P(), mat, vec, mat, mat, mat, rows)
    out_specs = (rows, rows, vec, mat, mat, mat, P(), P(), mat, vec, mat, mat, mat)
    return jax.shard_map(body, mesh=fine, in_specs=in_specs, out_specs=out_specs, check_vma=False)
```

time: 2700 us -> 1050 us (0.39)
  waiting for transfers between devices: 2110 us -> 419 us
  matrix products: 361 us -> 0 us
  Pallas kernels: 0 us -> 343 us
  starting transfers between devices: 5.33 us -> 130 us
  blocking collectives: 79.8 us -> 0 us
    reduce_scatter x7 -> x0, waiting for transfers between devices: 1630 us -> none  [the longest x1 427 us: body(): lax.psum_scatter(grad_gate_w, ('seq', 'fsdp'), scatter_dimension=0, tiled...]
    all_gather x7 -> x2, waiting for transfers between devices: 441 us -> 30.1 us  [the longest x1 30.1 us: body(): lax.all_gather(jnp.concatenate(lows + highs + (gains,), axis=1), AXES, ax...]
    dot_general x27 -> x0, matrix products: 361 us -> none  [the longest x1 34.2 us: attend_back(): jnp.einsum('qhgd,khd->hgqk', grad_heads, value_head_split, preferred_elem...]
    ppermute x2 -> x73, waiting for transfers between devices: 35.6 us -> 389 us  [the longest x45 350 us: exchange(): lax.ppermute(value, axis, [(i, i ^ step) for i in range(lax.axis_size(axi...]
    pallas_call x0 -> x37, Pallas kernels: none -> 343 us  [the longest x4 65.4 us: hidden_units(): call(kernel, (rows // tile,), groups + groups + [once(gate_up.shape), onc...]
    ppermute x2 -> x73, starting transfers between devices: 4.78 us -> 130 us  [the longest x45 64.6 us: exchange(): lax.ppermute(value, axis, [(i, i ^ step) for i in range(lax.axis_size(axi...]
    unnamed x2 -> x0, blocking collectives: 79.8 us -> none
  transfers between devices with their start and end apart: 16 -> 75, of which waited for: 14 -> 29; matrix products, arithmetic and copies ran while one was open for 10% -> 8% of each run, Pallas kernels for 0% -> 30%
where the time goes in v1:
time: 1050 us; the launch traced here: 1040 us
  waiting for transfers between devices  419 us (40%)
  Pallas kernels  343 us (33%)
  starting transfers between devices  130 us (12%)
  other arithmetic  82.7 us (8%)
  local copies, waits for them, and re-layouts  48.1 us (5%)
  between operations  15.8 us (2%)
    ppermute x45, waiting for transfers between devices, exchange(): lax.ppermute(value, axis, [(i, i ^ step) for i in range(lax.axis_size(axi...  350 us
    pallas_call x4, Pallas kernels, hidden_units(): call(kernel, (rows // tile,), groups + groups + [once(gate_up.shape), onc...  65.4 us
    ppermute x45, starting transfers between devices, exchange(): lax.ppermute(value, axis, [(i, i ^ step) for i in range(lax.axis_size(axi...  64.6 us
    pallas_call x5, Pallas kernels, sum_products(): call(kernel, (width // tile,), [once(a.shape) for a in lefts] + right, [c...  60.5 us
    pallas_call x4, Pallas kernels, tall_grad(): call(kernel, (steps,), [pl.BlockSpec((half, tile), column)] * count + [on...  49 us
    pallas_call x12, Pallas kernels, placed(): call(place_kernel, (lead, inner // part), [side, side], pl.BlockSpec((1,...  36 us
    ppermute x2, starting transfers between devices, swap_seq(): return lax.ppermute(value, 'seq', [(0, 1), (1, 0)])  36 us
    ppermute x7, waiting for transfers between devices, swap_x(): return lax.ppermute(value, 'x', [(0, 1), (1, 0)])  34.4 us
  transfers between devices with their start and end apart: 75, of which 29 were waited for; matrix products, arithmetic and copies ran while one was open for 8% of the time, Pallas kernels for 30%

profile of v1, /device:TPU:1, one launch (start us, length us, event | category | flops | bytes accessed | tf_op | source)
XLA Modules:
  0.0 1038.6 jit_solution(10861614640602949840)
XLA Ops:
  52.7 40.6 %collective-permute-done.4 = bf16[1,1,1,256,1280]{4,3,2,1,0:T(8,128)(2,1)S(1)} collective-permute-done((bf16[1,1,1,256,1280]{4,3,2,1,0:T(8,128)(2,1)S(1)}, bf16[1,1,1,256,1280]{4,3,2,1,0:T(8,128)(2,1)S(1)}, u32[]{:S(2)}, u32[]{:S(2)}) %collective-permute-start.4) | collective-permute-done | bytes 655392 | tf_op jit(solution)/shard_map/ppermute | solution.py:685
  96.6 30.1 %all-gather.3.cloned.1.call-done.refs_2_.refs_3_.refs_4_.refs_5_ = bf16[2048,2432]{1,0:T(8,128)(2,1)} async-done(((bf16[64,2432]{1,0:T(8,128)(2,1)}), bf16[2048,2432]{1,0:T(8,128)(2,1)}) %all-gather.3.cloned.1.call-update) | async-done | bytes 9961488 | tf_op jit(solution)/shard_map/all_gather | solution.py:890
  155.1 37.6 %collective-permute-done.10 = bf16[1,1,1,256,1280]{4,3,2,1,0:T(8,128)(2,1)} collective-permute-done((bf16[1,1,1,256,1280]{4,3,2,1,0:T(8,128)(2,1)}, bf16[1,1,1,256,1280]{4,3,2,1,0:T(8,128)(2,1)}, u32[]{:S(2)}, u32[]{:S(2)}) %collective-permute-start.10) | collective-permute-done | bytes 655392 | tf_op jit(solution)/shard_map/ppermute | solution.py:685
  202.1 18.2 %attend.1 = (bf16[2,512,768]{2,1,0:T(8,128)(2,1)}, f32[2,512,128]{2,1,0:T(8,128)}) custom-call(s32[8]{0:T(128)} %reshape.454.lo_ref, bf16[2,512,768]{2,1,0:T(8,128)(2,1)} %bitcast.184, bf16[2,512,384]{2,1,0:T(8,128)(2,1)} %collective-permute-done.8.prior_ref, bf16[2,512,384]{2,1,0:T(8,128)(2,1)} %bitcast.193, s32[2,512,1]{2,1,0:T(8,128)} %copy.67.qseg_ref, ...), custom_call_target="tpu_custom_call" | custom-call | tf_op jit(solution)/shard_map/attend/pallas_call | solution.py:273
  229.0 17.9 %collective-permute-start.15 = (bf16[1,2,2,256,1280]{4,3,2,1,0:T(8,128)(2,1)}, bf16[1,2,2,256,1280]{4,3,2,1,0:T(8,128)(2,1)}, u32[]{:S(2)}, u32[]{:S(2)}) collective-permute-start(bf16[1,2,2,256,1280]{4,3,2,1,0:T(8,128)(2,1)} %bitcast.30), channel_id=1, source_target_pairs={{0,16},{16,0},{1,17},{17,1},{2,18},{18,2},{3,19},{19,3},{4,20},{20... | collective-permute-start | bytes 7864328 | tf_op jit(solution)/shard_map/ppermute | solution.py:685
  274.5 18.3 %collective-permute-done.16 = bf16[1,2,1,256,1280]{4,3,1,2,0:T(8,128)(2,1)} collective-permute-done((bf16[1,2,1,256,1280]{4,3,1,2,0:T(8,128)(2,1)}, bf16[1,2,1,256,1280]{4,3,1,2,0:T(8,128)(2,1)}, u32[]{:S(2)}, u32[]{:S(2)}) %collective-permute-start.16) | collective-permute-done | bytes 1310752 | tf_op jit(solution)/shard_map/ppermute | solution.py:685
  295.7 25.2 %collective-permute-done.17 = bf16[2,2,1,80,2048]{4,3,1,0,2:T(8,128)(2,1)} collective-permute-done((bf16[2,2,1,80,2048]{4,3,1,0,2:T(8,128)(2,1)}, bf16[2,2,1,80,2048]{4,3,1,0,2:T(8,128)(2,1)}, u32[]{:S(2)}, u32[]{:S(2)}) %collective-permute-start.17) | collective-permute-done | bytes 1310752 | tf_op jit(solution)/shard_map/ppermute | solution.py:685
  334.5 16.3 %hidden_units.4 = (bf16[1024,640]{1,0:T(8,128)(2,1)}, bf16[1024,1280]{1,0:T(8,128)(2,1)}) custom-call(bf16[512,2048]{1,0:T(8,128)(2,1)} %copy-done.3, bf16[512,2048]{1,0:T(8,128)(2,1)} %copy-done.8, bf16[512,2048]{1,0:T(8,128)(2,1)} %bitcast.158, bf16[512,2048]{1,0:T(8,128)(2,1)} %copy-done.7, bf16[2048,1280]{1,0:T(8,128)(2,1)} %bitcast.141, ...), custom_call_target="tpu_custom_call" | custom-call | tf_op jit(solution)/shard_map/hidden_units/pallas_call | solution.py:393
  350.8 43.4 %collective-permute-done.21 = bf16[1,2,1,80,2048]{4,3,1,2,0:T(8,128)(2,1)} collective-permute-done((bf16[1,2,1,80,2048]{4,3,1,2,0:T(8,128)(2,1)}, bf16[1,2,1,80,2048]{4,3,1,2,0:T(8,128)(2,1)}, u32[]{:S(2)}, u32[]{:S(2)}) %collective-permute-start.21) | collective-permute-done | bytes 655392 | tf_op jit(solution)/shard_map/ppermute | solution.py:685
  403.8 16.5 %hidden_units.5 = (bf16[1024,640]{1,0:T(8,128)(2,1)}, bf16[1024,1280]{1,0:T(8,128)(2,1)}) custom-call(bf16[512,2048]{1,0:T(8,128)(2,1)} %collective-permute-done.19.refs_0_.refs_2_, bf16[512,2048]{1,0:T(8,128)(2,1)} %copy-done.10, bf16[512,2048]{1,0:T(8,128)(2,1)} %collective-permute-done.6.refs_2_.refs_4_, bf16[512,2048]{1,0:T(8,128)(2,1)} %copy-done.9, ...), custom_call_target="tpu_custom_call" | custom-call | tf_op jit(solution)/shard_map/hidden_units/pallas_call | solution.py:393
  430.2 17.5 %units_grad.2 = (bf16[1024,1280]{1,0:T(8,128)(2,1)}, bf16[1024,1280]{1,0:T(8,128)(2,1)}) custom-call(s32[1]{0:T(128)} %bitcast.56.bit_ref, bf16[512,2048]{1,0:T(8,128)(2,1)} %copy-done.3, bf16[512,2048]{1,0:T(8,128)(2,1)} %copy-done.8, bf16[512,2048]{1,0:T(8,128)(2,1)} %collective-permute-done.19.refs_0_.refs_2_, bf16[512,2048]{1,0:T(8,128)(2,1)} %copy-done.10, ...), custom_call_target="tpu_custom_call" | custom-call | tf_op jit(solution)/shard_map/units_grad/pallas_call | solution.py:438
  458.9 16.3 %hidden_units.6 = (bf16[1024,640]{1,0:T(8,128)(2,1)}, bf16[1024,1280]{1,0:T(8,128)(2,1)}) custom-call(bf16[512,2048]{1,0:T(8,128)(2,1)} %copy-done.3, bf16[512,2048]{1,0:T(8,128)(2,1)} %copy-done.8, bf16[512,2048]{1,0:T(8,128)(2,1)} %bitcast.160, bf16[512,2048]{1,0:T(8,128)(2,1)} %copy-done.7, bf16[2048,1280]{1,0:T(8,128)(2,1)} %bitcast.145, ...), custom_call_target="tpu_custom_call" | custom-call | tf_op jit(solution)/shard_map/hidden_units/pallas_call | solution.py:393
  475.2 16.3 %hidden_units.7 = (bf16[1024,640]{1,0:T(8,128)(2,1)}, bf16[1024,1280]{1,0:T(8,128)(2,1)}) custom-call(bf16[512,2048]{1,0:T(8,128)(2,1)} %collective-permute-done.19.refs_0_.refs_2_, bf16[512,2048]{1,0:T(8,128)(2,1)} %copy-done.10, bf16[512,2048]{1,0:T(8,128)(2,1)} %collective-permute-done.6.refs_2_.refs_4_, bf16[512,2048]{1,0:T(8,128)(2,1)} %copy-done.9, ...), custom_call_target="tpu_custom_call" | custom-call | tf_op jit(solution)/shard_map/hidden_units/pallas_call | solution.py:393
  512.4 16.1 %hidden_sum.2 = (f32[512,2048]{1,0:T(8,128)}, bf16[512,2048]{1,0:T(8,128)(2,1)}) custom-call(s32[1]{0:T(128)} %constant.255.clone.1.core_ref.bit_ref, bf16[1024,1280]{1,0:T(8,128)(2,1)} %get-tuple-element.647.refs_5_.refs_0_, bf16[1024,1280]{1,0:T(8,128)(2,1)} %get-tuple-element.648.refs_1_.refs_5_, bf16[2048,1280]{1,0:T(8,128)(2,1)} %bitcast.143, ...), custom_call_target="tpu_custom_call" | custom-call | tf_op jit(solution)/shard_map/hidden_sum/pallas_call | solution.py:496
  532.7 17.4 %units_grad.3 = (bf16[1024,1280]{1,0:T(8,128)(2,1)}, bf16[1024,1280]{1,0:T(8,128)(2,1)}) custom-call(s32[1]{0:T(128)} %bitcast.56.bit_ref, bf16[512,2048]{1,0:T(8,128)(2,1)} %copy-done.3, bf16[512,2048]{1,0:T(8,128)(2,1)} %copy-done.8, bf16[512,2048]{1,0:T(8,128)(2,1)} %collective-permute-done.19.refs_0_.refs_2_, bf16[512,2048]{1,0:T(8,128)(2,1)} %copy-done.10, ...), custom_call_target="tpu_custom_call" | custom-call | tf_op jit(solution)/shard_map/units_grad/pallas_call | solution.py:438
  585.5 16.1 %hidden_sum.3 = (f32[512,2048]{1,0:T(8,128)}, bf16[512,2048]{1,0:T(8,128)(2,1)}) custom-call(s32[1]{0:T(128)} %constant.255.clone.1.core_ref.bit_ref, bf16[1024,1280]{1,0:T(8,128)(2,1)} %get-tuple-element.699.refs_4_.refs_0_, bf16[1024,1280]{1,0:T(8,128)(2,1)} %get-tuple-element.700.refs_4_.refs_1_, bf16[2048,1280]{1,0:T(8,128)(2,1)} %bitcast.144, ...), custom_call_target="tpu_custom_call" | custom-call | tf_op jit(solution)/shard_map/hidden_sum/pallas_call | solution.py:496
  633.6 27.4 %collective-permute-done.34 = bf16[1,1,1,256,1280]{4,3,2,1,0:T(8,128)(2,1)S(1)} collective-permute-done((bf16[1,1,1,256,1280]{4,3,2,1,0:T(8,128)(2,1)S(1)}, bf16[1,1,1,256,1280]{4,3,2,1,0:T(8,128)(2,1)S(1)}, u32[]{:S(2)}, u32[]{:S(2)}) %collective-permute-start.34) | collective-permute-done | bytes 655392 | tf_op jit(solution)/shard_map/ppermute | solution.py:685
  672.8 16.5 %collective-permute-done.35 = bf16[1,2,2,256,1280]{4,3,2,1,0:T(8,128)(2,1)S(1)} collective-permute-done((bf16[1,2,2,256,1280]{4,3,2,1,0:T(8,128)(2,1)S(1)}, bf16[1,2,2,256,1280]{4,3,2,1,0:T(8,128)(2,1)S(1)}, u32[]{:S(2)}, u32[]{:S(2)}) %collective-permute-start.35) | collective-permute-done | bytes 2621472 | tf_op jit(solution)/shard_map/ppermute | solution.py:685
  691.4 16.7 %collective-permute-done.30 = bf16[512,2048]{1,0:T(8,128)(2,1)S(1)} collective-permute-done((bf16[512,2048]{1,0:T(8,128)(2,1)S(1)}, bf16[512,2048]{1,0:T(8,128)(2,1)S(1)}, u32[]{:S(2)}, u32[]{:S(2)}) %collective-permute-start.30) | collective-permute-done | bytes 2097184 | tf_op jit(solution)/shard_map/ppermute | solution.py:653
  721.5 30.1 %collective-permute-done.42 = bf16[1,1,1,80,2048]{4,3,2,1,0:T(8,128)(2,1)S(1)} collective-permute-done((bf16[1,1,1,80,2048]{4,3,2,1,0:T(8,128)(2,1)S(1)}, bf16[1,1,1,80,2048]{4,3,2,1,0:T(8,128)(2,1)S(1)}, u32[]{:S(2)}, u32[]{:S(2)}) %collective-permute-start.42) | collective-permute-done | bytes 327712 | tf_op jit(solution)/shard_map/ppermute | solution.py:685
  784.8 33.0 %attend_back.1 = (f32[2,512,768]{2,1,0:T(8,128)}, bf16[2,512,384]{2,1,0:T(8,128)(2,1)}, f32[2,512,384]{2,1,0:T(8,128)}) custom-call(s32[8]{0:T(128)} %reshape.483.lo_ref, bf16[2,512,768]{2,1,0:T(8,128)(2,1)} %bitcast.185, bf16[2,512,384]{2,1,0:T(8,128)(2,1)} %collective-permute-done.8.prior_ref, bf16[2,512,384]{2,1,0:T(8,128)(2,1)} %bitcast.194, ...), custom_call_target="tpu_custom_call" | custom-call | tf_op jit(solution)/shard_map/attend_back/pallas_call | solution.py:354
  822.5 35.6 %collective-permute-start.47 = (bf16[2,512,384]{2,1,0:T(8,128)(2,1)}, bf16[2,512,384]{2,1,0:T(8,128)(2,1)}, u32[]{:S(2)}, u32[]{:S(2)}) collective-permute-start(bf16[2,512,384]{2,1,0:T(8,128)(2,1)} %get-tuple-element.816), channel_id=1, source_target_pairs={{0,16},{16,0},{1,17},{17,1},{2,18},{18,2},{3,19},{19,3},{4,20},{20... | collective-permute-start | bytes 2359304 | tf_op jit(solution)/shard_map/ppermute | solution.py:649
  903.2 19.1 %collective-permute-done.51 = bf16[1,2,1,1,48,1024]{5,4,3,2,1,0:T(8,128)(2,1)S(1)} collective-permute-done((bf16[1,2,1,1,48,1024]{5,4,3,2,1,0:T(8,128)(2,1)S(1)}, bf16[1,2,1,1,48,1024]{5,4,3,2,1,0:T(8,128)(2,1)S(1)}, u32[]{:S(2)}, u32[]{:S(2)}) %collective-permute-start.51) | collective-permute-done | bytes 196640 | tf_op jit(solution)/shard_map/ppermute | solution.py:685
  950.4 15.9 %collective-permute-done.55 = bf16[1,1,1,1,48,1024]{5,4,3,2,1,0:T(8,128)(2,1)S(1)} collective-permute-done((bf16[1,1,1,1,48,1024]{5,4,3,2,1,0:T(8,128)(2,1)S(1)}, bf16[1,1,1,1,48,1024]{5,4,3,2,1,0:T(8,128)(2,1)S(1)}, u32[]{:S(2)}, u32[]{:S(2)}) %collective-permute-start.55) | collective-permute-done | bytes 98336 | tf_op jit(solution)/shard_map/ppermute | solution.py:685
  (460 shorter events, 464.7 us)
Async XLA Ops:
  7.2 119.5 %all-gather.3.cloned.1.call-start = ((), (), s32[]{:S(2)}) async-start(), calls=%async_computation | async-start | bytes 10272768 | tf_op jit(solution)/shard_map/all_gather | solution.py:890
  10.8 209.6 %all-gather.5.cloned.1.call-start = ((), (), s32[]{:S(2)}) async-start(), calls=%async_computation.1 | async-start | bytes 6488064 | tf_op jit(solution)/shard_map/all_gather | solution.py:915
  10.9 85.6 %collective-permute-start.1 = (bf16[512,2048]{1,0:T(8,128)(2,1)}, bf16[512,2048]{1,0:T(8,128)(2,1)S(1)}, u32[]{:S(2)}, u32[]{:S(2)}) collective-permute-start(bf16[512,2048]{1,0:T(8,128)(2,1)} %bitcast.157), channel_id=1, source_target_pairs={{0,1},{1,0},{2,3},{3,2},{4,5},{5,4},{6,7},{7,6},{8,9},{9,8},{10,11... | collective-permute-start | bytes 6291464 | tf_op jit(solution)/shard_map/ppermute | solution.py:635
  134.4 66.1 %collective-permute-start.6 = (bf16[512,2048]{1,0:T(8,128)(2,1)S(1)}, bf16[512,2048]{1,0:T(8,128)(2,1)}, u32[]{:S(2)}, u32[]{:S(2)}) collective-permute-start(bf16[512,2048]{1,0:T(8,128)(2,1)S(1)} %bitcast.162), channel_id=1, source_target_pairs={{0,2},{2,0},{1,3},{3,1},{4,6},{6,4},{5,7},{7,5},{8,10},{10,8},{9,1... | collective-permute-start | bytes 6291464 | tf_op jit(solution)/shard_map/ppermute | solution.py:653
  135.5 62.1 %collective-permute-start.9 = (bf16[1,2,1,256,1280]{4,3,1,2,0:T(8,128)(2,1)}, bf16[1,2,1,256,1280]{4,3,1,2,0:T(8,128)(2,1)}, u32[]{:S(2)}, u32[]{:S(2)}) collective-permute-start(bf16[1,2,1,256,1280]{4,3,1,2,0:T(8,128)(2,1)} %bitcast.28), channel_id=1, source_target_pairs={{0,4},{4,0},{8,12},{12,8},{1,5},{5,1},{9,13},{13,9},{2,6},{6,2},{1... | collective-permute-start | bytes 3932168 | tf_op jit(solution)/shard_map/ppermute | solution.py:685
  152.9 47.6 %collective-permute-start.8 = (bf16[2,512,384]{2,1,0:T(8,128)(2,1)}, bf16[2,512,384]{2,1,0:T(8,128)(2,1)}, u32[]{:S(2)}, u32[]{:S(2)}) collective-permute-start(bf16[2,512,384]{2,1,0:T(8,128)(2,1)} %bitcast.192), channel_id=1, source_target_pairs={{0,16},{16,0},{1,17},{17,1},{2,18},{18,2},{3,19},{19,3},{4,20},{20... | collective-permute-start | bytes 2359304 | tf_op jit(solution)/shard_map/ppermute | solution.py:649
  229.0 91.9 %collective-permute-start.14 = (bf16[512,2048]{1,0:T(8,128)(2,1)}, bf16[512,2048]{1,0:T(8,128)(2,1)S(1)}, u32[]{:S(2)}, u32[]{:S(2)}) collective-permute-start(bf16[512,2048]{1,0:T(8,128)(2,1)} %collective-permute-done.6.refs_2_.refs_4_), channel_id=1, source_target_pairs={{0,1},{1,0},{2,3},{3,2},{4,5},{5,4},{6,7},{7,6},{8,9},{9,8},{10,11... | collective-permute-start | bytes 6291464 | tf_op jit(solution)/shard_map/ppermute | solution.py:635
  229.0 91.9 %collective-permute-start.15 = (bf16[1,2,2,256,1280]{4,3,2,1,0:T(8,128)(2,1)}, bf16[1,2,2,256,1280]{4,3,2,1,0:T(8,128)(2,1)}, u32[]{:S(2)}, u32[]{:S(2)}) collective-permute-start(bf16[1,2,2,256,1280]{4,3,2,1,0:T(8,128)(2,1)} %bitcast.30), channel_id=1, source_target_pairs={{0,16},{16,0},{1,17},{17,1},{2,18},{18,2},{3,19},{19,3},{4,20},{20... | collective-permute-start | bytes 7864328 | tf_op jit(solution)/shard_map/ppermute | solution.py:685
  254.0 66.9 %collective-permute-start.13 = (bf16[512,2048]{1,0:T(8,128)(2,1)S(1)}, bf16[512,2048]{1,0:T(8,128)(2,1)S(1)}, u32[]{:S(2)}, u32[]{:S(2)}) collective-permute-start(bf16[512,2048]{1,0:T(8,128)(2,1)S(1)} %get-tuple-element.656.refs_0_), channel_id=1, source_target_pairs={{0,1},{1,0},{2,3},{3,2},{4,5},{5,4},{6,7},{7,6},{8,9},{9,8},{10,11... | collective-permute-start | bytes 6291464 | tf_op jit(solution)/shard_map/ppermute | solution.py:635
  271.8 49.1 %collective-permute-start.17 = (bf16[2,2,1,80,2048]{4,3,1,0,2:T(8,128)(2,1)}, bf16[2,2,1,80,2048]{4,3,1,0,2:T(8,128)(2,1)}, u32[]{:S(2)}, u32[]{:S(2)}) collective-permute-start(bf16[2,2,1,80,2048]{4,3,1,0,2:T(8,128)(2,1)} %bitcast.37), channel_id=1, source_target_pairs={{0,4},{4,0},{8,12},{12,8},{1,5},{5,1},{9,13},{13,9},{2,6},{6,2},{1... | collective-permute-start | bytes 3932168 | tf_op jit(solution)/shard_map/ppermute | solution.py:685
  320.9 75.7 %collective-permute-start.20 = (bf16[1,2,2,256,1280]{4,3,2,1,0:T(8,128)(2,1)}, bf16[1,2,2,256,1280]{4,3,2,1,0:T(8,128)(2,1)}, u32[]{:S(2)}, u32[]{:S(2)}) collective-permute-start(bf16[1,2,2,256,1280]{4,3,2,1,0:T(8,128)(2,1)} %bitcast.167), channel_id=1, source_target_pairs={{0,16},{16,0},{1,17},{17,1},{2,18},{18,2},{3,19},{19,3},{4,20},{20... | collective-permute-start | bytes 7864328 | tf_op jit(solution)/shard_map/ppermute | solution.py:685
  323.8 72.8 %collective-permute-start.19 = (bf16[512,2048]{1,0:T(8,128)(2,1)S(1)}, bf16[512,2048]{1,0:T(8,128)(2,1)}, u32[]{:S(2)}, u32[]{:S(2)}) collective-permute-start(bf16[512,2048]{1,0:T(8,128)(2,1)S(1)} %get-tuple-element.656.refs_0_), channel_id=1, source_target_pairs={{0,2},{2,0},{1,3},{3,1},{4,6},{6,4},{5,7},{7,5},{8,10},{10,8},{9,1... | collective-permute-start | bytes 6291464 | tf_op jit(solution)/shard_map/ppermute | solution.py:653
  326.1 68.1 %collective-permute-start.21 = (bf16[1,2,1,80,2048]{4,3,1,2,0:T(8,128)(2,1)}, bf16[1,2,1,80,2048]{4,3,1,2,0:T(8,128)(2,1)}, u32[]{:S(2)}, u32[]{:S(2)}) collective-permute-start(bf16[1,2,1,80,2048]{4,3,1,2,0:T(8,128)(2,1)} %bitcast.196), channel_id=1, source_target_pairs={{0,16},{16,0},{1,17},{17,1},{2,18},{18,2},{3,19},{19,3},{4,20},{20... | collective-permute-start | bytes 1966088 | tf_op jit(solution)/shard_map/ppermute | solution.py:685
  398.5 49.3 %collective-permute-start.23 = (bf16[2,2,1,80,2048]{4,3,1,0,2:T(8,128)(2,1)}, bf16[2,2,1,80,2048]{4,3,1,0,2:T(8,128)(2,1)}, u32[]{:S(2)}, u32[]{:S(2)}) collective-permute-start(bf16[2,2,1,80,2048]{4,3,1,0,2:T(8,128)(2,1)} %bitcast.188), channel_id=1, source_target_pairs={{0,4},{4,0},{8,12},{12,8},{1,5},{5,1},{9,13},{13,9},{2,6},{6,2},{1... | collective-permute-start | bytes 3932168 | tf_op jit(solution)/shard_map/ppermute | solution.py:685
  447.7 58.5 %collective-permute-start.24 = (bf16[1,2,2,256,1280]{4,3,2,1,0:T(8,128)(2,1)}, bf16[1,2,2,256,1280]{4,3,2,1,0:T(8,128)(2,1)}, u32[]{:S(2)}, u32[]{:S(2)}) collective-permute-start(bf16[1,2,2,256,1280]{4,3,2,1,0:T(8,128)(2,1)} %bitcast.218), channel_id=1, source_target_pairs={{0,16},{16,0},{1,17},{17,1},{2,18},{18,2},{3,19},{19,3},{4,20},{20... | collective-permute-start | bytes 7864328 | tf_op jit(solution)/shard_map/ppermute | solution.py:685
  450.5 51.6 %collective-permute-start.25 = (bf16[2,2,1,80,2048]{4,3,2,1,0:T(8,128)(2,1)S(1)}, bf16[2,2,1,80,2048]{4,3,2,1,0:T(8,128)(2,1)}, u32[]{:S(2)}, u32[]{:S(2)}) collective-permute-start(bf16[2,2,1,80,2048]{4,3,2,1,0:T(8,128)(2,1)S(1)} %constant_dynamic-slice_fusion.24), channel_id=1, source_target_pairs={{0,4},{4,0},{8,12},{12,8},{1,5},{5,1},{9,13},{13,9},{2,6},{6,2},{1... | collective-permute-start | bytes 3932168 | tf_op jit(solution)/shard_map/ppermute | solution.py:685
  583.4 82.5 %collective-permute-start.31 = (bf16[512,2048]{1,0:T(8,128)(2,1)}, bf16[512,2048]{1,0:T(8,128)(2,1)}, u32[]{:S(2)}, u32[]{:S(2)}) collective-permute-start(bf16[512,2048]{1,0:T(8,128)(2,1)} %get-tuple-element.697), channel_id=1, source_target_pairs={{0,1},{1,0},{2,3},{3,2},{4,5},{5,4},{6,7},{7,6},{8,9},{9,8},{10,11... | collective-permute-start | bytes 6291464 | tf_op jit(solution)/shard_map/ppermute | solution.py:635
  601.6 61.8 %collective-permute-start.32 = (bf16[512,2048]{1,0:T(8,128)(2,1)}, bf16[512,2048]{1,0:T(8,128)(2,1)}, u32[]{:S(2)}, u32[]{:S(2)}) collective-permute-start(bf16[512,2048]{1,0:T(8,128)(2,1)} %get-tuple-element.712), channel_id=1, source_target_pairs={{0,1},{1,0},{2,3},{3,2},{4,5},{5,4},{6,7},{7,6},{8,9},{9,8},{10,11... | collective-permute-start | bytes 6291464 | tf_op jit(solution)/shard_map/ppermute | solution.py:635
  612.2 57.9 %collective-permute-start.33 = (bf16[512,2048]{1,0:T(8,128)(2,1)}, bf16[512,2048]{1,0:T(8,128)(2,1)S(1)}, u32[]{:S(2)}, u32[]{:S(2)}) collective-permute-start(bf16[512,2048]{1,0:T(8,128)(2,1)} %get-tuple-element.714), channel_id=1, source_target_pairs={{0,1},{1,0},{2,3},{3,2},{4,5},{5,4},{6,7},{7,6},{8,9},{9,8},{10,11... | collective-permute-start | bytes 6291464 | tf_op jit(solution)/shard_map/ppermute | solution.py:635
  631.2 58.1 %collective-permute-start.35 = (bf16[1,2,2,256,1280]{4,3,2,1,0:T(8,128)(2,1)S(1)}, bf16[1,2,2,256,1280]{4,3,2,1,0:T(8,128)(2,1)S(1)}, u32[]{:S(2)}, u32[]{:S(2)}) collective-permute-start(bf16[1,2,2,256,1280]{4,3,2,1,0:T(8,128)(2,1)S(1)} %bitcast.217), channel_id=1, source_target_pairs={{0,16},{16,0},{1,17},{17,1},{2,18},{18,2},{3,19},{19,3},{4,20},{20... | collective-permute-start | bytes 7864328 | tf_op jit(solution)/shard_map/ppermute | solution.py:685
  716.9 60.8 %collective-permute-start.38 = (bf16[512,2048]{1,0:T(8,128)(2,1)}, bf16[512,2048]{1,0:T(8,128)(2,1)}, u32[]{:S(2)}, u32[]{:S(2)}) collective-permute-start(bf16[512,2048]{1,0:T(8,128)(2,1)} %add_convert_fusion.3), channel_id=1, source_target_pairs={{0,2},{2,0},{1,3},{3,1},{4,6},{6,4},{5,7},{7,5},{8,10},{10,8},{9,1... | collective-permute-start | bytes 6291464 | tf_op jit(solution)/shard_map/ppermute | solution.py:653
  721.5 56.2 %collective-permute-start.40 = (f32[128,1280]{1,0:T(8,128)}, f32[128,1280]{1,0:T(8,128)}, u32[]{:S(2)}, u32[]{:S(2)}) collective-permute-start(f32[128,1280]{1,0:T(8,128)} %get-tuple-element.944), channel_id=1, source_target_pairs={{0,2},{2,0},{1,3},{3,1},{4,6},{6,4},{5,7},{7,5},{8,10},{10,8},{9,1... | collective-permute-start | bytes 1966088 | tf_op jit(solution)/shard_map/ppermute | solution.py:653
  822.5 63.2 %collective-permute-start.46 = (f32[128,1280]{1,0:T(8,128)}, f32[128,1280]{1,0:T(8,128)}, u32[]{:S(2)}, u32[]{:S(2)}) collective-permute-start(f32[128,1280]{1,0:T(8,128)} %get-tuple-element.942), channel_id=1, source_target_pairs={{0,2},{2,0},{1,3},{3,1},{4,6},{6,4},{5,7},{7,5},{8,10},{10,8},{9,1... | collective-permute-start | bytes 1966088 | tf_op jit(solution)/shard_map/ppermute | solution.py:653
  822.5 63.2 %collective-permute-start.47 = (bf16[2,512,384]{2,1,0:T(8,128)(2,1)}, bf16[2,512,384]{2,1,0:T(8,128)(2,1)}, u32[]{:S(2)}, u32[]{:S(2)}) collective-permute-start(bf16[2,512,384]{2,1,0:T(8,128)(2,1)} %get-tuple-element.816), channel_id=1, source_target_pairs={{0,16},{16,0},{1,17},{17,1},{2,18},{18,2},{3,19},{19,3},{4,20},{20... | collective-permute-start | bytes 2359304 | tf_op jit(solution)/shard_map/ppermute | solution.py:649
  (118 other events, 1958.3 us)
Sparse Core Ops, SparseCore 0:
  10.9 115.7 all-gather.2
  129.6 85.5 all-gather.4

commit v2 on v1

--- a/solution.py
+++ b/solution.py
@@ -197,30 +197,42 @@
     return jnp.where(even, values[base : base + TILE], values[base + TILE : base + 2 * TILE])
 
 
-def widen(refs, k_ref, v_ref, heads):
+def transposed_pair(values, p, even):
+    at = 2 * p * TILE
+    low, high = values[:, at : at + TILE].T, values[:, at + TILE : at + 2 * TILE].T
+    return jnp.where(even, low, high)
+
+
+def widen(refs, heads, place):
     at = 0
+    even = lane_of((TILE, TILE)) < HEAD_SIZE
     for ref in refs:
         for r in range(0, ref.shape[1], TILE):
-            rows = slice(at, at + TILE)
-            lane = lane_of((TILE, TILE))
-            even = lane < HEAD_SIZE
             for t in range(heads):
                 x = ref[0, r : r + TILE, t * TILE : (t + 1) * TILE].astype(F32)
                 other = pltpu.roll(x, HEAD_SIZE, 1)
                 for part, value in enumerate((jnp.where(even, x, other), jnp.where(even, other, x))):
                     n = 2 * t + part
-                    out = k_ref if n < heads else v_ref
-                    out[rows, (n % heads) * TILE : (n % heads + 1) * TILE] = value.astype(BF)
+                    col = slice((n % heads) * TILE, (n % heads + 1) * TILE)
+                    place(n < heads, slice(at, at + TILE), col, value)
             at += TILE
 
 
 def narrow(k_ref, v_ref, rows, t, heads, even):
     tiles = []
     for n in (2 * t, 2 * t + 1):
-        ref, scale = (k_ref, SCALE) if n < heads else (v_ref, 1.0)
+        ref = k_ref if n < heads else v_ref
         x = ref[rows, (n % heads) * TILE : (n % heads + 1) * TILE]
-        tiles.append((x + pltpu.roll(x, HEAD_SIZE, 1)) * scale)
+        tiles.append(x + pltpu.roll(x, HEAD_SIZE, 1))
     return jnp.where(even, tiles[0], tiles[1])
+
+
+def key_bias(qseg_ref, kseg_ref, j, i, blocks):
+    at = pl.ds(pl.multiple_of(j * TILE, TILE), TILE)
+    key_at = lax.broadcasted_iota(jnp.int32, (TILE, TILE), 0) + j * TILE
+    query_at = lane_of((TILE, TILE)) + (i + blocks) * TILE
+    ok = (kseg_ref[0, at, :] == qseg_ref[0, pl.ds(i, 1), :]) & (key_at <= query_at)
+    return at, jnp.concatenate([jnp.where(ok, 0.0, -1e30)] * 4, axis=1)
 
 
 def attend(low_block, q, kv_prior, kv, qseg, kseg):
@@ -228,6 +240,7 @@
     blocks = rows // TILE
     heads = kv.shape[2] // TILE
     keys = 2 * rows
+    lse_rows = -(-4 * heads // 8) * 8
 
     def kernel(lo_ref, q_ref, prior_ref, kv_ref, qseg_ref, kseg_ref, o_ref, lse_ref, acc_ref, sum_ref, k_ref, v_ref):
         b, i = pl.program_id(0), pl.program_id(1)
@@ -236,9 +249,12 @@
 
         @pl.when(i == 0)
         def _():
-            widen((prior_ref, kv_ref), k_ref, v_ref, heads)
-
-        qs = [stacked(q_ref, g, even) for g in range(heads)]
+            def place(is_key, at, col, value):
+                (k_ref if is_key else v_ref)[at, col] = value.astype(BF)
+
+            widen((prior_ref, kv_ref), heads, place)
+
+        qs = [stacked(q_ref, g, even) * jnp.asarray(SCALE, BF) for g in range(heads)]
         acc_ref[...] = jnp.zeros_like(acc_ref)
         sum_ref[...] = jnp.zeros_like(sum_ref)
         seg = qseg_ref[0]
@@ -251,7 +267,7 @@
             bias = jnp.concatenate([bias] * 4, axis=0)
             for g in range(heads):
                 col = slice(g * TILE, (g + 1) * TILE)
-                e = jnp.exp(dot_nt(qs[g], k_ref[at, col]) * SCALE + bias)
+                e = jnp.exp(dot_nt(qs[g], k_ref[at, col]) + bias)
                 sum_ref[g] += e
                 acc_ref[g] += dot(e.astype(BF), v_ref[at, col])
             return carry
@@ -266,7 +282,7 @@
                 o_ref[0, :, (2 * g + p) * TILE : (2 * g + p + 1) * TILE] = unstacked(out, p, even).astype(BF)
             for h in range(4):
                 lse = jnp.where(lane == 4 * g + h, log[h * TILE : (h + 1) * TILE], lse)
-        lse_ref[0] = lse
+        lse_ref[0, 0] = lse.T[:lse_rows]
 
     per_q = lambda n: pl.BlockSpec((1, TILE, n), lambda b, i, lo: (b, i, 0))
     per_b = lambda s: pl.BlockSpec((1,) + s[1:], lambda b, i, lo: (b, 0, 0))
@@ -274,8 +290,8 @@
         kernel,
         (batch, blocks),
         [per_q(cols), per_b(kv.shape), per_b(kv.shape), per_q(1), per_b(kseg.shape)],
-        [per_q(cols), per_q(TILE)],
-        [shaped(q.shape, BF), shaped((batch, rows, TILE), F32)],
+        [per_q(cols), pl.BlockSpec((1, 1, lse_rows, TILE), lambda b, i, lo: (b, i, 0, 0))],
+        [shaped(q.shape, BF), shaped((batch, blocks, lse_rows, TILE), F32)],
         "attend",
         [pltpu.VMEM((heads, 4 * TILE, TILE), F32)] * 2 + [pltpu.VMEM((keys, heads * TILE), BF)] * 2,
         [low_block],
@@ -288,52 +304,57 @@
     heads = kv.shape[2] // TILE
     keys = 2 * rows
 
-    def kernel(lo_ref, q_ref, prior_ref, kv_ref, qseg_ref, kseg_ref, o_ref, lse_ref, do_ref, dq_ref, dprior_ref, dkv_ref, acc_ref, k_ref, v_ref, dk_ref, dv_ref):
+    def kernel(lo_ref, q_ref, prior_ref, kv_ref, qseg_ref, kseg_ref, o_ref, lse_ref, do_ref, dq_ref, dprior_ref, dkv_ref, acc_ref, k_ref, kt_ref, v_ref, dk_ref, dv_ref):
         b, i = pl.program_id(0), pl.program_id(1)
-        lane = lane_of((TILE, TILE))
-        even = lane < HEAD_SIZE
+        even = lane_of((TILE, TILE)) < HEAD_SIZE
 
         @pl.when(i == 0)
         def _():
-            widen((prior_ref, kv_ref), k_ref, v_ref, heads)
+            def place(is_key, at, col, value):
+                if is_key:
+                    k_ref[at, col] = value.astype(BF)
+                    kt_ref[col, at] = value.T.astype(BF)
+                else:
+                    v_ref[at, col] = value.astype(BF)
+
+            widen((prior_ref, kv_ref), heads, place)
             dk_ref[...] = jnp.zeros_like(dk_ref)
             dv_ref[...] = jnp.zeros_like(dv_ref)
 
-        qs = [stacked(q_ref, g, even) for g in range(heads)]
+        qs = [stacked(q_ref, g, even) * jnp.asarray(SCALE, BF) for g in range(heads)]
         dos = [stacked(do_ref, g, even) for g in range(heads)]
         lses, deltas = [], []
         for g in range(heads):
-            os = stacked(o_ref, g, even)
-            deltas.append(jnp.sum(os.astype(F32) * dos[g].astype(F32), axis=-1, keepdims=True))
-            each = [
-                jnp.sum(jnp.where(lane == 4 * g + h, lse_ref[0], 0.0), axis=-1, keepdims=True)
-                for h in range(4)
-            ]
-            lses.append(jnp.concatenate(each, axis=0))
+            each = []
+            for p in range(2):
+                at = slice((2 * g + p) * TILE, (2 * g + p + 1) * TILE)
+                both = (o_ref[0, :, at].astype(F32) * do_ref[0, :, at].astype(F32)).T
+                each += [
+                    jnp.sum(both[n : n + HEAD_SIZE], axis=0, keepdims=True)
+                    for n in (0, HEAD_SIZE)
+                ]
+            deltas.append(jnp.concatenate(each, axis=1))
+            lses.append(
+                jnp.concatenate([lse_ref[0, 0, 4 * g + h : 4 * g + h + 1, :] for h in range(4)], axis=1)
+            )
         acc_ref[...] = jnp.zeros_like(acc_ref)
-        seg = qseg_ref[0]
-        row_at = lax.broadcasted_iota(jnp.int32, (TILE, TILE), 0) + (i + blocks) * TILE
 
         def step(j, carry):
-            at = pl.ds(pl.multiple_of(j * TILE, TILE), TILE)
-            ok = (seg == kseg_ref[0, pl.ds(j, 1), :]) & (lane + j * TILE <= row_at)
-            bias = jnp.where(ok, 0.0, -1e30)
-            bias = jnp.concatenate([bias] * 4, axis=0)
+            at, bias = key_bias(qseg_ref, kseg_ref, j, i, blocks)
             for g in range(heads):
                 col = slice(g * TILE, (g + 1) * TILE)
-                k, v = k_ref[at, col], v_ref[at, col]
-                p = jnp.exp(dot_nt(qs[g], k) * SCALE + (bias - lses[g]))
-                ds = (p * (dot_nt(dos[g], v) - deltas[g])).astype(BF)
-                dv_ref[at, col] += dot_tn(p.astype(BF), dos[g])
-                dk_ref[at, col] += dot_tn(ds, qs[g])
-                acc_ref[g] += dot(ds, k)
+                p = jnp.exp(dot_nt(k_ref[at, col], qs[g]) + (bias - lses[g]))
+                ds = (p * (dot_nt(v_ref[at, col], dos[g]) - deltas[g])).astype(BF)
+                dv_ref[at, col] += dot(p.astype(BF), dos[g])
+                dk_ref[at, col] += dot(ds, qs[g])
+                acc_ref[g] += dot(kt_ref[col, at], ds)
             return carry
 
         lax.fori_loop(lo_ref[b * blocks + i], i + blocks + 1, step, 0)
         for g in range(heads):
             for p in range(2):
                 dq_ref[0, :, (2 * g + p) * TILE : (2 * g + p + 1) * TILE] = (
-                    unstacked(acc_ref[g], p, even) * SCALE
+                    transposed_pair(acc_ref[g], p, even) * SCALE
                 )
 
         @pl.when(i == blocks - 1)
@@ -354,13 +375,20 @@
     return call(
         kernel,
         (batch, blocks),
-        [per_q(cols), per_b(kv.shape), per_b(kv.shape), per_q(1), per_b(kseg.shape)]
-        + [per_q(cols), per_q(TILE), per_q(cols)],
+        [per_q(cols), per_b(kv.shape), per_b(kv.shape), per_b(qseg.shape), per_b(kseg.shape)]
+        + [per_q(cols), pl.BlockSpec((1, 1) + lse.shape[2:], lambda b, i, lo: (b, i, 0, 0))]
+        + [per_q(cols)],
         [per_q(cols), per_b(kv.shape), per_b(kv.shape)],
         [shaped(q.shape, F32), shaped(kv.shape, BF), shaped(kv.shape, F32)],
         "attend_back",
-        [pltpu.VMEM((heads, 4 * TILE, TILE), F32)]
-        + [pltpu.VMEM(wide, BF)] * 2 + [pltpu.VMEM(wide, F32)] * 2,
+        [
+            pltpu.VMEM((heads, TILE, 4 * TILE), F32),
+            pltpu.VMEM(wide, BF),
+            pltpu.VMEM(wide[::-1], BF),
+            pltpu.VMEM(wide, BF),
+            pltpu.VMEM(wide, F32),
+            pltpu.VMEM(wide, F32),
+        ],
         [low_block],
     )(q, kv_prior, kv, qseg, kseg, o, lse, do)
 
@@ -616,18 +644,18 @@
 CHUNKS = 2
 UNITS, DOWN, OUT, QKV = range(4)
 PLAN = {
-    (UNITS, 0): (0, 1, 2),
-    (DOWN, 0): (0, 1, 2),
-    (UNITS, 1): (1, 2, 3),
-    (DOWN, 1): (2, 3, 4),
-    (DOWN, 0, True): (5, 6, 7),
-    (UNITS, 0, True): (5, 6, 7),
-    (DOWN, 1, True): (6, 7, 8),
-    (UNITS, 1, True): (7, 8, 9),
-    (OUT, 0, True): (9, 10, 11, 12),
-    (OUT, 1, True): (9, 10, 11, 12),
-    (QKV, 0, True): (11, 12, 13, 14),
-    (QKV, 1, True): (12, 13, 14, 15),
+    (UNITS, 0): (0, 2, 3),
+    (DOWN, 0): (0, 2, 3),
+    (UNITS, 1): (3, 5, 6),
+    (DOWN, 1): (3, 5, 6),
+    (DOWN, 0, True): (7, 10, 12),
+    (UNITS, 0, True): (7, 8, 10),
+    (DOWN, 1, True): (8, 10, 12),
+    (UNITS, 1, True): (8, 10, 13),
+    (OUT, 0, True): (13, 14, 15, 16),
+    (OUT, 1, True): (14, 15, 16, 17),
+    (QKV, 0, True): (15, 16, 17, 18),
+    (QKV, 1, True): (16, 17, 18, 19),
 }
 
 
@@ -712,7 +740,7 @@
 
 class Values:
     def __init__(self):
-        for name in ("low", "hidden", "wgu", "wd", "act", "ggu", "keep", "home"):
+        for name in ("low", "hidden", "wgu", "wd", "act", "ggu", "keep", "home", "hidden_sum", "down_sum"):
             setattr(self, name, {})
 
 
@@ -887,9 +915,11 @@
     weights = (w_query, key_projection_weight, value_projection_weight)
     lows, highs = zip(*(halves(w) for w in weights))
     gains = jnp.pad(jnp.stack([attn_gain, ffn_gain], axis=1), ((0, 0), (0, TILE - 2)))
-    qkv_all = lax.all_gather(
-        jnp.concatenate(lows + highs + (gains,), axis=1), AXES, axis=0, tiled=True
+    block = jnp.concatenate(lows + highs + (gains,), axis=1)
+    block = jnp.concatenate(
+        [block, jnp.pad(w_out, ((0, 0), (0, block.shape[1] - width)))], axis=0
     )
+    gathered = lax.all_gather(block, AXES, axis=0)
 
     quarters = split_units(w_gate, w_up, groups, ff_rows, pieces, padded)
     mine = [core_pick(quarters[2 * x], quarters[2 * x + 1]) for x in range(2)]
@@ -905,14 +935,11 @@
         down_block = jnp.pad(w_down[a:b], ((0, padded - b + a), (0, 0)))
         flow.gather((UNITS, j), units_block)
         flow.gather((DOWN, j), down_block)
-    live.w_out = w_out
-    pending = {}
-
-    def gather_qkv():
-        flow.live.qkv = qkv_all
-
-    def gather_out():
-        pending[OUT] = lax.all_gather(flow.live.w_out, AXES, axis=0, tiled=True)
+
+    def take_gathered():
+        live = flow.live
+        live.qkv = gathered[:, :in_rows].reshape(width, -1)
+        live.out = gathered[:, in_rows:, :width].reshape(-1, width)
 
     def tables():
         live = flow.live
@@ -927,8 +954,8 @@
         key_ids = jnp.concatenate([prior_ids, own_ids], axis=1)
         low_block = jnp.sum(key_ids[:, None, :] < own_ids[:, ::TILE, None], axis=-1) // TILE
         live.low_block = low_block.astype(jnp.int32)
-        live.query_ids = own_ids[:, :, None]
-        live.key_ids = key_ids.reshape(2, -1, TILE)
+        live.query_rows, live.query_columns = own_ids.reshape(2, -1, TILE), own_ids[:, :, None]
+        live.key_rows, live.key_columns = key_ids.reshape(2, -1, TILE), key_ids[:, :, None]
         live.cos, live.sin = rotary_tables(own_positions.reshape(2 * half))
         live.q_gain = jnp.tile(query_norm_gain.astype(F32), 2).reshape(1, TILE)
         live.k_gain = jnp.tile(key_gain.astype(F32), 2).reshape(1, TILE)
@@ -944,39 +971,42 @@
     def near_low():
         flow.live.low[1] = pair(flow.live.far_low)
 
-    def heads():
+    def first_hidden():
         live = flow.live
         n = q_cols + 2 * kv_cols
         live.gains = live.qkv[:, 2 * n : 2 * n + 2].T.astype(F32)
         live.hidden_first = pair((live.normed * live.gains[0]).astype(BF))
+
+    def heads():
+        live = flow.live
         q_rot, kv, live.raw = project(
             live.hidden_first, live.qkv, core, live.q_gain, live.k_gain, live.cos,
             live.sin, q_cols, kv_cols,
         )
         live.q, live.kv = q_rot.reshape(2, half, -1), kv.reshape(2, half, -1)
-        flow.post(swap_seq(live.kv), "prior_kv")
+
+    def prior_keys():
+        flow.post(swap_seq(flow.live.kv), "prior_kv")
 
     def attention():
         live = flow.live
         attn, live.lse = attend(
-            live.low_block, live.q, live.prior_kv, live.kv, live.query_ids,
-            live.key_ids,
+            live.low_block, live.q, live.prior_kv, live.kv, live.query_columns, live.key_rows
         )
         live.attn = attn.reshape(2 * half, q_cols)
 
     def near_rows(sums):
         return sums[0] + swap_core(sums[1]).astype(F32)
 
+    def branch_sum():
+        live = flow.live
+        live.branch = sum_products([live.attn], [live.out], False, "branch", core, q_cols)
+
     def branch():
         live = flow.live
-        live.out = pending.pop(OUT)
-        term = near_rows(
-            sum_products([live.attn], [live.out], False, "branch", core, q_cols)
-        )
-        live.middle = tokens.reshape(half, width).astype(F32) + term
+        live.middle = tokens.reshape(half, width).astype(F32) + near_rows(live.branch)
         live.normed2, live.scale2 = row_norm(live.middle)
-        hidden = (live.normed2 * live.gains[1]).astype(BF)
-        live.hidden[0] = pair(hidden)
+        live.hidden[0] = pair((live.normed2 * live.gains[1]).astype(BF))
 
     def far_hidden():
         flow.post(swap_x(flow.live.hidden[0][0]), "far_hidden")
@@ -1007,15 +1037,14 @@
     def hidden_sum(h):
         live = flow.live
         js = range(CHUNKS)
-        total = near_rows(
-            sum_products(
-                [live.ggu[j, h] for j in js], [live.wgu[j] for j in js], True, "hidden_sum"
-            )
+        live.hidden_sum[h] = sum_products(
+            [live.ggu[j, h] for j in js], [live.wgu[j] for j in js], True, "hidden_sum"
         )
-        if h:
-            live.far_grad_sum = total.astype(BF)
-        else:
-            live.near_grad = total
+
+    def near_hidden_sums():
+        live = flow.live
+        live.far_grad_sum = near_rows(live.hidden_sum.pop(1)).astype(BF)
+        live.near_grad = near_rows(live.hidden_sum.pop(0))
 
     def far_grad():
         flow.post(swap_x(flow.live.far_grad_sum), "far_grad")
@@ -1023,15 +1052,14 @@
     def down_sum(h):
         live = flow.live
         js = range(CHUNKS)
-        total = near_rows(
-            sum_products(
-                [live.act[j, h] for j in js], [live.wd[j] for j in js], False, "down_sum"
-            )
+        live.down_sum[h] = sum_products(
+            [live.act[j, h] for j in js], [live.wd[j] for j in js], False, "down_sum"
         )
-        if h:
-            live.far_result_sum = total.astype(BF)
-        else:
-            live.near_result = total
+
+    def near_down_sums():
+        live = flow.live
+        live.far_result_sum = near_rows(live.down_sum.pop(1)).astype(BF)
+        live.near_result = near_rows(live.down_sum.pop(0))
 
     def far_result():
         flow.post(swap_x(flow.live.far_result_sum), "far_result")
@@ -1058,8 +1086,8 @@
     def attention_back():
         live = flow.live
         dq, live.sent_dkv, live.dkv = attend_back(
-            live.low_block, live.q, live.prior_kv, live.kv, live.query_ids,
-            live.key_ids, live.attn.reshape(2, half, q_cols), live.lse,
+            live.low_block, live.q, live.prior_kv, live.kv, live.query_rows,
+            live.key_columns, live.attn.reshape(2, half, q_cols), live.lse,
             live.grad_attn.reshape(2, half, q_cols),
         )
         live.dq = dq.reshape(2 * half, q_cols)
@@ -1087,11 +1115,14 @@
         parts = jnp.stack([live.q_part, k_part]).sum(axis=1)
         live.head_gains = parts.reshape(2, 2, HEAD_SIZE).sum(axis=1)
 
+    def first_sums():
+        live = flow.live
+        live.first = first_sum(live.grad_q, live.grad_kv, live.qkv, core)
+
     def first_back():
         live = flow.live
-        grad = near_rows(first_sum(live.grad_q, live.grad_kv, live.qkv, core))
         live.input_grad = live.grad_middle + norm_back(
-            grad, live.normed, live.scale, live.gains[0]
+            near_rows(live.first), live.normed, live.scale, live.gains[0]
         )
 
     def finish_output():
@@ -1138,21 +1169,25 @@
 
     gain_order = [("core", 1), ("x", 1)] + group_axes()
     schedule = (
-        (tables, first_norm, gather_qkv),
-        (gather_out, far_low, heads),
-        (attention, branch, near_low),
+        (tables, first_norm, take_gathered),
+        (first_hidden,),
+        (heads, prior_keys),
+        (far_low, attention, branch_sum),
+        (branch, near_low),
         (far_hidden, do(units, 0, 0)),
         (near_hidden, do(units, 0, 1), do(down_grad, 0), do(units_grad, 0)),
-        (do(units, 1, 0), do(units, 1, 1), do(down_grad, 1)),
-        (do(units_grad, 1), do(hidden_sum, 1)),
-        (far_grad, do(hidden_sum, 0), do(down_sum, 1), do(down_sum, 0)),
-        (far_result, do(home, 0), second_back, out_grad),
-        (attention_back,),
-        (prior_back, do(home, 1), queries_back, finish_output),
+        (do(units, 1, 0), do(units, 1, 1), do(down_grad, 1), do(units_grad, 1)),
+        (do(hidden_sum, 1), do(hidden_sum, 0)),
+        (near_hidden_sums,),
+        (far_grad, do(down_sum, 1), do(down_sum, 0)),
+        (second_back, near_down_sums),
+        (do(home, 0), out_grad),
+        (far_result, attention_back),
+        (prior_back, do(home, 1), queries_back),
         (keys_back,),
-        (first_back,),
-        (finish_units, do(gain_hops, gain_order[:2])),
-        (finish_out, do(gain_hops, gain_order[2:4]),),
+        (first_sums,),
+        (first_back, finish_output, do(gain_hops, gain_order[:2])),
+        (finish_units, finish_out, do(gain_hops, gain_order[2:4])),
         (do(gain_hops, gain_order[4:]),),
     )
     for work in schedule:

time: 1050 us -> 925 us (0.88)
  waiting for transfers between devices: 419 us -> 279 us
  other arithmetic: 82.7 us -> 110 us
  starting transfers between devices: 130 us -> 104 us
  local copies, waits for them, and re-layouts: 48.1 us -> 70.5 us
    ppermute x45, waiting for transfers between devices: 350 us -> 170 us  [exchange(): lax.ppermute(value, axis, [(i, i ^ step) for i in range(lax.axis_size(axi...]
    all_gather x2 -> x1, waiting for transfers between devices: 30.1 us -> 54.3 us  [body(): gathered = lax.all_gather(block, AXES, axis=0)]
    convert_element_type x20, other arithmetic: 19.5 us -> 35 us  [land(): self.rest[name] = total if last else total.astype(BF)]
    ppermute x2, starting transfers between devices: 36 us -> 20.9 us  [swap_seq(): return lax.ppermute(value, 'seq', [(0, 1), (1, 0)])]
    slice x2 -> x4, local copies, waits for them, and re-layouts: 0.97 us -> 15.8 us  [the longest x1 8.26 us: take_gathered(): live.qkv = gathered[:, :in_rows].reshape(width, -1)]
    ppermute x18, waiting for transfers between devices: 4.27 us -> 18 us  [swap_core(): return lax.ppermute(value, 'core', [(0, 1), (1, 0)])]
  transfers between devices with their start and end apart: 75 -> 74, of which waited for: 29 -> 28; matrix products, arithmetic and copies ran while one was open for 8% -> 15% of each run, Pallas kernels for 30% -> 37%
where the time goes in v2:
time: 925 us; the launch traced here: 918 us
  Pallas kernels  338 us (37%)
  waiting for transfers between devices  279 us (30%)
  other arithmetic  110 us (12%)
  starting transfers between devices  104 us (11%)
  local copies, waits for them, and re-layouts  70.5 us (8%)
  between operations  15.7 us (2%)
    ppermute x45, waiting for transfers between devices, exchange(): lax.ppermute(value, axis, [(i, i ^ step) for i in range(lax.axis_size(axi...  170 us
    pallas_call x4, Pallas kernels, hidden_units(): call(kernel, (rows // tile,), groups + groups + [once(gate_up.shape), onc...  65.3 us
    pallas_call x5, Pallas kernels, sum_products(): call(kernel, (width // tile,), [once(a.shape) for a in lefts] + right, [c...  60.7 us
    all_gather x1, waiting for transfers between devices, body(): gathered = lax.all_gather(block, AXES, axis=0)  54.3 us
    ppermute x45, starting transfers between devices, exchange(): lax.ppermute(value, axis, [(i, i ^ step) for i in range(lax.axis_size(axi...  54.2 us
    pallas_call x4, Pallas kernels, tall_grad(): call(kernel, (steps,), [pl.BlockSpec((half, tile), column)] * count + [on...  48.8 us
    ppermute x7, waiting for transfers between devices, swap_x(): return lax.ppermute(value, 'x', [(0, 1), (1, 0)])  36.1 us
    pallas_call x12, Pallas kernels, placed(): call(place_kernel, (lead, inner // part), [side, side], pl.BlockSpec((1,...  36 us
  transfers between devices with their start and end apart: 74, of which 28 were waited for; matrix products, arithmetic and copies ran while one was open for 15% of the time, Pallas kernels for 37%

profile of v2, /device:TPU:1, one launch (start us, length us, event | category | flops | bytes accessed | tf_op | source)
XLA Modules:
  0.0 917.9 jit_solution(3726956474743055096)
XLA Ops:
  35.9 13.5 %collective-permute-done.3 = bf16[128,2560]{1,0:T(8,128)(2,1)S(1)} collective-permute-done((bf16[128,2560]{1,0:T(8,128)(2,1)}, bf16[128,2560]{1,0:T(8,128)(2,1)S(1)}, u32[]{:S(2)}, u32[]{:S(2)}) %collective-permute-start.3) | collective-permute-done | bytes 655392 | tf_op jit(solution)/shard_map/ppermute | solution.py:681
  53.8 50.2 %collective-permute-done.4 = bf16[1,1,1,256,1280]{4,3,2,1,0:T(8,128)(2,1)S(1)} collective-permute-done((bf16[1,1,1,256,1280]{4,3,2,1,0:T(8,128)(2,1)S(1)}, bf16[1,1,1,256,1280]{4,3,2,1,0:T(8,128)(2,1)S(1)}, u32[]{:S(2)}, u32[]{:S(2)}) %collective-permute-start.4) | collective-permute-done | bytes 655392 | tf_op jit(solution)/shard_map/ppermute | solution.py:713
  107.2 54.3 %all-gather.3.cloned.1.call-done = bf16[3584,2432]{1,0:T(8,128)(2,1)} async-done(((bf16[112,2432]{1,0:T(8,128)(2,1)}), bf16[3584,2432]{1,0:T(8,128)(2,1)}) %all-gather.3.cloned.1.call-update) | async-done | bytes 17432592 | tf_op jit(solution)/shard_map/all_gather | solution.py:922
  193.3 12.1 %project_heads.1 = (bf16[1024,768]{1,0:T(8,128)(2,1)}, bf16[1024,384]{1,0:T(8,128)(2,1)}, f32[1024,1024]{1,0:T(8,128)}) custom-call(s32[1]{0:T(128)} %bitcast.27.core_ref, bf16[512,2048]{1,0:T(8,128)(2,1)} %copy-done.7, bf16[512,2048]{1,0:T(8,128)(2,1)} %copy-done.11, bf16[2048,2432]{1,0:T(8,128)(2,1)} %bitcast.147, f32[1,128]{1,0:T(1,128)} %reshape_tile.7.refs_3_.refs_2_, ...), custom_call_target="tpu_custom_call" | custom-call | tf_op jit(solution)/shard_map/project_heads/pallas_call | solution.py:127
  206.9 31.5 %collective-permute-done.9 = bf16[1,2,1,80,2048]{4,3,1,2,0:T(8,128)(2,1)} collective-permute-done((bf16[1,2,1,80,2048]{4,3,1,2,0:T(8,128)(2,1)}, bf16[1,2,1,80,2048]{4,3,1,2,0:T(8,128)(2,1)}, u32[]{:S(2)}, u32[]{:S(2)}) %collective-permute-start.9) | collective-permute-done | bytes 655392 | tf_op jit(solution)/shard_map/ppermute | solution.py:713
  250.6 18.1 %attend.1 = (bf16[2,512,768]{2,1,0:T(8,128)(2,1)}, f32[2,4,16,128]{3,2,1,0:T(8,128)}) custom-call(s32[8]{0:T(128)} %reshape.464.lo_ref, bf16[2,512,768]{2,1,0:T(8,128)(2,1)} %bitcast.196, bf16[2,512,384]{2,1,0:T(8,128)(2,1)} %collective-permute-done.7.prior_ref, bf16[2,512,384]{2,1,0:T(8,128)(2,1)} %bitcast.209, s32[2,512,1]{2,1,0:T(8,128)} %copy.51.qseg_ref, ...), custom_call_target="tpu_custom_call" | custom-call | tf_op jit(solution)/shard_map/attend/pallas_call | solution.py:289
  276.1 18.0 %collective-permute-done.14 = bf16[1,1,1,80,2048]{4,3,2,1,0:T(8,128)(2,1)} collective-permute-done((bf16[1,1,1,80,2048]{4,3,2,1,0:T(8,128)(2,1)S(1)}, bf16[1,1,1,80,2048]{4,3,2,1,0:T(8,128)(2,1)}, u32[]{:S(2)}, u32[]{:S(2)}) %collective-permute-start.14) | collective-permute-done | bytes 327712 | tf_op jit(solution)/shard_map/ppermute | solution.py:713
  329.1 16.3 %hidden_units.4 = (bf16[1024,640]{1,0:T(8,128)(2,1)}, bf16[1024,1280]{1,0:T(8,128)(2,1)}) custom-call(bf16[512,2048]{1,0:T(8,128)(2,1)} %copy-done.3, bf16[512,2048]{1,0:T(8,128)(2,1)} %copy-done.9, bf16[512,2048]{1,0:T(8,128)(2,1)} %bitcast.169, bf16[512,2048]{1,0:T(8,128)(2,1)} %collective-permute-done.1.refs_3_, bf16[2048,1280]{1,0:T(8,128)(2,1)} %bitcast.151, ...), custom_call_target="tpu_custom_call" | custom-call | tf_op jit(solution)/shard_map/hidden_units/pallas_call | solution.py:421
  352.1 12.8 %collective-permute-done.18.refs_0_.refs_2_ = bf16[512,2048]{1,0:T(8,128)(2,1)} collective-permute-done((bf16[512,2048]{1,0:T(8,128)(2,1)S(1)}, bf16[512,2048]{1,0:T(8,128)(2,1)}, u32[]{:S(2)}, u32[]{:S(2)}) %collective-permute-start.18) | collective-permute-done | bytes 2097184 | tf_op jit(solution)/shard_map/ppermute | solution.py:681
  372.9 16.5 %hidden_units.5 = (bf16[1024,640]{1,0:T(8,128)(2,1)}, bf16[1024,1280]{1,0:T(8,128)(2,1)}) custom-call(bf16[512,2048]{1,0:T(8,128)(2,1)} %collective-permute-done.18.refs_0_.refs_2_, bf16[512,2048]{1,0:T(8,128)(2,1)} %copy-done.10, bf16[512,2048]{1,0:T(8,128)(2,1)} %collective-permute-done.10.refs_2_.refs_4_, bf16[512,2048]{1,0:T(8,128)(2,1)} %copy-done.8, ...), custom_call_target="tpu_custom_call" | custom-call | tf_op jit(solution)/shard_map/hidden_units/pallas_call | solution.py:421
  399.3 17.4 %units_grad.2 = (bf16[1024,1280]{1,0:T(8,128)(2,1)}, bf16[1024,1280]{1,0:T(8,128)(2,1)}) custom-call(s32[1]{0:T(128)} %bitcast.60.bit_ref, bf16[512,2048]{1,0:T(8,128)(2,1)} %copy-done.3, bf16[512,2048]{1,0:T(8,128)(2,1)} %copy-done.9, bf16[512,2048]{1,0:T(8,128)(2,1)} %collective-permute-done.18.refs_0_.refs_2_, bf16[512,2048]{1,0:T(8,128)(2,1)} %copy-done.10, ...), custom_call_target="tpu_custom_call" | custom-call | tf_op jit(solution)/shard_map/units_grad/pallas_call | solution.py:466
  434.6 16.3 %hidden_units.7 = (bf16[1024,640]{1,0:T(8,128)(2,1)}, bf16[1024,1280]{1,0:T(8,128)(2,1)}) custom-call(bf16[512,2048]{1,0:T(8,128)(2,1)} %collective-permute-done.18.refs_0_.refs_2_, bf16[512,2048]{1,0:T(8,128)(2,1)} %copy-done.10, bf16[512,2048]{1,0:T(8,128)(2,1)} %collective-permute-done.10.refs_2_.refs_4_, bf16[512,2048]{1,0:T(8,128)(2,1)} %copy-done.8, ...), custom_call_target="tpu_custom_call" | custom-call | tf_op jit(solution)/shard_map/hidden_units/pallas_call | solution.py:421
  450.9 16.3 %hidden_units.6 = (bf16[1024,640]{1,0:T(8,128)(2,1)}, bf16[1024,1280]{1,0:T(8,128)(2,1)}) custom-call(bf16[512,2048]{1,0:T(8,128)(2,1)} %copy-done.3, bf16[512,2048]{1,0:T(8,128)(2,1)} %copy-done.9, bf16[512,2048]{1,0:T(8,128)(2,1)} %bitcast.171, bf16[512,2048]{1,0:T(8,128)(2,1)} %collective-permute-done.1.refs_3_, bf16[2048,1280]{1,0:T(8,128)(2,1)} %bitcast.156, ...), custom_call_target="tpu_custom_call" | custom-call | tf_op jit(solution)/shard_map/hidden_units/pallas_call | solution.py:421
  477.5 17.5 %units_grad.3 = (bf16[1024,1280]{1,0:T(8,128)(2,1)}, bf16[1024,1280]{1,0:T(8,128)(2,1)}) custom-call(s32[1]{0:T(128)} %bitcast.60.bit_ref, bf16[512,2048]{1,0:T(8,128)(2,1)} %copy-done.3, bf16[512,2048]{1,0:T(8,128)(2,1)} %copy-done.9, bf16[512,2048]{1,0:T(8,128)(2,1)} %collective-permute-done.18.refs_0_.refs_2_, bf16[512,2048]{1,0:T(8,128)(2,1)} %copy-done.10, ...), custom_call_target="tpu_custom_call" | custom-call | tf_op jit(solution)/shard_map/units_grad/pallas_call | solution.py:466
  504.6 16.1 %hidden_sum.2 = (f32[512,2048]{1,0:T(8,128)}, bf16[512,2048]{1,0:T(8,128)(2,1)}) custom-call(s32[1]{0:T(128)} %constant.255.clone.1.core_ref.bit_ref, bf16[1024,1280]{1,0:T(8,128)(2,1)} %get-tuple-element.852.refs_4_.refs_0_, bf16[1024,1280]{1,0:T(8,128)(2,1)} %get-tuple-element.854.refs_4_.refs_1_, bf16[2048,1280]{1,0:T(8,128)(2,1)} %bitcast.153, ...), custom_call_target="tpu_custom_call" | custom-call | tf_op jit(solution)/shard_map/hidden_sum/pallas_call | solution.py:524
  520.8 16.1 %hidden_sum.3 = (f32[512,2048]{1,0:T(8,128)}, bf16[512,2048]{1,0:T(8,128)(2,1)}) custom-call(s32[1]{0:T(128)} %constant.255.clone.1.core_ref.bit_ref, bf16[1024,1280]{1,0:T(8,128)(2,1)} %get-tuple-element.853.refs_5_.refs_0_, bf16[1024,1280]{1,0:T(8,128)(2,1)} %get-tuple-element.855.refs_5_.refs_1_, bf16[2048,1280]{1,0:T(8,128)(2,1)} %bitcast.154, ...), custom_call_target="tpu_custom_call" | custom-call | tf_op jit(solution)/shard_map/hidden_sum/pallas_call | solution.py:524
  539.9 18.1 %collective-permute-done.26 = bf16[1,2,1,256,1280]{4,3,2,1,0:T(8,128)(2,1)S(1)} collective-permute-done((bf16[1,2,1,256,1280]{4,3,2,1,0:T(8,128)(2,1)}, bf16[1,2,1,256,1280]{4,3,2,1,0:T(8,128)(2,1)S(1)}, u32[]{:S(2)}, u32[]{:S(2)}) %collective-permute-start.26) | collective-permute-done | bytes 1310752 | tf_op jit(solution)/shard_map/ppermute | solution.py:713
  586.1 10.7 %down_sum.2 = (f32[512,2048]{1,0:T(8,128)}, bf16[512,2048]{1,0:T(8,128)(2,1)}) custom-call(s32[1]{0:T(128)} %constant.255.clone.1.core_ref.bit_ref, bf16[1024,640]{1,0:T(8,128)(2,1)} %get-tuple-element.926.refs_0_, bf16[1024,640]{1,0:T(8,128)(2,1)} %get-tuple-element.928.refs_0_.refs_1_, bf16[640,2048]{1,0:T(8,128)(2,1)} %bitcast.161, ...), custom_call_target="tpu_custom_call" | custom-call | tf_op jit(solution)/shard_map/down_sum/pallas_call | solution.py:524
  596.8 10.5 %down_sum.3 = (f32[512,2048]{1,0:T(8,128)}, bf16[512,2048]{1,0:T(8,128)(2,1)}) custom-call(s32[1]{0:T(128)} %constant.255.clone.1.core_ref.bit_ref, bf16[1024,640]{1,0:T(8,128)(2,1)} %get-tuple-element.927.refs_1_.refs_0_, bf16[1024,640]{1,0:T(8,128)(2,1)} %get-tuple-element.929.refs_1_, bf16[640,2048]{1,0:T(8,128)(2,1)} %bitcast.162, ...), custom_call_target="tpu_custom_call" | custom-call | tf_op jit(solution)/shard_map/down_sum/pallas_call | solution.py:524
  616.7 12.2 %collective-permute-done.33 = bf16[1,2,1,256,1280]{4,3,2,1,0:T(8,128)(2,1)} collective-permute-done((bf16[1,2,1,256,1280]{4,3,2,1,0:T(8,128)(2,1)}, bf16[1,2,1,256,1280]{4,3,2,1,0:T(8,128)(2,1)}, u32[]{:S(2)}, u32[]{:S(2)}) %collective-permute-start.33) | collective-permute-done | bytes 1310752 | tf_op jit(solution)/shard_map/ppermute | solution.py:713
  687.4 28.8 %attend_back.1 = (f32[2,512,768]{2,1,0:T(8,128)}, bf16[2,512,384]{2,1,0:T(8,128)(2,1)}, f32[2,512,384]{2,1,0:T(8,128)}) custom-call(s32[8]{0:T(128)} %reshape.495.lo_ref, bf16[2,512,768]{2,1,0:T(8,128)(2,1)} %bitcast.197, bf16[2,512,384]{2,1,0:T(8,128)(2,1)} %collective-permute-done.7.prior_ref, bf16[2,512,384]{2,1,0:T(8,128)(2,1)} %bitcast.210, ...), custom_call_target="tpu_custom_call" | custom-call | tf_op jit(solution)/shard_map/attend_back/pallas_call | solution.py:375
  731.5 19.7 %collective-permute-start.46 = (bf16[2,512,384]{2,1,0:T(8,128)(2,1)}, bf16[2,512,384]{2,1,0:T(8,128)(2,1)}, u32[]{:S(2)}, u32[]{:S(2)}) collective-permute-start(bf16[2,512,384]{2,1,0:T(8,128)(2,1)} %get-tuple-element.1081), channel_id=1, source_target_pairs={{0,16},{16,0},{1,17},{17,1},{2,18},{18,2},{3,19},{19,3},{4,20},{20... | collective-permute-start | bytes 2359304 | tf_op jit(solution)/shard_map/ppermute | solution.py:677
  802.7 10.5 %collective-permute-done.51 = bf16[1,2,2,2,128,768]{5,4,3,2,1,0:T(8,128)(2,1)} collective-permute-done((bf16[1,2,2,2,128,768]{5,4,3,2,1,0:T(8,128)(2,1)}, bf16[1,2,2,2,128,768]{5,4,3,2,1,0:T(8,128)(2,1)}, u32[]{:S(2)}, u32[]{:S(2)}) %collective-permute-start.51) | collective-permute-done | bytes 1572896 | tf_op jit(solution)/shard_map/ppermute | solution.py:713
  828.8 10.9 %first_sum.1 = (f32[512,2048]{1,0:T(8,128)}, bf16[512,2048]{1,0:T(8,128)(2,1)}) custom-call(s32[1]{0:T(128)} %bitcast.27.core_ref, bf16[1024,768]{1,0:T(8,128)(2,1)} %get-tuple-element.1122.refs_2_.refs_0_.refs_1_, bf16[1024,768]{1,0:T(8,128)(2,1)} %get-tuple-element.1122.refs_2_.refs_0_.refs_1_, bf16[1024,384]{1,0:T(8,128)(2,1)} %get-tuple-element.1123.refs_2_, ...), custom_call_target="tpu_custom_call" | custom-call | tf_op jit(solution)/shard_map/first_sum/pallas_call | solution.py:553
  (495 shorter events, 438.1 us)
Async XLA Ops:
  7.2 154.3 %all-gather.3.cloned.1.call-start = ((), (), s32[]{:S(2)}) async-start(), calls=%async_computation | async-start | bytes 17977344 | tf_op jit(solution)/shard_map/all_gather | solution.py:922
  12.9 38.9 %collective-permute-start.5 = (bf16[1,1,1,80,2048]{4,3,2,1,0:T(8,128)(2,1)}, bf16[1,1,1,80,2048]{4,3,2,1,0:T(8,128)(2,1)}, u32[]{:S(2)}, u32[]{:S(2)}) collective-permute-start(bf16[1,1,1,80,2048]{4,3,2,1,0:T(8,128)(2,1)} %get-tuple-element.1232), channel_id=1, source_target_pairs={{0,8},{4,12},{8,0},{12,4},{1,9},{5,13},{9,1},{13,5},{2,10},{6,14},... | collective-permute-start | bytes 983048 | tf_op jit(solution)/shard_map/ppermute | solution.py:713
  23.8 152.6 %collective-permute-start.1 = (bf16[512,2048]{1,0:T(8,128)(2,1)S(1)}, bf16[512,2048]{1,0:T(8,128)(2,1)}, u32[]{:S(2)}, u32[]{:S(2)}) collective-permute-start(bf16[512,2048]{1,0:T(8,128)(2,1)S(1)} %bitcast.173), channel_id=1, source_target_pairs={{0,1},{1,0},{2,3},{3,2},{4,5},{5,4},{6,7},{7,6},{8,9},{9,8},{10,11... | collective-permute-start | bytes 6291464 | tf_op jit(solution)/shard_map/ppermute | solution.py:663
  50.8 53.1 %collective-permute-start.4 = (bf16[1,1,1,256,1280]{4,3,2,1,0:T(8,128)(2,1)S(1)}, bf16[1,1,1,256,1280]{4,3,2,1,0:T(8,128)(2,1)S(1)}, u32[]{:S(2)}, u32[]{:S(2)}) collective-permute-start(bf16[1,1,1,256,1280]{4,3,2,1,0:T(8,128)(2,1)S(1)} %get-tuple-element.1224), channel_id=1, source_target_pairs={{0,8},{4,12},{8,0},{12,4},{1,9},{5,13},{9,1},{13,5},{2,10},{6,14},... | collective-permute-start | bytes 1966088 | tf_op jit(solution)/shard_map/ppermute | solution.py:713
  189.2 51.6 %collective-permute-start.8 = (bf16[1,2,1,256,1280]{4,3,1,2,0:T(8,128)(2,1)}, bf16[1,2,1,256,1280]{4,3,1,2,0:T(8,128)(2,1)}, u32[]{:S(2)}, u32[]{:S(2)}) collective-permute-start(bf16[1,2,1,256,1280]{4,3,1,2,0:T(8,128)(2,1)} %bitcast.32), channel_id=1, source_target_pairs={{0,4},{4,0},{8,12},{12,8},{1,5},{5,1},{9,13},{13,9},{2,6},{6,2},{1... | collective-permute-start | bytes 3932168 | tf_op jit(solution)/shard_map/ppermute | solution.py:713
  243.7 57.3 %collective-permute-start.11 = (bf16[1,2,2,256,1280]{4,3,2,1,0:T(8,128)(2,1)}, bf16[1,2,2,256,1280]{4,3,2,1,0:T(8,128)(2,1)}, u32[]{:S(2)}, u32[]{:S(2)}) collective-permute-start(bf16[1,2,2,256,1280]{4,3,2,1,0:T(8,128)(2,1)} %bitcast.181), channel_id=1, source_target_pairs={{0,16},{16,0},{1,17},{17,1},{2,18},{18,2},{3,19},{19,3},{4,20},{20... | collective-permute-start | bytes 7864328 | tf_op jit(solution)/shard_map/ppermute | solution.py:713
  244.9 53.7 %collective-permute-start.10 = (bf16[512,2048]{1,0:T(8,128)(2,1)S(1)}, bf16[512,2048]{1,0:T(8,128)(2,1)}, u32[]{:S(2)}, u32[]{:S(2)}) collective-permute-start(bf16[512,2048]{1,0:T(8,128)(2,1)S(1)} %bitcast.174), channel_id=1, source_target_pairs={{0,2},{2,0},{1,3},{3,1},{4,6},{6,4},{5,7},{7,5},{8,10},{10,8},{9,1... | collective-permute-start | bytes 6291464 | tf_op jit(solution)/shard_map/ppermute | solution.py:681
  245.2 53.4 %collective-permute-start.13 = (bf16[2,2,1,80,2048]{4,3,1,0,2:T(8,128)(2,1)}, bf16[2,2,1,80,2048]{4,3,1,0,2:T(8,128)(2,1)}, u32[]{:S(2)}, u32[]{:S(2)}) collective-permute-start(bf16[2,2,1,80,2048]{4,3,1,0,2:T(8,128)(2,1)} %bitcast.39), channel_id=1, source_target_pairs={{0,4},{4,0},{8,12},{12,8},{1,5},{5,1},{9,13},{13,9},{2,6},{6,2},{1... | collective-permute-start | bytes 3932168 | tf_op jit(solution)/shard_map/ppermute | solution.py:713
  246.7 49.4 %collective-permute-start.12 = (bf16[1,1,1,256,1280]{4,3,2,1,0:T(8,128)(2,1)}, bf16[1,1,1,256,1280]{4,3,2,1,0:T(8,128)(2,1)}, u32[]{:S(2)}, u32[]{:S(2)}) collective-permute-start(bf16[1,1,1,256,1280]{4,3,2,1,0:T(8,128)(2,1)} %get-tuple-element.677), channel_id=1, source_target_pairs={{0,8},{4,12},{8,0},{12,4},{1,9},{5,13},{9,1},{13,5},{2,10},{6,14},... | collective-permute-start | bytes 1966088 | tf_op jit(solution)/shard_map/ppermute | solution.py:713
  247.9 46.2 %collective-permute-start.14 = (bf16[1,1,1,80,2048]{4,3,2,1,0:T(8,128)(2,1)S(1)}, bf16[1,1,1,80,2048]{4,3,2,1,0:T(8,128)(2,1)}, u32[]{:S(2)}, u32[]{:S(2)}) collective-permute-start(bf16[1,1,1,80,2048]{4,3,2,1,0:T(8,128)(2,1)S(1)} %copy-done.62), channel_id=1, source_target_pairs={{0,8},{4,12},{8,0},{12,4},{1,9},{5,13},{9,1},{13,5},{2,10},{6,14},... | collective-permute-start | bytes 983048 | tf_op jit(solution)/shard_map/ppermute | solution.py:713
  317.9 46.9 %collective-permute-start.18 = (bf16[512,2048]{1,0:T(8,128)(2,1)S(1)}, bf16[512,2048]{1,0:T(8,128)(2,1)}, u32[]{:S(2)}, u32[]{:S(2)}) collective-permute-start(bf16[512,2048]{1,0:T(8,128)(2,1)S(1)} %get-tuple-element.797.refs_0_), channel_id=1, source_target_pairs={{0,2},{2,0},{1,3},{3,1},{4,6},{6,4},{5,7},{7,5},{8,10},{10,8},{9,1... | collective-permute-start | bytes 6291464 | tf_op jit(solution)/shard_map/ppermute | solution.py:681
  364.9 57.5 %collective-permute-start.22 = (bf16[1,2,2,256,1280]{4,3,2,1,0:T(8,128)(2,1)}, bf16[1,2,2,256,1280]{4,3,2,1,0:T(8,128)(2,1)}, u32[]{:S(2)}, u32[]{:S(2)}) collective-permute-start(bf16[1,2,2,256,1280]{4,3,2,1,0:T(8,128)(2,1)} %bitcast.185), channel_id=1, source_target_pairs={{0,16},{16,0},{1,17},{17,1},{2,18},{18,2},{3,19},{19,3},{4,20},{20... | collective-permute-start | bytes 7864328 | tf_op jit(solution)/shard_map/ppermute | solution.py:713
  367.6 49.1 %collective-permute-start.23 = (bf16[2,2,1,80,2048]{4,3,1,0,2:T(8,128)(2,1)S(1)}, bf16[2,2,1,80,2048]{4,3,1,0,2:T(8,128)(2,1)S(1)}, u32[]{:S(2)}, u32[]{:S(2)}) collective-permute-start(bf16[2,2,1,80,2048]{4,3,1,0,2:T(8,128)(2,1)S(1)} %bitcast.205), channel_id=1, source_target_pairs={{0,4},{4,0},{8,12},{12,8},{1,5},{5,1},{9,13},{13,9},{2,6},{6,2},{1... | collective-permute-start | bytes 3932168 | tf_op jit(solution)/shard_map/ppermute | solution.py:713
  422.4 74.6 %collective-permute-start.24 = (bf16[1,2,2,256,1280]{4,3,2,1,0:T(8,128)(2,1)}, bf16[1,2,2,256,1280]{4,3,2,1,0:T(8,128)(2,1)}, u32[]{:S(2)}, u32[]{:S(2)}) collective-permute-start(bf16[1,2,2,256,1280]{4,3,2,1,0:T(8,128)(2,1)} %bitcast.229), channel_id=1, source_target_pairs={{0,16},{16,0},{1,17},{17,1},{2,18},{18,2},{3,19},{19,3},{4,20},{20... | collective-permute-start | bytes 7864328 | tf_op jit(solution)/shard_map/ppermute | solution.py:713
  425.0 70.0 %collective-permute-start.25 = (bf16[2,2,1,80,2048]{4,3,2,1,0:T(8,128)(2,1)S(1)}, bf16[2,2,1,80,2048]{4,3,2,1,0:T(8,128)(2,1)}, u32[]{:S(2)}, u32[]{:S(2)}) collective-permute-start(bf16[2,2,1,80,2048]{4,3,2,1,0:T(8,128)(2,1)S(1)} %constant_dynamic-slice_fusion.24), channel_id=1, source_target_pairs={{0,4},{4,0},{8,12},{12,8},{1,5},{5,1},{9,13},{13,9},{2,6},{6,2},{1... | collective-permute-start | bytes 3932168 | tf_op jit(solution)/shard_map/ppermute | solution.py:713
  500.1 59.3 %collective-permute-start.27 = (bf16[1,2,2,256,1280]{4,3,2,1,0:T(8,128)(2,1)}, bf16[1,2,2,256,1280]{4,3,2,1,0:T(8,128)(2,1)}, u32[]{:S(2)}, u32[]{:S(2)}) collective-permute-start(bf16[1,2,2,256,1280]{4,3,2,1,0:T(8,128)(2,1)} %bitcast.71), channel_id=1, source_target_pairs={{0,16},{16,0},{1,17},{17,1},{2,18},{18,2},{3,19},{19,3},{4,20},{20... | collective-permute-start | bytes 7864328 | tf_op jit(solution)/shard_map/ppermute | solution.py:713
  503.2 54.8 %collective-permute-start.26 = (bf16[1,2,1,256,1280]{4,3,2,1,0:T(8,128)(2,1)}, bf16[1,2,1,256,1280]{4,3,2,1,0:T(8,128)(2,1)S(1)}, u32[]{:S(2)}, u32[]{:S(2)}) collective-permute-start(bf16[1,2,1,256,1280]{4,3,2,1,0:T(8,128)(2,1)} %constant_dynamic-slice_fusion.23), channel_id=1, source_target_pairs={{0,4},{4,0},{8,12},{12,8},{1,5},{5,1},{9,13},{13,9},{2,6},{6,2},{1... | collective-permute-start | bytes 3932168 | tf_op jit(solution)/shard_map/ppermute | solution.py:713
  583.9 47.8 %collective-permute-start.31 = (bf16[512,2048]{1,0:T(8,128)(2,1)}, bf16[512,2048]{1,0:T(8,128)(2,1)S(1)}, u32[]{:S(2)}, u32[]{:S(2)}) collective-permute-start(bf16[512,2048]{1,0:T(8,128)(2,1)} %add_convert_fusion.4), channel_id=1, source_target_pairs={{0,2},{2,0},{1,3},{3,1},{4,6},{6,4},{5,7},{7,5},{8,10},{10,8},{9,1... | collective-permute-start | bytes 6291464 | tf_op jit(solution)/shard_map/ppermute | solution.py:681
  585.8 43.0 %collective-permute-start.33 = (bf16[1,2,1,256,1280]{4,3,2,1,0:T(8,128)(2,1)}, bf16[1,2,1,256,1280]{4,3,2,1,0:T(8,128)(2,1)}, u32[]{:S(2)}, u32[]{:S(2)}) collective-permute-start(bf16[1,2,1,256,1280]{4,3,2,1,0:T(8,128)(2,1)} %constant_dynamic-slice_fusion.20), channel_id=1, source_target_pairs={{0,4},{4,0},{8,12},{12,8},{1,5},{5,1},{9,13},{13,9},{2,6},{6,2},{1... | collective-permute-start | bytes 3932168 | tf_op jit(solution)/shard_map/ppermute | solution.py:713
  682.1 47.0 %collective-permute-start.42 = (bf16[512,2048]{1,0:T(8,128)(2,1)}, bf16[512,2048]{1,0:T(8,128)(2,1)}, u32[]{:S(2)}, u32[]{:S(2)}) collective-permute-start(bf16[512,2048]{1,0:T(8,128)(2,1)} %add_convert_fusion.3), channel_id=1, source_target_pairs={{0,2},{2,0},{1,3},{3,1},{4,6},{6,4},{5,7},{7,5},{8,10},{10,8},{9,1... | collective-permute-start | bytes 6291464 | tf_op jit(solution)/shard_map/ppermute | solution.py:681
  729.9 42.1 %collective-permute-start.47 = (bf16[1,2,1,2,48,1024]{5,4,3,2,1,0:T(8,128)(2,1)}, bf16[1,2,1,2,48,1024]{5,4,3,2,1,0:T(8,128)(2,1)}, u32[]{:S(2)}, u32[]{:S(2)}) collective-permute-start(bf16[1,2,1,2,48,1024]{5,4,3,2,1,0:T(8,128)(2,1)} %constant_dynamic-slice_fusion.13), channel_id=1, source_target_pairs={{0,4},{4,0},{8,12},{12,8},{1,5},{5,1},{9,13},{13,9},{2,6},{6,2},{1... | collective-permute-start | bytes 1179656 | tf_op jit(solution)/shard_map/ppermute | solution.py:713
  730.9 42.3 %collective-permute-start.48 = (bf16[2,2,2,1,48,1024]{5,4,3,2,1,0:T(8,128)(2,1)}, bf16[2,2,2,1,48,1024]{5,4,3,2,1,0:T(8,128)(2,1)}, u32[]{:S(2)}, u32[]{:S(2)}) collective-permute-start(bf16[2,2,2,1,48,1024]{5,4,3,2,1,0:T(8,128)(2,1)} %constant_dynamic-slice_fusion.12), channel_id=1, source_target_pairs={{0,2},{2,0},{1,3},{3,1},{4,6},{6,4},{5,7},{7,5},{8,10},{10,8},{9,1... | collective-permute-start | bytes 2359304 | tf_op jit(solution)/shard_map/ppermute | solution.py:713
  731.5 43.2 %collective-permute-start.46 = (bf16[2,512,384]{2,1,0:T(8,128)(2,1)}, bf16[2,512,384]{2,1,0:T(8,128)(2,1)}, u32[]{:S(2)}, u32[]{:S(2)}) collective-permute-start(bf16[2,512,384]{2,1,0:T(8,128)(2,1)} %get-tuple-element.1081), channel_id=1, source_target_pairs={{0,16},{16,0},{1,17},{17,1},{2,18},{18,2},{3,19},{19,3},{4,20},{20... | collective-permute-start | bytes 2359304 | tf_op jit(solution)/shard_map/ppermute | solution.py:677
  774.8 38.5 %collective-permute-start.51 = (bf16[1,2,2,2,128,768]{5,4,3,2,1,0:T(8,128)(2,1)}, bf16[1,2,2,2,128,768]{5,4,3,2,1,0:T(8,128)(2,1)}, u32[]{:S(2)}, u32[]{:S(2)}) collective-permute-start(bf16[1,2,2,2,128,768]{5,4,3,2,1,0:T(8,128)(2,1)} %bitcast.88), channel_id=1, source_target_pairs={{0,16},{16,0},{1,17},{17,1},{2,18},{18,2},{3,19},{19,3},{4,20},{20... | collective-permute-start | bytes 4718600 | tf_op jit(solution)/shard_map/ppermute | solution.py:713
  (134 other events, 1577.2 us)
Sparse Core Ops, SparseCore 0:
  12.0 149.4 all-gather.2

commit v3 on v2

--- a/solution.py
+++ b/solution.py
@@ -648,14 +648,14 @@
     (DOWN, 0): (0, 2, 3),
     (UNITS, 1): (3, 5, 6),
     (DOWN, 1): (3, 5, 6),
-    (DOWN, 0, True): (7, 10, 12),
-    (UNITS, 0, True): (7, 8, 10),
-    (DOWN, 1, True): (8, 10, 12),
-    (UNITS, 1, True): (8, 10, 13),
-    (OUT, 0, True): (13, 14, 15, 16),
-    (OUT, 1, True): (14, 15, 16, 17),
-    (QKV, 0, True): (15, 16, 17, 18),
-    (QKV, 1, True): (16, 17, 18, 19),
+    (DOWN, 0, True): (7, 9, 11),
+    (UNITS, 0, True): (7, 9, 11),
+    (DOWN, 1, True): (9, 14, 15),
+    (UNITS, 1, True): (11, 12, 13),
+    (OUT, 0, True): (14, 15, 16, 17),
+    (OUT, 1, True): (12, 13, 15, 16),
+    (QKV, 0, True): (13, 14, 15, 16),
+    (QKV, 1, True): (14, 15, 16, 17),
 }
 
 
@@ -938,8 +938,13 @@
 
     def take_gathered():
         live = flow.live
+        live.gathered = gathered
         live.qkv = gathered[:, :in_rows].reshape(width, -1)
-        live.out = gathered[:, in_rows:, :width].reshape(-1, width)
+
+    def take_out():
+        live = flow.live
+        live.out = live.gathered[:, in_rows:, :width].reshape(-1, width)
+        del live.gathered
 
     def tables():
         live = flow.live
@@ -1041,9 +1046,12 @@
             [live.ggu[j, h] for j in js], [live.wgu[j] for j in js], True, "hidden_sum"
         )
 
-    def near_hidden_sums():
+    def far_hidden_sum():
         live = flow.live
         live.far_grad_sum = near_rows(live.hidden_sum.pop(1)).astype(BF)
+
+    def near_hidden_sum():
+        live = flow.live
         live.near_grad = near_rows(live.hidden_sum.pop(0))
 
     def far_grad():
@@ -1171,27 +1179,26 @@
     schedule = (
         (tables, first_norm, take_gathered),
         (first_hidden,),
-        (heads, prior_keys),
+        (heads, prior_keys, take_out),
         (far_low, attention, branch_sum),
         (branch, near_low),
         (far_hidden, do(units, 0, 0)),
         (near_hidden, do(units, 0, 1), do(down_grad, 0), do(units_grad, 0)),
-        (do(units, 1, 0), do(units, 1, 1), do(down_grad, 1), do(units_grad, 1)),
-        (do(hidden_sum, 1), do(hidden_sum, 0)),
-        (near_hidden_sums,),
-        (far_grad, do(down_sum, 1), do(down_sum, 0)),
-        (second_back, near_down_sums),
-        (do(home, 0), out_grad),
-        (far_result, attention_back),
-        (prior_back, do(home, 1), queries_back),
+        (do(units, 1, 0), do(units, 1, 1), do(down_grad, 1), do(hidden_sum, 1)),
+        (far_hidden_sum,),
+        (far_grad, do(units_grad, 1), do(hidden_sum, 0), do(down_sum, 1), do(down_sum, 0)),
+        (near_hidden_sum, second_back, near_down_sums),
+        (far_result, out_grad, attention_back),
+        (prior_back, do(home, 0), queries_back),
         (keys_back,),
-        (first_sums,),
+        (first_sums, do(home, 1)),
         (first_back, finish_output, do(gain_hops, gain_order[:2])),
-        (finish_units, finish_out, do(gain_hops, gain_order[2:4])),
-        (do(gain_hops, gain_order[4:]),),
+        (do(gain_hops, gain_order[2:4]),),
+        (finish_units, do(gain_hops, gain_order[4:])),
     )
     for work in schedule:
         flow.interval(*work)
+    finish_out()
     live = flow.live
 
     grads = []

time: 925 us -> 906 us (0.979)
  waiting for transfers between devices: 279 us -> 267 us
  other arithmetic: 110 us -> 98.6 us
    ppermute x2, starting transfers between devices: 20.9 us -> 30.8 us  [swap_seq(): return lax.ppermute(value, 'seq', [(0, 1), (1, 0)])]
    ppermute x7, waiting for transfers between devices: 36.1 us -> 26.6 us  [swap_x(): return lax.ppermute(value, 'x', [(0, 1), (1, 0)])]
  transfers between devices with their start and end apart: 74 -> 74, of which waited for: 28 -> 29; matrix products, arithmetic and copies ran while one was open for 15% -> 14% of each run, Pallas kernels for 37% -> 37%
where the time goes in v3:
time: 906 us; the launch traced here: 897 us
  Pallas kernels  336 us (37%)
  waiting for transfers between devices  267 us (29%)
  starting transfers between devices  108 us (12%)
  other arithmetic  98.6 us (11%)
  local copies, waits for them, and re-layouts  72.4 us (8%)
  between operations  15.7 us (2%)
    ppermute x45, waiting for transfers between devices, exchange(): lax.ppermute(value, axis, [(i, i ^ step) for i in range(lax.axis_size(axi...  161 us
    pallas_call x4, Pallas kernels, hidden_units(): call(kernel, (rows // tile,), groups + groups + [once(gate_up.shape), onc...  65.6 us
    pallas_call x5, Pallas kernels, sum_products(): call(kernel, (width // tile,), [once(a.shape) for a in lefts] + right, [c...  60.5 us
    ppermute x45, starting transfers between devices, exchange(): lax.ppermute(value, axis, [(i, i ^ step) for i in range(lax.axis_size(axi...  55.4 us
    all_gather x1, waiting for transfers between devices, body(): gathered = lax.all_gather(block, AXES, axis=0)  54.3 us
    pallas_call x4, Pallas kernels, tall_grad(): call(kernel, (steps,), [pl.BlockSpec((half, tile), column)] * count + [on...  49.1 us
    pallas_call x12, Pallas kernels, placed(): call(place_kernel, (lead, inner // part), [side, side], pl.BlockSpec((1,...  36.1 us
    ppermute x2, starting transfers between devices, swap_seq(): return lax.ppermute(value, 'seq', [(0, 1), (1, 0)])  30.8 us
  transfers between devices with their start and end apart: 74, of which 29 were waited for; matrix products, arithmetic and copies ran while one was open for 14% of the time, Pallas kernels for 37%

profile of v3, /device:TPU:1, one launch (start us, length us, event | category | flops | bytes accessed | tf_op | source)
XLA Modules:
  0.0 897.5 jit_solution(6226527206208288759)
XLA Ops:
  35.9 13.5 %collective-permute-done.3 = bf16[128,2560]{1,0:T(8,128)(2,1)S(1)} collective-permute-done((bf16[128,2560]{1,0:T(8,128)(2,1)}, bf16[128,2560]{1,0:T(8,128)(2,1)S(1)}, u32[]{:S(2)}, u32[]{:S(2)}) %collective-permute-start.3) | collective-permute-done | bytes 655392 | tf_op jit(solution)/shard_map/ppermute | solution.py:681
  53.9 50.1 %collective-permute-done.4 = bf16[1,1,1,256,1280]{4,3,2,1,0:T(8,128)(2,1)S(1)} collective-permute-done((bf16[1,1,1,256,1280]{4,3,2,1,0:T(8,128)(2,1)S(1)}, bf16[1,1,1,256,1280]{4,3,2,1,0:T(8,128)(2,1)S(1)}, u32[]{:S(2)}, u32[]{:S(2)}) %collective-permute-start.4) | collective-permute-done | bytes 655392 | tf_op jit(solution)/shard_map/ppermute | solution.py:713
  107.2 54.3 %all-gather.3.cloned.1.call-done = bf16[3584,2432]{1,0:T(8,128)(2,1)} async-done(((bf16[112,2432]{1,0:T(8,128)(2,1)}), bf16[3584,2432]{1,0:T(8,128)(2,1)}) %all-gather.3.cloned.1.call-update) | async-done | bytes 17432592 | tf_op jit(solution)/shard_map/all_gather | solution.py:922
  186.7 12.1 %project_heads.1 = (bf16[1024,768]{1,0:T(8,128)(2,1)}, bf16[1024,384]{1,0:T(8,128)(2,1)}, f32[1024,1024]{1,0:T(8,128)}) custom-call(s32[1]{0:T(128)} %bitcast.26.core_ref, bf16[512,2048]{1,0:T(8,128)(2,1)} %copy-done.7, bf16[512,2048]{1,0:T(8,128)(2,1)} %copy-done.12, bf16[2048,2432]{1,0:T(8,128)(2,1)} %bitcast.147, f32[1,128]{1,0:T(1,128)} %reshape_tile.7.refs_3_.refs_2_, ...), custom_call_target="tpu_custom_call" | custom-call | tf_op jit(solution)/shard_map/project_heads/pallas_call | solution.py:127
  206.9 24.9 %collective-permute-done.9 = bf16[1,2,1,80,2048]{4,3,1,2,0:T(8,128)(2,1)} collective-permute-done((bf16[1,2,1,80,2048]{4,3,1,2,0:T(8,128)(2,1)}, bf16[1,2,1,80,2048]{4,3,1,2,0:T(8,128)(2,1)}, u32[]{:S(2)}, u32[]{:S(2)}) %collective-permute-start.9) | collective-permute-done | bytes 655392 | tf_op jit(solution)/shard_map/ppermute | solution.py:713
  244.0 16.9 %attend.1 = (bf16[2,512,768]{2,1,0:T(8,128)(2,1)}, f32[2,4,16,128]{3,2,1,0:T(8,128)}) custom-call(s32[8]{0:T(128)} %reshape.464.lo_ref, bf16[2,512,768]{2,1,0:T(8,128)(2,1)} %bitcast.196, bf16[2,512,384]{2,1,0:T(8,128)(2,1)} %collective-permute-done.7.prior_ref, bf16[2,512,384]{2,1,0:T(8,128)(2,1)} %bitcast.209, s32[2,512,1]{2,1,0:T(8,128)} %copy.51.qseg_ref, ...), custom_call_target="tpu_custom_call" | custom-call | tf_op jit(solution)/shard_map/attend/pallas_call | solution.py:289
  268.2 19.2 %collective-permute-done.14 = bf16[1,1,1,80,2048]{4,3,2,1,0:T(8,128)(2,1)} collective-permute-done((bf16[1,1,1,80,2048]{4,3,2,1,0:T(8,128)(2,1)S(1)}, bf16[1,1,1,80,2048]{4,3,2,1,0:T(8,128)(2,1)}, u32[]{:S(2)}, u32[]{:S(2)}) %collective-permute-start.14) | collective-permute-done | bytes 327712 | tf_op jit(solution)/shard_map/ppermute | solution.py:713
  322.3 16.5 %hidden_units.4 = (bf16[1024,640]{1,0:T(8,128)(2,1)}, bf16[1024,1280]{1,0:T(8,128)(2,1)}) custom-call(bf16[512,2048]{1,0:T(8,128)(2,1)} %copy-done.3, bf16[512,2048]{1,0:T(8,128)(2,1)} %copy-done.8, bf16[512,2048]{1,0:T(8,128)(2,1)} %bitcast.169, bf16[512,2048]{1,0:T(8,128)(2,1)} %collective-permute-done.1.refs_3_, bf16[2048,1280]{1,0:T(8,128)(2,1)} %bitcast.151, ...), custom_call_target="tpu_custom_call" | custom-call | tf_op jit(solution)/shard_map/hidden_units/pallas_call | solution.py:421
  345.4 12.7 %collective-permute-done.18.refs_0_.refs_2_ = bf16[512,2048]{1,0:T(8,128)(2,1)S(1)} collective-permute-done((bf16[512,2048]{1,0:T(8,128)(2,1)S(1)}, bf16[512,2048]{1,0:T(8,128)(2,1)S(1)}, u32[]{:S(2)}, u32[]{:S(2)}) %collective-permute-start.18) | collective-permute-done | bytes 2097184 | tf_op jit(solution)/shard_map/ppermute | solution.py:681
  365.8 16.5 %hidden_units.5 = (bf16[1024,640]{1,0:T(8,128)(2,1)}, bf16[1024,1280]{1,0:T(8,128)(2,1)}) custom-call(bf16[512,2048]{1,0:T(8,128)(2,1)} %copy-done.9, bf16[512,2048]{1,0:T(8,128)(2,1)} %copy-done.10, bf16[512,2048]{1,0:T(8,128)(2,1)} %collective-permute-done.10.refs_2_.refs_4_, bf16[512,2048]{1,0:T(8,128)(2,1)} %copy-done.11, bf16[2048,1280]{1,0:T(8,128)(2,1)} %bitcast.152, ...), custom_call_target="tpu_custom_call" | custom-call | tf_op jit(solution)/shard_map/hidden_units/pallas_call | solution.py:421
  382.3 10.0 %down_grad.2 = bf16[640,2048]{1,0:T(8,128)(2,1)} custom-call(bf16[1024,640]{1,0:T(8,128)(2,1)} %get-tuple-element.820.refs_0_, bf16[1024,640]{1,0:T(8,128)(2,1)} %get-tuple-element.821.refs_1_.refs_0_, bf16[512,2048]{1,0:T(8,128)(2,1)} %bitcast.170, bf16[512,2048]{1,0:T(8,128)(2,1)} %collective-permute-done.1.refs_3_, ...), custom_call_target="tpu_custom_call" | custom-call | tf_op jit(solution)/shard_map/down_grad/pallas_call | solution.py:491
  392.3 17.4 %units_grad.2 = (bf16[1024,1280]{1,0:T(8,128)(2,1)}, bf16[1024,1280]{1,0:T(8,128)(2,1)}) custom-call(s32[1]{0:T(128)} %bitcast.60.bit_ref, bf16[512,2048]{1,0:T(8,128)(2,1)} %copy-done.3, bf16[512,2048]{1,0:T(8,128)(2,1)} %copy-done.8, bf16[512,2048]{1,0:T(8,128)(2,1)} %copy-done.9, bf16[512,2048]{1,0:T(8,128)(2,1)} %copy-done.10, ...), custom_call_target="tpu_custom_call" | custom-call | tf_op jit(solution)/shard_map/units_grad/pallas_call | solution.py:466
  427.7 16.3 %hidden_units.7 = (bf16[1024,640]{1,0:T(8,128)(2,1)}, bf16[1024,1280]{1,0:T(8,128)(2,1)}) custom-call(bf16[512,2048]{1,0:T(8,128)(2,1)} %copy-done.9, bf16[512,2048]{1,0:T(8,128)(2,1)} %copy-done.10, bf16[512,2048]{1,0:T(8,128)(2,1)} %collective-permute-done.10.refs_2_.refs_4_, bf16[512,2048]{1,0:T(8,128)(2,1)} %copy-done.11, bf16[2048,1280]{1,0:T(8,128)(2,1)} %bitcast.155, ...), custom_call_target="tpu_custom_call" | custom-call | tf_op jit(solution)/shard_map/hidden_units/pallas_call | solution.py:421
  444.1 16.3 %hidden_units.6 = (bf16[1024,640]{1,0:T(8,128)(2,1)}, bf16[1024,1280]{1,0:T(8,128)(2,1)}) custom-call(bf16[512,2048]{1,0:T(8,128)(2,1)} %copy-done.3, bf16[512,2048]{1,0:T(8,128)(2,1)} %copy-done.8, bf16[512,2048]{1,0:T(8,128)(2,1)} %bitcast.171, bf16[512,2048]{1,0:T(8,128)(2,1)} %collective-permute-done.1.refs_3_, bf16[2048,1280]{1,0:T(8,128)(2,1)} %bitcast.156, ...), custom_call_target="tpu_custom_call" | custom-call | tf_op jit(solution)/shard_map/hidden_units/pallas_call | solution.py:421
  460.4 10.3 %down_grad.3 = bf16[640,2048]{1,0:T(8,128)(2,1)} custom-call(bf16[1024,640]{1,0:T(8,128)(2,1)} %get-tuple-element.822.refs_0_.refs_1_, bf16[1024,640]{1,0:T(8,128)(2,1)} %get-tuple-element.823.refs_1_, bf16[512,2048]{1,0:T(8,128)(2,1)} %bitcast.172, bf16[512,2048]{1,0:T(8,128)(2,1)} %collective-permute-done.1.refs_3_, ...), custom_call_target="tpu_custom_call" | custom-call | tf_op jit(solution)/shard_map/down_grad/pallas_call | solution.py:491
  470.7 16.2 %hidden_sum.2 = (f32[512,2048]{1,0:T(8,128)}, bf16[512,2048]{1,0:T(8,128)(2,1)}) custom-call(s32[1]{0:T(128)} %constant.254.clone.1.core_ref.bit_ref, bf16[1024,1280]{1,0:T(8,128)(2,1)} %get-tuple-element.747.refs_5_.refs_0_, bf16[1024,1280]{1,0:T(8,128)(2,1)} %get-tuple-element.836.refs_1_.refs_5_, bf16[2048,1280]{1,0:T(8,128)(2,1)} %bitcast.153, ...), custom_call_target="tpu_custom_call" | custom-call | tf_op jit(solution)/shard_map/hidden_sum/pallas_call | solution.py:524
  511.2 10.4 %down_sum.2 = (f32[512,2048]{1,0:T(8,128)}, bf16[512,2048]{1,0:T(8,128)(2,1)}) custom-call(s32[1]{0:T(128)} %constant.254.clone.1.core_ref.bit_ref, bf16[1024,640]{1,0:T(8,128)(2,1)} %get-tuple-element.820.refs_0_, bf16[1024,640]{1,0:T(8,128)(2,1)} %get-tuple-element.822.refs_0_.refs_1_, bf16[640,2048]{1,0:T(8,128)(2,1)} %bitcast.161, ...), custom_call_target="tpu_custom_call" | custom-call | tf_op jit(solution)/shard_map/down_sum/pallas_call | solution.py:524
  521.6 10.5 %down_sum.3 = (f32[512,2048]{1,0:T(8,128)}, bf16[512,2048]{1,0:T(8,128)(2,1)}) custom-call(s32[1]{0:T(128)} %constant.254.clone.1.core_ref.bit_ref, bf16[1024,640]{1,0:T(8,128)(2,1)} %get-tuple-element.821.refs_1_.refs_0_, bf16[1024,640]{1,0:T(8,128)(2,1)} %get-tuple-element.823.refs_1_, bf16[640,2048]{1,0:T(8,128)(2,1)} %bitcast.162, ...), custom_call_target="tpu_custom_call" | custom-call | tf_op jit(solution)/shard_map/down_sum/pallas_call | solution.py:524
  532.1 16.1 %hidden_sum.3 = (f32[512,2048]{1,0:T(8,128)}, bf16[512,2048]{1,0:T(8,128)(2,1)}) custom-call(s32[1]{0:T(128)} %constant.254.clone.1.core_ref.bit_ref, bf16[1024,1280]{1,0:T(8,128)(2,1)} %get-tuple-element.834.refs_4_.refs_0_, bf16[1024,1280]{1,0:T(8,128)(2,1)} %get-tuple-element.835.refs_1_.refs_4_, bf16[2048,1280]{1,0:T(8,128)(2,1)} %bitcast.154, ...), custom_call_target="tpu_custom_call" | custom-call | tf_op jit(solution)/shard_map/hidden_sum/pallas_call | solution.py:524
  548.2 17.7 %units_grad.3 = (bf16[1024,1280]{1,0:T(8,128)(2,1)}, bf16[1024,1280]{1,0:T(8,128)(2,1)}) custom-call(s32[1]{0:T(128)} %bitcast.60.bit_ref, bf16[512,2048]{1,0:T(8,128)(2,1)} %copy-done.3, bf16[512,2048]{1,0:T(8,128)(2,1)} %copy-done.8, bf16[512,2048]{1,0:T(8,128)(2,1)} %copy-done.9, bf16[512,2048]{1,0:T(8,128)(2,1)} %copy-done.10, ...), custom_call_target="tpu_custom_call" | custom-call | tf_op jit(solution)/shard_map/units_grad/pallas_call | solution.py:466
  624.8 26.7 %attend_back.1 = (f32[2,512,768]{2,1,0:T(8,128)}, bf16[2,512,384]{2,1,0:T(8,128)(2,1)}, f32[2,512,384]{2,1,0:T(8,128)}) custom-call(s32[8]{0:T(128)} %reshape.491.lo_ref, bf16[2,512,768]{2,1,0:T(8,128)(2,1)} %bitcast.197, bf16[2,512,384]{2,1,0:T(8,128)(2,1)} %collective-permute-done.7.prior_ref, bf16[2,512,384]{2,1,0:T(8,128)(2,1)} %bitcast.210, ...), custom_call_target="tpu_custom_call" | custom-call | tf_op jit(solution)/shard_map/attend_back/pallas_call | solution.py:375
  668.7 29.6 %collective-permute-start.40 = (bf16[2,512,384]{2,1,0:T(8,128)(2,1)}, bf16[2,512,384]{2,1,0:T(8,128)(2,1)}, u32[]{:S(2)}, u32[]{:S(2)}) collective-permute-start(bf16[2,512,384]{2,1,0:T(8,128)(2,1)} %get-tuple-element.956), channel_id=1, source_target_pairs={{0,16},{16,0},{1,17},{17,1},{2,18},{18,2},{3,19},{19,3},{4,20},{20... | collective-permute-start | bytes 2359304 | tf_op jit(solution)/shard_map/ppermute | solution.py:677
  699.4 8.9 head_grads.2
  770.5 10.8 %first_sum.1 = (f32[512,2048]{1,0:T(8,128)}, bf16[512,2048]{1,0:T(8,128)(2,1)}) custom-call(s32[1]{0:T(128)} %bitcast.26.core_ref, bf16[1024,768]{1,0:T(8,128)(2,1)} %get-tuple-element.997.refs_2_.refs_0_.refs_1_, bf16[1024,768]{1,0:T(8,128)(2,1)} %get-tuple-element.997.refs_2_.refs_0_.refs_1_, bf16[1024,384]{1,0:T(8,128)(2,1)} %get-tuple-element.998.refs_2_, ...), custom_call_target="tpu_custom_call" | custom-call | tf_op jit(solution)/shard_map/first_sum/pallas_call | solution.py:553
  (466 shorter events, 427.8 us)
Async XLA Ops:
  7.2 154.3 %all-gather.3.cloned.1.call-start = ((), (), s32[]{:S(2)}) async-start(), calls=%async_computation | async-start | bytes 17977344 | tf_op jit(solution)/shard_map/all_gather | solution.py:922
  23.8 146.0 %collective-permute-start.1 = (bf16[512,2048]{1,0:T(8,128)(2,1)S(1)}, bf16[512,2048]{1,0:T(8,128)(2,1)}, u32[]{:S(2)}, u32[]{:S(2)}) collective-permute-start(bf16[512,2048]{1,0:T(8,128)(2,1)S(1)} %bitcast.173), channel_id=1, source_target_pairs={{0,1},{1,0},{2,3},{3,2},{4,5},{5,4},{6,7},{7,6},{8,9},{9,8},{10,11... | collective-permute-start | bytes 6291464 | tf_op jit(solution)/shard_map/ppermute | solution.py:663
  50.9 53.1 %collective-permute-start.4 = (bf16[1,1,1,256,1280]{4,3,2,1,0:T(8,128)(2,1)S(1)}, bf16[1,1,1,256,1280]{4,3,2,1,0:T(8,128)(2,1)S(1)}, u32[]{:S(2)}, u32[]{:S(2)}) collective-permute-start(bf16[1,1,1,256,1280]{4,3,2,1,0:T(8,128)(2,1)S(1)} %get-tuple-element.1104), channel_id=1, source_target_pairs={{0,8},{4,12},{8,0},{12,4},{1,9},{5,13},{9,1},{13,5},{2,10},{6,14},... | collective-permute-start | bytes 1966088 | tf_op jit(solution)/shard_map/ppermute | solution.py:713
  182.5 51.7 %collective-permute-start.8 = (bf16[1,2,1,256,1280]{4,3,1,2,0:T(8,128)(2,1)}, bf16[1,2,1,256,1280]{4,3,1,2,0:T(8,128)(2,1)}, u32[]{:S(2)}, u32[]{:S(2)}) collective-permute-start(bf16[1,2,1,256,1280]{4,3,1,2,0:T(8,128)(2,1)} %bitcast.32), channel_id=1, source_target_pairs={{0,4},{4,0},{8,12},{12,8},{1,5},{5,1},{9,13},{13,9},{2,6},{6,2},{1... | collective-permute-start | bytes 3932168 | tf_op jit(solution)/shard_map/ppermute | solution.py:713
  237.1 57.3 %collective-permute-start.11 = (bf16[1,2,2,256,1280]{4,3,2,1,0:T(8,128)(2,1)}, bf16[1,2,2,256,1280]{4,3,2,1,0:T(8,128)(2,1)}, u32[]{:S(2)}, u32[]{:S(2)}) collective-permute-start(bf16[1,2,2,256,1280]{4,3,2,1,0:T(8,128)(2,1)} %bitcast.181), channel_id=1, source_target_pairs={{0,16},{16,0},{1,17},{17,1},{2,18},{18,2},{3,19},{19,3},{4,20},{20... | collective-permute-start | bytes 7864328 | tf_op jit(solution)/shard_map/ppermute | solution.py:713
  238.3 53.7 %collective-permute-start.10 = (bf16[512,2048]{1,0:T(8,128)(2,1)S(1)}, bf16[512,2048]{1,0:T(8,128)(2,1)}, u32[]{:S(2)}, u32[]{:S(2)}) collective-permute-start(bf16[512,2048]{1,0:T(8,128)(2,1)S(1)} %bitcast.174), channel_id=1, source_target_pairs={{0,2},{2,0},{1,3},{3,1},{4,6},{6,4},{5,7},{7,5},{8,10},{10,8},{9,1... | collective-permute-start | bytes 6291464 | tf_op jit(solution)/shard_map/ppermute | solution.py:681
  238.6 53.4 %collective-permute-start.13 = (bf16[2,2,1,80,2048]{4,3,1,0,2:T(8,128)(2,1)}, bf16[2,2,1,80,2048]{4,3,1,0,2:T(8,128)(2,1)}, u32[]{:S(2)}, u32[]{:S(2)}) collective-permute-start(bf16[2,2,1,80,2048]{4,3,1,0,2:T(8,128)(2,1)} %bitcast.39), channel_id=1, source_target_pairs={{0,4},{4,0},{8,12},{12,8},{1,5},{5,1},{9,13},{13,9},{2,6},{6,2},{1... | collective-permute-start | bytes 3932168 | tf_op jit(solution)/shard_map/ppermute | solution.py:713
  240.0 49.4 %collective-permute-start.12 = (bf16[1,1,1,256,1280]{4,3,2,1,0:T(8,128)(2,1)}, bf16[1,1,1,256,1280]{4,3,2,1,0:T(8,128)(2,1)}, u32[]{:S(2)}, u32[]{:S(2)}) collective-permute-start(bf16[1,1,1,256,1280]{4,3,2,1,0:T(8,128)(2,1)} %get-tuple-element.616), channel_id=1, source_target_pairs={{0,8},{4,12},{8,0},{12,4},{1,9},{5,13},{9,1},{13,5},{2,10},{6,14},... | collective-permute-start | bytes 1966088 | tf_op jit(solution)/shard_map/ppermute | solution.py:713
  311.2 46.8 %collective-permute-start.18 = (bf16[512,2048]{1,0:T(8,128)(2,1)S(1)}, bf16[512,2048]{1,0:T(8,128)(2,1)S(1)}, u32[]{:S(2)}, u32[]{:S(2)}) collective-permute-start(bf16[512,2048]{1,0:T(8,128)(2,1)S(1)} %get-tuple-element.837.refs_0_), channel_id=1, source_target_pairs={{0,2},{2,0},{1,3},{3,1},{4,6},{6,4},{5,7},{7,5},{8,10},{10,8},{9,1... | collective-permute-start | bytes 6291464 | tf_op jit(solution)/shard_map/ppermute | solution.py:681
  358.1 57.5 %collective-permute-start.22 = (bf16[1,2,2,256,1280]{4,3,2,1,0:T(8,128)(2,1)}, bf16[1,2,2,256,1280]{4,3,2,1,0:T(8,128)(2,1)}, u32[]{:S(2)}, u32[]{:S(2)}) collective-permute-start(bf16[1,2,2,256,1280]{4,3,2,1,0:T(8,128)(2,1)} %bitcast.185), channel_id=1, source_target_pairs={{0,16},{16,0},{1,17},{17,1},{2,18},{18,2},{3,19},{19,3},{4,20},{20... | collective-permute-start | bytes 7864328 | tf_op jit(solution)/shard_map/ppermute | solution.py:713
  360.7 48.9 %collective-permute-start.23 = (bf16[2,2,1,80,2048]{4,3,1,0,2:T(8,128)(2,1)S(1)}, bf16[2,2,1,80,2048]{4,3,1,0,2:T(8,128)(2,1)}, u32[]{:S(2)}, u32[]{:S(2)}) collective-permute-start(bf16[2,2,1,80,2048]{4,3,1,0,2:T(8,128)(2,1)S(1)} %bitcast.205), channel_id=1, source_target_pairs={{0,4},{4,0},{8,12},{12,8},{1,5},{5,1},{9,13},{13,9},{2,6},{6,2},{1... | collective-permute-start | bytes 3932168 | tf_op jit(solution)/shard_map/ppermute | solution.py:713
  415.5 73.4 %collective-permute-start.24 = (bf16[1,2,2,256,1280]{4,3,2,1,0:T(8,128)(2,1)}, bf16[1,2,2,256,1280]{4,3,2,1,0:T(8,128)(2,1)}, u32[]{:S(2)}, u32[]{:S(2)}) collective-permute-start(bf16[1,2,2,256,1280]{4,3,2,1,0:T(8,128)(2,1)} %bitcast.228), channel_id=1, source_target_pairs={{0,16},{16,0},{1,17},{17,1},{2,18},{18,2},{3,19},{19,3},{4,20},{20... | collective-permute-start | bytes 7864328 | tf_op jit(solution)/shard_map/ppermute | solution.py:713
  418.1 68.8 %collective-permute-start.25 = (bf16[2,2,1,80,2048]{4,3,2,1,0:T(8,128)(2,1)S(1)}, bf16[2,2,1,80,2048]{4,3,2,1,0:T(8,128)(2,1)}, u32[]{:S(2)}, u32[]{:S(2)}) collective-permute-start(bf16[2,2,1,80,2048]{4,3,2,1,0:T(8,128)(2,1)S(1)} %constant_dynamic-slice_fusion.24), channel_id=1, source_target_pairs={{0,4},{4,0},{8,12},{12,8},{1,5},{5,1},{9,13},{13,9},{2,6},{6,2},{1... | collective-permute-start | bytes 3932168 | tf_op jit(solution)/shard_map/ppermute | solution.py:713
  506.3 61.8 %collective-permute-start.30 = (bf16[2,2,1,80,2048]{4,3,2,1,0:T(8,128)(2,1)}, bf16[2,2,1,80,2048]{4,3,2,1,0:T(8,128)(2,1)}, u32[]{:S(2)}, u32[]{:S(2)}) collective-permute-start(bf16[2,2,1,80,2048]{4,3,2,1,0:T(8,128)(2,1)} %constant_dynamic-slice_fusion.21), channel_id=1, source_target_pairs={{0,4},{4,0},{8,12},{12,8},{1,5},{5,1},{9,13},{13,9},{2,6},{6,2},{1... | collective-permute-start | bytes 3932168 | tf_op jit(solution)/shard_map/ppermute | solution.py:713
  507.2 58.7 %collective-permute-start.29 = (bf16[1,2,1,80,2048]{4,3,2,1,0:T(8,128)(2,1)}, bf16[1,2,1,80,2048]{4,3,2,1,0:T(8,128)(2,1)}, u32[]{:S(2)}, u32[]{:S(2)}) collective-permute-start(bf16[1,2,1,80,2048]{4,3,2,1,0:T(8,128)(2,1)} %constant_dynamic-slice_fusion.22), channel_id=1, source_target_pairs={{0,16},{16,0},{1,17},{17,1},{2,18},{18,2},{3,19},{19,3},{4,20},{20... | collective-permute-start | bytes 1966088 | tf_op jit(solution)/shard_map/ppermute | solution.py:713
  507.5 66.6 %collective-permute-start.27 = (bf16[512,2048]{1,0:T(8,128)(2,1)}, bf16[512,2048]{1,0:T(8,128)(2,1)S(1)}, u32[]{:S(2)}, u32[]{:S(2)}) collective-permute-start(bf16[512,2048]{1,0:T(8,128)(2,1)} %add_convert_fusion.4), channel_id=1, source_target_pairs={{0,2},{2,0},{1,3},{3,1},{4,6},{6,4},{5,7},{7,5},{8,10},{10,8},{9,1... | collective-permute-start | bytes 6291464 | tf_op jit(solution)/shard_map/ppermute | solution.py:681
  509.8 61.4 %collective-permute-start.28 = (bf16[1,2,1,256,1280]{4,3,2,1,0:T(8,128)(2,1)}, bf16[1,2,1,256,1280]{4,3,2,1,0:T(8,128)(2,1)}, u32[]{:S(2)}, u32[]{:S(2)}) collective-permute-start(bf16[1,2,1,256,1280]{4,3,2,1,0:T(8,128)(2,1)} %constant_dynamic-slice_fusion.23), channel_id=1, source_target_pairs={{0,4},{4,0},{8,12},{12,8},{1,5},{5,1},{9,13},{13,9},{2,6},{6,2},{1... | collective-permute-start | bytes 3932168 | tf_op jit(solution)/shard_map/ppermute | solution.py:713
  598.5 58.4 %collective-permute-start.37 = (bf16[1,2,2,256,1280]{4,3,2,1,0:T(8,128)(2,1)}, bf16[1,2,2,256,1280]{4,3,2,1,0:T(8,128)(2,1)}, u32[]{:S(2)}, u32[]{:S(2)}) collective-permute-start(bf16[1,2,2,256,1280]{4,3,2,1,0:T(8,128)(2,1)} %bitcast.72), channel_id=1, source_target_pairs={{0,16},{16,0},{1,17},{17,1},{2,18},{18,2},{3,19},{19,3},{4,20},{20... | collective-permute-start | bytes 7864328 | tf_op jit(solution)/shard_map/ppermute | solution.py:713
  600.7 52.9 %collective-permute-start.38 = (bf16[1,1,1,80,2048]{4,3,2,1,0:T(8,128)(2,1)S(1)}, bf16[1,1,1,80,2048]{4,3,2,1,0:T(8,128)(2,1)}, u32[]{:S(2)}, u32[]{:S(2)}) collective-permute-start(bf16[1,1,1,80,2048]{4,3,2,1,0:T(8,128)(2,1)S(1)} %constant_dynamic-slice_fusion.19), channel_id=1, source_target_pairs={{0,8},{4,12},{8,0},{12,4},{1,9},{5,13},{9,1},{13,5},{2,10},{6,14},... | collective-permute-start | bytes 983048 | tf_op jit(solution)/shard_map/ppermute | solution.py:713
  604.0 51.7 %collective-permute-start.36 = (bf16[1,1,1,256,1280]{4,3,2,1,0:T(8,128)(2,1)}, bf16[1,1,1,256,1280]{4,3,2,1,0:T(8,128)(2,1)}, u32[]{:S(2)}, u32[]{:S(2)}) collective-permute-start(bf16[1,1,1,256,1280]{4,3,2,1,0:T(8,128)(2,1)} %constant_dynamic-slice_fusion.20), channel_id=1, source_target_pairs={{0,8},{4,12},{8,0},{12,4},{1,9},{5,13},{9,1},{13,5},{2,10},{6,14},... | collective-permute-start | bytes 1966088 | tf_op jit(solution)/shard_map/ppermute | solution.py:713
  606.5 52.9 %collective-permute-start.35 = (bf16[512,2048]{1,0:T(8,128)(2,1)}, bf16[512,2048]{1,0:T(8,128)(2,1)}, u32[]{:S(2)}, u32[]{:S(2)}) collective-permute-start(bf16[512,2048]{1,0:T(8,128)(2,1)} %add_convert_fusion.3), channel_id=1, source_target_pairs={{0,2},{2,0},{1,3},{3,1},{4,6},{6,4},{5,7},{7,5},{8,10},{10,8},{9,1... | collective-permute-start | bytes 6291464 | tf_op jit(solution)/shard_map/ppermute | solution.py:681
  662.1 55.6 %collective-permute-start.41 = (bf16[1,2,1,256,1280]{4,3,2,1,0:T(8,128)(2,1)}, bf16[1,2,1,256,1280]{4,3,2,1,0:T(8,128)(2,1)}, u32[]{:S(2)}, u32[]{:S(2)}) collective-permute-start(bf16[1,2,1,256,1280]{4,3,2,1,0:T(8,128)(2,1)} %constant_dynamic-slice_fusion.18), channel_id=1, source_target_pairs={{0,4},{4,0},{8,12},{12,8},{1,5},{5,1},{9,13},{13,9},{2,6},{6,2},{1... | collective-permute-start | bytes 3932168 | tf_op jit(solution)/shard_map/ppermute | solution.py:713
  664.2 52.1 %collective-permute-start.42 = (bf16[2,2,2,1,48,1024]{5,4,3,2,1,0:T(8,128)(2,1)}, bf16[2,2,2,1,48,1024]{5,4,3,2,1,0:T(8,128)(2,1)}, u32[]{:S(2)}, u32[]{:S(2)}) collective-permute-start(bf16[2,2,2,1,48,1024]{5,4,3,2,1,0:T(8,128)(2,1)} %constant_dynamic-slice_fusion.17), channel_id=1, source_target_pairs={{0,2},{2,0},{1,3},{3,1},{4,6},{6,4},{5,7},{7,5},{8,10},{10,8},{9,1... | collective-permute-start | bytes 2359304 | tf_op jit(solution)/shard_map/ppermute | solution.py:713
  668.7 51.0 %collective-permute-start.40 = (bf16[2,512,384]{2,1,0:T(8,128)(2,1)}, bf16[2,512,384]{2,1,0:T(8,128)(2,1)}, u32[]{:S(2)}, u32[]{:S(2)}) collective-permute-start(bf16[2,512,384]{2,1,0:T(8,128)(2,1)} %get-tuple-element.956), channel_id=1, source_target_pairs={{0,16},{16,0},{1,17},{17,1},{2,18},{18,2},{3,19},{19,3},{4,20},{20... | collective-permute-start | bytes 2359304 | tf_op jit(solution)/shard_map/ppermute | solution.py:677
  (120 other events, 1320.2 us)
Sparse Core Ops, SparseCore 0:
  12.1 149.4 all-gather.2
